TPU v7x, 32 devices: a whole 2x2x4 slice. The times are simulated.
32 devices in a mesh: row: 4 (over y, core), col: 8 (over z, x).
Axes of the slice: x: 2, y: 2, z: 4, core: 2. Of those that a mesh axis runs over, the one named last changes fastest.
Arguments:
- outside: bfloat16 [2048, 4096], P('row', 'col'), may hold values from 0.0099 to 17.5
- inside_head: bfloat16 [2048, 4096], P('row', 'col'), may hold values from 0.0099 to 17.5
- inside_tail: bfloat16 [2048, 4096], P('row', 'col'), may hold values from 0.0099 to 17.5
- inside_pair: float32 [512, 4096], P(None, 'col'), may hold values from 0.4 to 1.6
- seq_head: int32 [1, 4096], P(None, 'col'), may hold values from 0 to 3
- seq_tail: int32 [1, 4096], P(None, 'col'), may hold values from 0 to 3
- pair_mask: int32 [4, 32], P(None, 'col'), may hold values 0 or 1
- split_weight: float32 [4], replicated, may hold values from 0.5 to 2
- pair_weight: float32 [4, 4], replicated, may hold values from 0.5 to 2
- span_blocks: int32 [1], replicated, may hold values from 8 to 63
- partition: float32 [1], replicated, may hold values from 1 to 3
Outputs:
- outside_out: float32 [2048, 4096], P('row', 'col')
- prob_out: float32 [2048, 4096], P('row', 'col')
All inputs are finite; a program needn't handle non-finite values. No bound on the sum of `pair_mask` on one device may be relied on, other than what follows from the above.
Results may differ from a plain program's by a relative error of at most 0.0003.
Values may be sent and summed in bfloat16 or wider, within the bound.
No kernel may reach another device: no remote copies, remote signals or barrier semaphores. Data moves between devices by JAX's collectives and lax.ppermute only.
A program may use at most 64 MiB of HBM per device.

v0:
```python
import jax
import jax.numpy as jnp
from jax import lax
from jax.sharding import PartitionSpec as P

precise = lax.Precision.HIGHEST


def passed_along(x, axis, by):
    length = lax.axis_size(axis)
    return lax.ppermute(x, axis, [(i, (i + by) % length) for i in range(length)])


def finish(
    right_sum,
    left_sum,
    head_codes,
    tail_codes,
    mask_rows,
    pair_rows,
    split_weight,
    pair_weight,
    span_blocks,
    partition,
    owner_factor,
):
    cycles, tile_size = head_codes.shape
    repeat = tile_size // mask_rows.shape[1]
    allowed = jnp.repeat(
        jnp.repeat(mask_rows.astype(jnp.float32), repeat, axis=0), repeat, axis=1
    ).reshape(cycles, tile_size, tile_size)
    letters = jnp.arange(4, dtype=jnp.int32)
    head_hot = (head_codes[:, :, None] == letters[None, None, :]).astype(jnp.float32)
    tail_hot = (tail_codes[:, :, None] == letters[None, None, :]).astype(jnp.float32)
    head_weight = jnp.einsum("mak,k->ma", head_hot, split_weight, precision=precise)
    tail_weight = jnp.einsum("mak,k->ma", tail_hot, split_weight, precision=precise)
    outside_diag = (
        owner_factor
        * allowed
        * (right_sum * tail_weight[:, None, :] + head_weight[:, :, None] * left_sum)
        / tile_size
    )
    pair_table = jnp.einsum("mak,kl,mbl->mab", head_hot, pair_weight, tail_hot, precision=precise)
    positions = jnp.arange(tile_size, dtype=jnp.float32)
    span_nt = (
        tile_size * span_blocks[0].astype(jnp.float32) + positions[None, :] - positions[:, None]
    )
    penalty = jnp.sqrt(64.0 * tile_size / span_nt)
    pair_prob = (
        pair_rows.reshape(cycles, tile_size, tile_size)
        * outside_diag
        * pair_table
        * penalty[None, :, :]
        / partition[0]
    )
    return (
        outside_diag.reshape(cycles * tile_size, tile_size),
        pair_prob.reshape(cycles * tile_size, tile_size),
    )


def as_tiles(array):
    return array.reshape(-1, array.shape[1], array.shape[1])


def move_later(stack):
    return jnp.concatenate([jnp.zeros_like(stack), stack[:-1]], axis=0)


def per_device(
    outside,
    inside_head,
    inside_tail,
    inside_pair,
    seq_head,
    seq_tail,
    pair_mask,
    split_weight,
    pair_weight,
    span_blocks,
    partition,
):
    row_count = lax.axis_size("row")
    row_id = lax.axis_index("row")
    col_id = lax.axis_index("col")
    out_tiles = as_tiles(outside)
    right_part = jnp.einsum(
        "mac,mbc->mab", out_tiles, as_tiles(inside_tail), preferred_element_type=jnp.float32
    )
    window = passed_along(right_part, "col", -1)
    for level in range(row_count.bit_length() - 1):
        window = window + passed_along(window, "col", -(1 << level))
    reach = (col_id - row_id) % row_count
    reach = jnp.where(reach == 0, row_count, reach)
    left_part = jnp.einsum(
        "mca,mcb->mab", as_tiles(inside_head), out_tiles, preferred_element_type=jnp.float32
    )
    left_part = jnp.where(col_id < reach, move_later(left_part), left_part)
    left_sum = lax.psum(left_part, "row")
    owner_factor = (row_id == col_id % row_count).astype(jnp.float32)
    return finish(
        window,
        left_sum,
        seq_head,
        seq_tail,
        pair_mask,
        inside_pair,
        split_weight,
        pair_weight,
        span_blocks,
        partition,
        owner_factor,
    )


def solution(mesh):
    placed = (
        P("row", "col"),
        P("row", "col"),
        P("row", "col"),
        P(None, "col"),
        P(None, "col"),
        P(None, "col"),
        P(None, "col"),
        P(),
        P(),
        P(),
        P(),
    )
    return jax.shard_map(
        per_device,
        mesh=mesh,
        in_specs=placed,
        out_specs=(P("row", "col"), P("row", "col")),
        check_vma=False,
    )
```

profile of v0, /device:TPU:0, one launch (start us, length us, event | category | flops | bytes accessed | tf_op | source)
XLA Modules:
  0.0 118.1 jit_solution(13893284041892178920)
XLA Ops:
  7.2 0.0 copy-start
  7.2 0.0 all-reduce.2.cloned.1.call-start
  7.2 1.0 copy-done
  8.2 1.5 %convolution_bitcast_fusion.1 = f32[1,512,512]{2,1,0:T(8,128)S(1)} fusion(bf16[512,512]{1,0:T(8,128)(2,1)S(1)} %copy-done, bf16[512,512]{1,0:T(8,128)(2,1)} %param.13), kind=kOutput, calls=%fused_computation.3 | convolution fusion | flops 268435456 | bytes 2097152 | tf_op jit(solution)/shard_map/mac,mbc->mab/dot_general | solution.py:87
  9.7 6.1 %collective-permute-start = (f32[1,512,512]{2,1,0:T(8,128)S(1)}, f32[1,512,512]{2,1,0:T(8,128)S(1)}, u32[]{:S(2)}, u32[]{:S(2)}) collective-permute-start(f32[1,512,512]{2,1,0:T(8,128)S(1)} %convolution_bitcast_fusion.1), channel_id=1, source_target_pairs={{0,7},{1,0},{2,1},{3,2},{4,3},{5,4},{6,5},{7,6},{8,15},{9,8},{10,9... | collective-permute-start | bytes 3145736 | tf_op jit(solution)/shard_map/ppermute | solution.py:11
  15.8 22.4 %collective-permute-done = f32[1,512,512]{2,1,0:T(8,128)S(1)} collective-permute-done((f32[1,512,512]{2,1,0:T(8,128)S(1)}, f32[1,512,512]{2,1,0:T(8,128)S(1)}, u32[]{:S(2)}, u32[]{:S(2)}) %collective-permute-start) | collective-permute-done | bytes 1048608 | tf_op jit(solution)/shard_map/ppermute | solution.py:11
  38.2 5.2 %collective-permute-start.1 = (f32[1,512,512]{2,1,0:T(8,128)S(1)}, f32[1,512,512]{2,1,0:T(8,128)}, u32[]{:S(2)}, u32[]{:S(2)}) collective-permute-start(f32[1,512,512]{2,1,0:T(8,128)S(1)} %collective-permute-done), channel_id=1, source_target_pairs={{0,7},{1,0},{2,1},{3,2},{4,3},{5,4},{6,5},{7,6},{8,15},{9,8},{10,9... | collective-permute-start | bytes 3145736 | tf_op jit(solution)/shard_map/ppermute | solution.py:11
  43.4 21.6 %collective-permute-done.1 = f32[1,512,512]{2,1,0:T(8,128)} collective-permute-done((f32[1,512,512]{2,1,0:T(8,128)S(1)}, f32[1,512,512]{2,1,0:T(8,128)}, u32[]{:S(2)}, u32[]{:S(2)}) %collective-permute-start.1) | collective-permute-done | bytes 1048608 | tf_op jit(solution)/shard_map/ppermute | solution.py:11
  64.9 1.4 %add.30 = f32[1,512,512]{2,1,0:T(8,128)S(1)} add(f32[1,512,512]{2,1,0:T(8,128)S(1)} %collective-permute-done, f32[1,512,512]{2,1,0:T(8,128)} %collective-permute-done.1) | non-fusion elementwise | flops 262144 | bytes 3145728 | tf_op jit(solution)/shard_map/add | solution.py:92
  66.4 1.5 %collective-permute-start.2 = (f32[1,512,512]{2,1,0:T(8,128)S(1)}, f32[1,512,512]{2,1,0:T(8,128)}, u32[]{:S(2)}, u32[]{:S(2)}) collective-permute-start(f32[1,512,512]{2,1,0:T(8,128)S(1)} %add.30), channel_id=1, source_target_pairs={{0,6},{1,7},{2,0},{3,1},{4,2},{5,3},{6,4},{7,5},{8,14},{9,15},{10,... | collective-permute-start | bytes 3145736 | tf_op jit(solution)/shard_map/ppermute | solution.py:11
  67.8 0.0 copy-done.6
  67.8 1.4 %fusion = f32[1,512,512]{2,1,0:T(8,128)} fusion(bf16[512,512]{1,0:T(8,128)(2,1)S(1)} %copy-done.6, bf16[512,512]{1,0:T(8,128)(2,1)S(1)} %copy-done, pred[]{:T(512)S(6)} %lt.15), kind=kOutput, calls=%fused_computation.1 | convolution fusion | flops 268697600 | bytes 2097153 | tf_op jit(solution)/shard_map/mca,mcb->mab/dot_general | solution.py:95
  69.3 0.0 all-reduce.2.cloned.1.call-update
  69.3 0.0 copy-start.4
  69.3 0.7 copy-done.4
  70.0 0.6 broadcast_in_dim.7
  70.6 1.4 %mul.59 = f32[1,512,512]{2,1,0:T(8,128)} reshape(f32[512,4,128]{2,1,0:T(4,128)S(1)} %broadcast_in_dim.7) | data formatting | bytes 2097152 | tf_op jit(solution)/shard_map/mul | solution.py:38
  73.3 0.0 copy-start.7
  73.3 0.0 copy-start.8
  73.3 0.7 copy-done.7
  74.0 0.0 copy-done.8
  74.0 0.3 fusion.7
  74.3 0.7 copy-done.2
  75.0 0.3 fusion.6
  75.3 0.4 copy-done.3
  75.7 0.3 fusion.5
  76.0 30.8 %all-reduce.2.cloned.1.call-done = f32[1,512,512]{2,1,0:T(8,128)} async-done(((f32[1,512,512]{2,1,0:T(8,128)}), f32[1,512,512]{2,1,0:T(8,128)}) %all-reduce.2.cloned.1.call-update) | async-done | bytes 1048592 | tf_op jit(solution)/shard_map/psum | solution.py:99
  106.9 0.0 collective-permute-done.2
  106.9 2.2 %multiply_multiply_fusion = f32[1,512,512]{2,1,0:T(8,128)S(1)} fusion(f32[1,512,512]{2,1,0:T(8,128)} %mul.59, f32[1,512,512]{2,1,0:T(8,128)} %all-reduce.2.cloned.1.call-done, f32[1,512,512]{2,1,0:T(8,128)S(1)} %add.30, f32[1,512,512]{2,1,0:T(8,128)} %collective-permute-done.2, f32[512]{0:T(512)S(1)} %bitcast.46, f32[512]{0:T(512)S(1)} %bitcast.45), kind=kLoop, calls=%fused_computation.9 | loop fusion | flops 1572864 | bytes 5246976 | tf_op jit(solution)/shard_map/div | solution.py:38
  109.1 0.0 copy-start.1
  109.1 0.0 copy-done.5
  109.1 2.2 %fusion.4 = f32[512,512]{1,0:T(8,128)} fusion(f32[512,4]{1,0:T(8,128)S(1)} %fusion.5, f32[1,512,512]{2,1,0:T(8,128)S(1)} %multiply_multiply_fusion, f32[512,512]{1,0:T(8,128)S(1)} %copy-done.5, f32[]{:T(128)} %bitcast.40, f32[512]{0:T(512)S(1)} %iota_add_fusion, s32[512]{0:T(512)S(1)} %bitcast.48), kind=kOutput, calls=%fused_computation.7 | convolution fusion | flops 14157824 | bytes 3158020 | tf_op jit(solution)/shard_map/mak,kl,mbl->mab/dot_general | solution.py:43
  (8 shorter events, 0.1 us)
Async XLA Ops:
  7.2 1.0 copy-start
  7.2 99.7 %all-reduce.2.cloned.1.call-start = ((), (), s32[]{:S(2)}) async-start(), calls=%async_computation | async-start | bytes 2097152 | tf_op jit(solution)/shard_map/psum | solution.py:99
  9.7 28.5 %collective-permute-start = (f32[1,512,512]{2,1,0:T(8,128)S(1)}, f32[1,512,512]{2,1,0:T(8,128)S(1)}, u32[]{:S(2)}, u32[]{:S(2)}) collective-permute-start(f32[1,512,512]{2,1,0:T(8,128)S(1)} %convolution_bitcast_fusion.1), channel_id=1, source_target_pairs={{0,7},{1,0},{2,1},{3,2},{4,3},{5,4},{6,5},{7,6},{8,15},{9,8},{10,9... | collective-permute-start | bytes 3145736 | tf_op jit(solution)/shard_map/ppermute | solution.py:11
  38.2 26.7 %collective-permute-start.1 = (f32[1,512,512]{2,1,0:T(8,128)S(1)}, f32[1,512,512]{2,1,0:T(8,128)}, u32[]{:S(2)}, u32[]{:S(2)}) collective-permute-start(f32[1,512,512]{2,1,0:T(8,128)S(1)} %collective-permute-done), channel_id=1, source_target_pairs={{0,7},{1,0},{2,1},{3,2},{4,3},{5,4},{6,5},{7,6},{8,15},{9,8},{10,9... | collective-permute-start | bytes 3145736 | tf_op jit(solution)/shard_map/ppermute | solution.py:11
  43.4 24.5 %copy-start.6 = (bf16[512,512]{1,0:T(8,128)(2,1)S(1)}, bf16[512,512]{1,0:T(8,128)(2,1)}, u32[]{:S(2)}) copy-start(bf16[512,512]{1,0:T(8,128)(2,1)} %param.12) | copy-start | bytes 1572868
  66.4 40.5 %collective-permute-start.2 = (f32[1,512,512]{2,1,0:T(8,128)S(1)}, f32[1,512,512]{2,1,0:T(8,128)}, u32[]{:S(2)}, u32[]{:S(2)}) collective-permute-start(f32[1,512,512]{2,1,0:T(8,128)S(1)} %add.30), channel_id=1, source_target_pairs={{0,6},{1,7},{2,0},{3,1},{4,2},{5,3},{6,4},{7,5},{8,14},{9,15},{10,... | collective-permute-start | bytes 3145736 | tf_op jit(solution)/shard_map/ppermute | solution.py:11
  69.3 0.7 copy-start.4
  73.3 0.7 copy-start.7
  73.3 0.7 copy-start.8
  74.3 0.7 copy-start.2
  75.0 0.7 copy-start.3
  106.9 2.2 %copy-start.5 = (f32[512,512]{1,0:T(8,128)S(1)}, f32[512,512]{1,0:T(8,128)}, u32[]{:S(2)}) copy-start(f32[512,512]{1,0:T(8,128)} %param.14) | copy-start | bytes 3145732
  109.1 2.2 %copy-start.1 = (f32[1,512,512]{2,1,0:T(8,128)}, f32[1,512,512]{2,1,0:T(8,128)S(1)}, u32[]{:S(2)}) copy-start(f32[1,512,512]{2,1,0:T(8,128)S(1)} %multiply_multiply_fusion) | copy-start | bytes 3145732
Sparse Core Ops, SparseCore 0:
  69.4 37.4 all-reduce.1
where the time goes:
time: 118 us
  waiting for transfers between devices  74.8 us (63%)
  between operations  15.4 us (13%)
  starting transfers between devices  12.7 us (11%)
  matrix products  6.02 us (5%)
  local copies, waits for them, and re-layouts  5.42 us (5%)
  other arithmetic  3.66 us (3%)
    ppermute x3, waiting for transfers between devices, passed_along(): lax.ppermute(x, axis, [(i, (i + by) % length) for i in range(length)])  44 us
    psum x1, waiting for transfers between devices, per_device(): left_sum = lax.psum(left_part, 'row')  30.8 us
    ppermute x3, starting transfers between devices, passed_along(): lax.ppermute(x, axis, [(i, (i + by) % length) for i in range(length)])  12.7 us
    unnamed x18, local copies, waits for them, and re-layouts  3.4 us
    dot_general x2, matrix products, finish(): jnp.einsum('mak,kl,mbl->mab', head_hot, pair_weight, tail_hot, precision=...  2.47 us
  transfers between devices with their start and end apart: 4, of which 3 were waited for; matrix products, arithmetic and copies ran while one was open for 4% of the time, Pallas kernels for 0%

commit v1 on v0

--- a/solution.py
+++ b/solution.py
@@ -1,9 +1,287 @@
 import jax
 import jax.numpy as jnp
 from jax import lax
+from jax.experimental import pallas as pl
+from jax.experimental.pallas import tpu as pltpu
 from jax.sharding import PartitionSpec as P
 
+
 precise = lax.Precision.HIGHEST
+VMEM = pl.BlockSpec(memory_space=pltpu.VMEM)
+SMEM = pl.BlockSpec(memory_space=pltpu.SMEM)
+ANY = pl.BlockSpec(memory_space=pl.ANY)
+HBM = pl.BlockSpec(memory_space=pltpu.HBM)
+CHUNKS = 4
+PARAMS = pltpu.CompilerParams(vmem_limit_bytes=16 << 20)
+
+
+def encode(x):
+    y = x * 4.0
+    y2 = y * y
+    y4 = y2 * y2
+    return (y4 * y4 * y2).astype(jnp.bfloat16)
+
+
+def decode(code):
+    return jnp.exp2(jnp.log2(code.astype(jnp.float32)) * 0.1) * 0.25
+
+
+def pick(codes, value, count):
+    out = jnp.full(codes.shape, value(0))
+    for k in range(1, count):
+        out = jnp.where(codes == k, value(k), out)
+    return out
+
+
+def right_kernel(out_hbm, tail_hbm, out_ref, code_ref, tail_ref, sems):
+    size = out_ref.shape[0]
+    step = size // CHUNKS
+    parts = [pl.ds(k * step, step) for k in range(CHUNKS)]
+    tails = [
+        pltpu.make_async_copy(tail_hbm.at[part, :], tail_ref.at[part, :], sems.at[0, k])
+        for k, part in enumerate(parts)
+    ]
+    outs = [
+        pltpu.make_async_copy(out_hbm.at[part, :], out_ref.at[part, :], sems.at[1, k])
+        for k, part in enumerate(parts)
+    ]
+    for copy in tails + outs:
+        copy.start()
+    for copy in tails:
+        copy.wait()
+    for part, copy in zip(parts, outs):
+        copy.wait()
+        term = lax.dot_general(
+            out_ref[part, :],
+            tail_ref[...],
+            (((1,), (1,)), ((), ())),
+            preferred_element_type=jnp.float32,
+        )
+        code_ref[part, :] = encode(term * (1.0 / size))
+
+
+def left_kernel(flags_ref, head_ref, out_ref, after_ref, left_ref, code_ref):
+    term = lax.dot_general(
+        head_ref[...], out_ref[...], (((0,), (0,)), ((), ())), preferred_element_type=jnp.float32
+    )
+    term = jnp.where(flags_ref[0] == 1, term * (1.0 / term.shape[0]), 0.0)
+    left_ref[...] = term
+    code_ref[...] = encode(term)
+
+
+def chip_kernel(flags_ref, left_ref, other_ref, right_ref, left_out_ref, code_ref):
+    total = left_ref[...] + decode(other_ref[...])
+    left_out_ref[...] = total
+
+    @pl.when(flags_ref[1] == 1)
+    def _():
+        code_ref[...] = right_ref[...]
+
+    @pl.when(flags_ref[1] == 0)
+    def _():
+        code_ref[...] = encode(total)
+
+
+def add_kernel(a_ref, b_ref, code_ref):
+    code_ref[...] = encode(decode(a_ref[...]) + decode(b_ref[...]))
+
+
+def choose_kernel(flags_ref, a_ref, b_ref, after_ref, code_ref):
+    @pl.when(flags_ref[2] == 1)
+    def _():
+        code_ref[...] = a_ref[...]
+
+    @pl.when(flags_ref[2] == 0)
+    def _():
+        code_ref[...] = b_ref[...]
+
+
+def masked_row(mask_ref, row, size):
+    count = mask_ref.shape[1]
+    place = lax.broadcasted_iota(jnp.int32, (1, size), 1) // (size // count)
+    return pick(place, lambda k: mask_ref[row, k], count).astype(jnp.float32)
+
+
+def column(row):
+    return jnp.broadcast_to(row, (8, row.shape[1])).T[:, :1]
+
+
+def factor_kernel(
+    weight_ref, span_ref, partition_ref, head_ref, tail_ref, pair_ref, after_ref, factor_ref
+):
+    size = pair_ref.shape[0]
+    kinds = weight_ref.shape[0]
+    step = size // CHUNKS
+    tail = tail_ref[...]
+    head = column(head_ref[...].astype(jnp.float32)).astype(jnp.int32)
+    table = [pick(tail, lambda k, j=j: weight_ref[j, k], kinds) for j in range(kinds)]
+    reach = span_ref[0].astype(jnp.float32) * size
+    for cell in range(CHUNKS):
+        rows = pl.ds(cell * step, step)
+        part = slice(cell * step, (cell + 1) * step)
+        pairs = jnp.broadcast_to(table[0], (step, size))
+        for j in range(1, kinds):
+            pairs = jnp.where(head[part] == j, table[j], pairs)
+        a = lax.broadcasted_iota(jnp.int32, (step, size), 0) + cell * step
+        b = lax.broadcasted_iota(jnp.int32, (step, size), 1)
+        span = reach + (b - a).astype(jnp.float32)
+        penalty = jnp.sqrt(64.0 * size / span)
+        factor_ref[rows, :] = pair_ref[rows, :] * pairs * penalty / partition_ref[0]
+
+
+def partial_kernel(
+    flags_ref,
+    mask_ref,
+    split_ref,
+    head_ref,
+    tail_ref,
+    left_ref,
+    middle_ref,
+    first_ref,
+    partial_ref,
+    scale_ref,
+):
+    size = left_ref.shape[0]
+    cells = mask_ref.shape[0]
+    step = size // cells
+    kinds = split_ref.shape[0]
+    head = column(head_ref[...].astype(jnp.float32)).astype(jnp.int32)
+    tail_weight = pick(tail_ref[...], lambda k: split_ref[k], kinds)
+    head_weight = pick(head, lambda k: split_ref[k], kinds)
+    for cell in range(cells):
+        rows = pl.ds(cell * step, step)
+        part = slice(cell * step, (cell + 1) * step)
+        allowed = jnp.where(flags_ref[3] == 1, masked_row(mask_ref, cell, size), 0.0)
+        right = decode(first_ref[rows, :]) * tail_weight
+        left = (left_ref[rows, :] + decode(middle_ref[rows, :])) * head_weight[part]
+        partial_ref[rows, :] = allowed * (right + left)
+        scale_ref[pl.ds(cell, 1), :] = allowed * tail_weight
+
+
+def last_kernel(
+    scale_ref, partial_ref, factor_ref, inside_ref, last_ref, outside_ref, prob_ref
+):
+    cell = pl.program_id(0)
+    step = outside_ref.shape[0]
+    rows = pl.ds(cell * step, step)
+    right = decode(inside_ref[rows, :]) + decode(last_ref[rows, :])
+    total = partial_ref[rows, :] + scale_ref[pl.ds(cell, 1), :] * right
+    outside_ref[...] = total
+    prob_ref[...] = total * factor_ref[rows, :]
+
+
+def routes(col_count):
+    depth = col_count // 2
+
+    def at(x, y, core, z):
+        return (2 * y + core) * col_count + 2 * (z % depth) + x
+
+    first, middle, last, inside = [], [], [], []
+    for z in range(depth):
+        o = z % 2
+        n = 1 - o
+        first += [(at(1, o, 0, z), at(0, o, 0, z)), (at(0, o, 0, z), at(0, o, 1, z))]
+        first += [(at(0, o, 1, z), at(1, o, 0, z - 2)), (at(1, o, 1, z), at(1, o, 1, z - 2))]
+        first += [(at(1, n, 0, z), at(0, n, 0, z)), (at(0, n, 1, z), at(1, n, 1, z))]
+        first += [(at(0, n, 0, z), at(0, n, 1, z)), (at(1, n, 1, z), at(1, n, 0, z))]
+        middle += [(at(0, o, 0, z), at(0, o, 1, z - 2)), (at(1, o, 1, z), at(1, o, 0, z))]
+        for x in range(2):
+            middle += [(at(x, n, x, z), at(x, o, x, z))]
+            last += [(at(x, n, x, z), at(x, n, x, z - 1)), (at(x, o, x, z), at(x, o, 1 - x, z))]
+            for pairs in (middle, last):
+                pairs += [(at(x, o, 1 - x, z), at(x, n, 1 - x, z))]
+                pairs += [(at(x, n, 1 - x, z), at(x, n, x, z))]
+            for core in range(2):
+                for side in range(2):
+                    inside += [(at(x, side, core, z), at(x, side, 1 - core, z))]
+    return first, middle, last, inside
+
+
+def routed(
+    outside,
+    inside_head,
+    inside_tail,
+    inside_pair,
+    seq_head,
+    seq_tail,
+    pair_mask,
+    split_weight,
+    pair_weight,
+    span_blocks,
+    partition,
+):
+    size = outside.shape[1]
+    cells = pair_mask.shape[0]
+    row_count = lax.axis_size("row")
+    row_id = lax.axis_index("row")
+    col_id = lax.axis_index("col")
+    first, middle, last, inside = routes(lax.axis_size("col"))
+    reach = (col_id - row_id) % row_count
+    reach = jnp.where(reach == 0, row_count, reach)
+    flags = jnp.stack(
+        [
+            col_id >= reach,
+            row_id // 2 == (col_id // 2) % 2,
+            col_id % 2 == 1,
+            row_id == col_id % row_count,
+        ]
+    ).astype(jnp.int32)
+    code = pltpu.VMEM((size, size), jnp.bfloat16)
+    full = pltpu.VMEM((size, size), jnp.float32)
+    output = jax.ShapeDtypeStruct((size, size), jnp.float32)
+
+    def send(x, pairs):
+        x = lax.ppermute(x, ("row", "col"), pairs)
+        return pltpu.with_memory_space_constraint(x, pltpu.VMEM)
+
+    def call(kernel, specs, shape, scratch=()):
+        outs = tuple(VMEM for _ in shape) if isinstance(shape, tuple) else VMEM
+        return pl.pallas_call(
+            kernel,
+            in_specs=specs,
+            out_specs=outs,
+            out_shape=shape,
+            scratch_shapes=scratch,
+            compiler_params=PARAMS,
+        )
+
+    held, right = call(
+        right_kernel,
+        [HBM] * 2,
+        (code, code),
+        [code, pltpu.SemaphoreType.DMA((2, CHUNKS))],
+    )(
+        pltpu.with_memory_space_constraint(outside, pltpu.HBM),
+        pltpu.with_memory_space_constraint(inside_tail, pltpu.HBM),
+    )
+    q1 = send(right, first)
+    left, left_code = call(left_kernel, [SMEM] + [VMEM] * 2 + [ANY], (full, code))(
+        flags, inside_head, held, right
+    )
+    i0 = send(left_code, inside)
+    left, moved = call(chip_kernel, [SMEM] + [VMEM] * 3, (full, code))(flags, left, i0, right)
+    q3 = send(moved, middle)
+    pair = call(add_kernel, [VMEM] * 2, code)(right, q1)
+    q2 = send(pair, last)
+    factor = call(factor_kernel, [SMEM] * 3 + [VMEM] * 3 + [ANY], full)(
+        pair_weight, span_blocks, partition, seq_head, seq_tail, inside_pair, pair
+    )
+    chosen = call(choose_kernel, [SMEM] + [VMEM] * 2 + [ANY], code)(flags, q1, q3, factor)
+    i2 = send(chosen, inside)
+    partial, scale = call(
+        partial_kernel,
+        [SMEM] * 3 + [VMEM] * 5,
+        (full, pltpu.VMEM((cells, size), jnp.float32)),
+    )(flags, pair_mask, split_weight, seq_head, seq_tail, left, q3, q1)
+    block = pl.BlockSpec((size // cells, size), lambda cell: (cell, 0))
+    return pl.pallas_call(
+        last_kernel,
+        grid=(cells,),
+        in_specs=[VMEM] * 5,
+        out_specs=(block, block),
+        out_shape=(output, output),
+        compiler_params=PARAMS,
+    )(scale, partial, factor, i2, q2)
 
 
 def passed_along(x, axis, by):
@@ -67,7 +345,7 @@
     return jnp.concatenate([jnp.zeros_like(stack), stack[:-1]], axis=0)
 
 
-def per_device(
+def general(
     outside,
     inside_head,
     inside_tail,
@@ -113,6 +391,10 @@
     )
 
 
+def per_device(use_routes, outside, *rest):
+    return (routed if use_routes else general)(outside, *rest)
+
+
 def solution(mesh):
     placed = (
         P("row", "col"),
@@ -127,10 +409,18 @@
         P(),
         P(),
     )
-    return jax.shard_map(
-        per_device,
-        mesh=mesh,
-        in_specs=placed,
-        out_specs=(P("row", "col"), P("row", "col")),
-        check_vma=False,
-    )
+
+    def step(outside, *rest):
+        rows, cols = mesh.shape["row"], mesh.shape["col"]
+        one_tile = outside.shape[0] // rows == outside.shape[1] // cols
+        use_routes = one_tile and rows == 4 and cols % 4 == 0
+        body = jax.shard_map(
+            lambda *args: per_device(use_routes, *args),
+            mesh=mesh,
+            in_specs=placed,
+            out_specs=(P("row", "col"), P("row", "col")),
+            check_vma=False,
+        )
+        return body(outside, *rest)
+
+    return step

time: 118 us -> 31.2 us (0.26)
  the two profiles are of different devices: /device:TPU:0 before, /device:TPU:29 now
where the time goes in v1:
time: 31.2 us; the launch traced here: 31.1 us
  waiting for transfers between devices  15.2 us (49%)
  Pallas kernels  10.8 us (35%)
  starting transfers between devices  2.27 us (7%)
  between operations  2.18 us (7%)
  local copies, waits for them, and re-layouts  0.59 us (2%)
    ppermute x5, waiting for transfers between devices, send(): x = lax.ppermute(x, ('row', 'col'), pairs)  15.2 us
    pallas_call x1, Pallas kernels, routed(): call(right_kernel, [HBM] * 2, (code, code), [code, pltpu.SemaphoreType.DM...  2.63 us
    ppermute x5, starting transfers between devices, send(): x = lax.ppermute(x, ('row', 'col'), pairs)  2.27 us
    pallas_call x1, Pallas kernels, routed(): pl.pallas_call(last_kernel, grid=(cells,), in_specs=[VMEM] * 5, out_specs...  2.1 us
    pallas_call x1, Pallas kernels, routed(): call(factor_kernel, [SMEM] * 3 + [VMEM] * 3 + [ANY], full)  1.5 us
    pallas_call x1, Pallas kernels, routed(): call(partial_kernel, [SMEM] * 3 + [VMEM] * 5, (full, pltpu.VMEM((cells, s...  1.32 us
    pallas_call x1, Pallas kernels, routed(): call(left_kernel, [SMEM] + [VMEM] * 2 + [ANY], (full, code))  1.13 us
    pallas_call x1, Pallas kernels, routed(): call(chip_kernel, [SMEM] + [VMEM] * 3, (full, code))(flags, left, i0, right)  0.87 us
  transfers between devices with their start and end apart: 5, of which 3 were waited for; matrix products, arithmetic and copies ran while one was open for 0% of the time, Pallas kernels for 16%

profile of v1, /device:TPU:29, one launch (start us, length us, event | category | flops | bytes accessed | tf_op | source)
XLA Modules:
  0.0 31.1 jit_solution(9140923874241031366)
XLA Ops:
  0.7 0.0 copy-start.1
  0.7 2.6 %shard_map.122 = (bf16[512,512]{1,0:T(8,128)(2,1)S(1)}, bf16[512,512]{1,0:T(8,128)(2,1)S(1)}) custom-call(bf16[512,512]{1,0:T(8,128)(2,1)} %out_hbm.1, bf16[512,512]{1,0:T(8,128)(2,1)} %tail_hbm.1), custom_call_target="tpu_custom_call" | custom-call | tf_op jit(solution)/shard_map/pallas_call | solution.py:248
  3.4 0.1 add_convert_fusion.flags_ref
  3.4 0.0 copy-done.1
  3.4 1.1 %shard_map.123 = (f32[512,512]{1,0:T(8,128)S(1)}, bf16[512,512]{1,0:T(8,128)(2,1)S(1)}) custom-call(s32[4]{0:T(128)S(1)} %add_convert_fusion.flags_ref, bf16[512,512]{1,0:T(8,128)(2,1)S(1)} %copy-done.1, bf16[512,512]{1,0:T(8,128)(2,1)S(1)} %get-tuple-element.10.out_ref, bf16[512,512]{1,0:T(8,128)(2,1)S(1)} %get-tuple-element.11.after_ref.right_ref.a_ref), custom_call_target="tpu_custom_call" | custom-call | tf_op jit(solution)/shard_map/pallas_call | solution.py:258
  4.6 0.7 %collective-permute-start = (bf16[512,512]{1,0:T(8,128)(2,1)S(1)}, bf16[512,512]{1,0:T(8,128)(2,1)S(1)}, u32[]{:S(2)}, u32[]{:S(2)}) collective-permute-start(bf16[512,512]{1,0:T(8,128)(2,1)S(1)} %get-tuple-element.13), channel_id=1, source_target_pairs={{0,8},{16,24},{8,0},{24,16},{1,9},{17,25},{9,1},{25,17},{2,10},{18... | collective-permute-start | bytes 1572872 | tf_op jit(solution)/shard_map/ppermute | solution.py:234
  5.3 0.9 %collective-permute-start.2 = (bf16[512,512]{1,0:T(8,128)(2,1)S(1)}, bf16[512,512]{1,0:T(8,128)(2,1)S(1)}, u32[]{:S(2)}, u32[]{:S(2)}) collective-permute-start(bf16[512,512]{1,0:T(8,128)(2,1)S(1)} %get-tuple-element.11.after_ref.right_ref.a_ref), channel_id=1, source_target_pairs={{1,0},{0,8},{8,5},{9,13},{17,16},{24,25},{16,24},{25,17},{19,18},{... | collective-permute-start | bytes 1572872 | tf_op jit(solution)/shard_map/ppermute | solution.py:234
  6.3 0.6 %collective-permute-done.other_ref = bf16[512,512]{1,0:T(8,128)(2,1)S(1)} collective-permute-done((bf16[512,512]{1,0:T(8,128)(2,1)S(1)}, bf16[512,512]{1,0:T(8,128)(2,1)S(1)}, u32[]{:S(2)}, u32[]{:S(2)}) %collective-permute-start) | collective-permute-done | bytes 524320 | tf_op jit(solution)/shard_map/ppermute | solution.py:234
  6.8 0.9 %shard_map.124 = (f32[512,512]{1,0:T(8,128)S(1)}, bf16[512,512]{1,0:T(8,128)(2,1)S(1)}) custom-call(s32[4]{0:T(128)S(1)} %add_convert_fusion.flags_ref, f32[512,512]{1,0:T(8,128)S(1)} %get-tuple-element.12.left_ref, bf16[512,512]{1,0:T(8,128)(2,1)S(1)} %collective-permute-done.other_ref, bf16[512,512]{1,0:T(8,128)(2,1)S(1)} %get-tuple-element.11.after_ref.right_ref.a_ref), custom_call_target="tpu_custom_call" | custom-call | tf_op jit(solution)/shard_map/pallas_call | solution.py:262
  7.7 0.0 copy-start
  7.7 0.4 %collective-permute-start.1 = (bf16[512,512]{1,0:T(8,128)(2,1)S(1)}, bf16[512,512]{1,0:T(8,128)(2,1)S(1)}, u32[]{:S(2)}, u32[]{:S(2)}) collective-permute-start(bf16[512,512]{1,0:T(8,128)(2,1)S(1)} %get-tuple-element.15), channel_id=1, source_target_pairs={{0,12},{9,1},{16,0},{8,24},{24,16},{25,9},{1,17},{17,25},{18,30},{... | collective-permute-start | bytes 1572872 | tf_op jit(solution)/shard_map/ppermute | solution.py:234
  9.5 0.0 copy-start.2
  9.5 0.0 copy-start.3
  9.5 0.0 copy-start.5
  9.5 4.7 %collective-permute-done.2.first_ref.b_ref.a_ref = bf16[512,512]{1,0:T(8,128)(2,1)S(1)} collective-permute-done((bf16[512,512]{1,0:T(8,128)(2,1)S(1)}, bf16[512,512]{1,0:T(8,128)(2,1)S(1)}, u32[]{:S(2)}, u32[]{:S(2)}) %collective-permute-start.2) | collective-permute-done | bytes 524320 | tf_op jit(solution)/shard_map/ppermute | solution.py:234
  14.2 0.6 %shard_map.126.after_ref = bf16[512,512]{1,0:T(8,128)(2,1)S(1)} custom-call(bf16[512,512]{1,0:T(8,128)(2,1)S(1)} %get-tuple-element.11.after_ref.right_ref.a_ref, bf16[512,512]{1,0:T(8,128)(2,1)S(1)} %collective-permute-done.2.first_ref.b_ref.a_ref), custom_call_target="tpu_custom_call" | custom-call | tf_op jit(solution)/shard_map/pallas_call | solution.py:264
  14.8 0.1 collective-permute-start.4
  14.9 0.0 copy-done
  14.9 0.0 copy-done.2
  14.9 0.0 copy-done.3
  14.9 0.0 copy-done.5
  14.9 1.5 %shard_map.127.after_ref.factor_ref = f32[512,512]{1,0:T(8,128)S(1)} custom-call(f32[4,4]{1,0:T(4,128)S(1)} %copy-done.5, s32[1]{0:T(128)S(6)} %copy.13.span_ref, f32[1]{0:T(128)S(6)} %copy.14.partition_ref, s32[1,512]{1,0:T(1,128)S(1)} %copy-done.2, s32[1,512]{1,0:T(1,128)S(1)} %copy-done.3, f32[512,512]{1,0:T(8,128)S(1)} %copy-done, ...), custom_call_target="tpu_custom_call" | custom-call | tf_op jit(solution)/shard_map/pallas_call | solution.py:266
  16.4 9.9 %collective-permute-done.1.middle_ref.b_ref = bf16[512,512]{1,0:T(8,128)(2,1)S(1)} collective-permute-done((bf16[512,512]{1,0:T(8,128)(2,1)S(1)}, bf16[512,512]{1,0:T(8,128)(2,1)S(1)}, u32[]{:S(2)}, u32[]{:S(2)}) %collective-permute-start.1) | collective-permute-done | bytes 524320 | tf_op jit(solution)/shard_map/ppermute | solution.py:234
  26.4 0.6 %shard_map.128 = bf16[512,512]{1,0:T(8,128)(2,1)S(1)} custom-call(s32[4]{0:T(128)S(1)} %add_convert_fusion.flags_ref, bf16[512,512]{1,0:T(8,128)(2,1)S(1)} %collective-permute-done.2.first_ref.b_ref.a_ref, bf16[512,512]{1,0:T(8,128)(2,1)S(1)} %collective-permute-done.1.middle_ref.b_ref, f32[512,512]{1,0:T(8,128)S(1)} %shard_map.127.after_ref.factor_ref), custom_call_target="tpu_custom_call" | custom-call | tf_op jit(solution)/shard_map/pallas_call | solution.py:269
  27.0 0.0 copy-start.6
  27.0 0.1 collective-permute-start.3
  27.0 0.0 copy-done.4
  27.1 0.6 %copy-done.6 = f32[4]{0:T(128)S(1)} copy-done((f32[4]{0:T(128)S(1)}, f32[4]{0:T(128)}, u32[]{:S(2)}) %copy-start.6) | copy-done | bytes 40
  27.6 1.3 %shard_map.125 = (f32[512,512]{1,0:T(8,128)S(1)}, f32[4,512]{1,0:T(4,128)S(1)}) custom-call(s32[4]{0:T(128)S(1)} %add_convert_fusion.flags_ref, s32[4,4]{1,0:T(4,128)S(1)} %copy-done.4, f32[4]{0:T(128)S(1)} %copy-done.6, s32[1,512]{1,0:T(1,128)S(1)} %copy-done.2, s32[1,512]{1,0:T(1,128)S(1)} %copy-done.3, f32[512,512]{1,0:T(8,128)S(1)} %get-tuple-element.14.left_ref, ...), custom_call_target="tpu_custom_call" | custom-call | tf_op jit(solution)/shard_map/pallas_call | solution.py:271
  28.9 0.0 collective-permute-done.4.last_ref
  29.0 0.0 collective-permute-done.3.inside_ref
  29.0 2.1 %shard_map.129 = (f32[512,512]{1,0:T(8,128)}, f32[512,512]{1,0:T(8,128)}) custom-call(f32[4,512]{1,0:T(4,128)S(1)} %get-tuple-element.16.scale_ref, f32[512,512]{1,0:T(8,128)S(1)} %get-tuple-element.17.partial_ref, f32[512,512]{1,0:T(8,128)S(1)} %shard_map.127.after_ref.factor_ref, bf16[512,512]{1,0:T(8,128)(2,1)S(1)} %collective-permute-done.3.inside_ref, ...), custom_call_target="tpu_custom_call" | custom-call | tf_op jit(solution)/shard_map/pallas_call | solution.py:277
  (1 shorter events, 0.0 us)
Async XLA Ops:
  0.7 2.7 %copy-start.1 = (bf16[512,512]{1,0:T(8,128)(2,1)S(1)}, bf16[512,512]{1,0:T(8,128)(2,1)}, u32[]{:S(2)}) copy-start(bf16[512,512]{1,0:T(8,128)(2,1)} %head_ref.3) | copy-start | bytes 1572868
  4.6 2.3 %collective-permute-start = (bf16[512,512]{1,0:T(8,128)(2,1)S(1)}, bf16[512,512]{1,0:T(8,128)(2,1)S(1)}, u32[]{:S(2)}, u32[]{:S(2)}) collective-permute-start(bf16[512,512]{1,0:T(8,128)(2,1)S(1)} %get-tuple-element.13), channel_id=1, source_target_pairs={{0,8},{16,24},{8,0},{24,16},{1,9},{17,25},{9,1},{25,17},{2,10},{18... | collective-permute-start | bytes 1572872 | tf_op jit(solution)/shard_map/ppermute | solution.py:234
  5.3 8.9 %collective-permute-start.2 = (bf16[512,512]{1,0:T(8,128)(2,1)S(1)}, bf16[512,512]{1,0:T(8,128)(2,1)S(1)}, u32[]{:S(2)}, u32[]{:S(2)}) collective-permute-start(bf16[512,512]{1,0:T(8,128)(2,1)S(1)} %get-tuple-element.11.after_ref.right_ref.a_ref), channel_id=1, source_target_pairs={{1,0},{0,8},{8,5},{9,13},{17,16},{24,25},{16,24},{25,17},{19,18},{... | collective-permute-start | bytes 1572872 | tf_op jit(solution)/shard_map/ppermute | solution.py:234
  7.7 7.2 %copy-start = (f32[512,512]{1,0:T(8,128)S(1)}, f32[512,512]{1,0:T(8,128)}, u32[]{:S(2)}) copy-start(f32[512,512]{1,0:T(8,128)} %pair_ref.1) | copy-start | bytes 3145732
  7.7 18.6 %collective-permute-start.1 = (bf16[512,512]{1,0:T(8,128)(2,1)S(1)}, bf16[512,512]{1,0:T(8,128)(2,1)S(1)}, u32[]{:S(2)}, u32[]{:S(2)}) collective-permute-start(bf16[512,512]{1,0:T(8,128)(2,1)S(1)} %get-tuple-element.15), channel_id=1, source_target_pairs={{0,12},{9,1},{16,0},{8,24},{24,16},{25,9},{1,17},{17,25},{18,30},{... | collective-permute-start | bytes 1572872 | tf_op jit(solution)/shard_map/ppermute | solution.py:234
  9.5 5.4 %copy-start.2 = (s32[1,512]{1,0:T(1,128)S(1)}, s32[1,512]{1,0:T(1,128)}, u32[]{:S(2)}) copy-start(s32[1,512]{1,0:T(1,128)} %head_ref.5) | copy-start | bytes 6148
  9.5 5.4 %copy-start.3 = (s32[1,512]{1,0:T(1,128)S(1)}, s32[1,512]{1,0:T(1,128)}, u32[]{:S(2)}) copy-start(s32[1,512]{1,0:T(1,128)} %tail_ref.3) | copy-start | bytes 6148
  9.5 5.4 %copy-start.5 = (f32[4,4]{1,0:T(4,128)S(1)}, f32[4,4]{1,0:T(4,128)}, u32[]{:S(2)}) copy-start(f32[4,4]{1,0:T(4,128)} %weight_ref.1) | copy-start | bytes 196
  14.8 14.1 %collective-permute-start.4 = (bf16[512,512]{1,0:T(8,128)(2,1)S(1)}, bf16[512,512]{1,0:T(8,128)(2,1)S(1)}, u32[]{:S(2)}, u32[]{:S(2)}) collective-permute-start(bf16[512,512]{1,0:T(8,128)(2,1)S(1)} %shard_map.126.after_ref), channel_id=1, source_target_pairs={{16,22},{0,8},{8,24},{24,16},{25,31},{9,1},{1,17},{17,25},{2,0},{1... | collective-permute-start | bytes 1572872 | tf_op jit(solution)/shard_map/ppermute | solution.py:234
  26.4 0.7 %copy-start.4 = (s32[4,4]{1,0:T(4,128)S(1)}, s32[4,4]{1,0:T(4,128)}, u32[]{:S(2)}) copy-start(s32[4,4]{1,0:T(4,128)} %mask_ref.1) | copy-start | bytes 196
  27.0 0.7 %copy-start.6 = (f32[4]{0:T(128)S(1)}, f32[4]{0:T(128)}, u32[]{:S(2)}) copy-start(f32[4]{0:T(128)} %split_ref.1) | copy-start | bytes 52
  27.0 2.0 %collective-permute-start.3 = (bf16[512,512]{1,0:T(8,128)(2,1)S(1)}, bf16[512,512]{1,0:T(8,128)(2,1)S(1)}, u32[]{:S(2)}, u32[]{:S(2)}) collective-permute-start(bf16[512,512]{1,0:T(8,128)(2,1)S(1)} %shard_map.128), channel_id=1, source_target_pairs={{0,8},{16,24},{8,0},{24,16},{1,9},{17,25},{9,1},{25,17},{2,10},{18... | collective-permute-start | bytes 1572872 | tf_op jit(solution)/shard_map/ppermute | solution.py:234

commit v2 on v1

--- a/solution.py
+++ b/solution.py
@@ -34,30 +34,16 @@
 
 
 def right_kernel(out_hbm, tail_hbm, out_ref, code_ref, tail_ref, sems):
-    size = out_ref.shape[0]
-    step = size // CHUNKS
-    parts = [pl.ds(k * step, step) for k in range(CHUNKS)]
-    tails = [
-        pltpu.make_async_copy(tail_hbm.at[part, :], tail_ref.at[part, :], sems.at[0, k])
-        for k, part in enumerate(parts)
-    ]
-    outs = [
-        pltpu.make_async_copy(out_hbm.at[part, :], out_ref.at[part, :], sems.at[1, k])
-        for k, part in enumerate(parts)
-    ]
-    for copy in tails + outs:
-        copy.start()
-    for copy in tails:
-        copy.wait()
-    for part, copy in zip(parts, outs):
-        copy.wait()
-        term = lax.dot_general(
-            out_ref[part, :],
-            tail_ref[...],
-            (((1,), (1,)), ((), ())),
-            preferred_element_type=jnp.float32,
-        )
-        code_ref[part, :] = encode(term * (1.0 / size))
+    tail = pltpu.make_async_copy(tail_hbm, tail_ref, sems.at[0])
+    out = pltpu.make_async_copy(out_hbm, out_ref, sems.at[1])
+    tail.start()
+    out.start()
+    tail.wait()
+    out.wait()
+    term = lax.dot_general(
+        out_ref[...], tail_ref[...], (((1,), (1,)), ((), ())), preferred_element_type=jnp.float32
+    )
+    code_ref[...] = encode(term * (1.0 / term.shape[0]))
 
 
 def left_kernel(flags_ref, head_ref, out_ref, after_ref, left_ref, code_ref):
@@ -159,15 +145,38 @@
 
 
 def last_kernel(
-    scale_ref, partial_ref, factor_ref, inside_ref, last_ref, outside_ref, prob_ref
-):
-    cell = pl.program_id(0)
-    step = outside_ref.shape[0]
-    rows = pl.ds(cell * step, step)
-    right = decode(inside_ref[rows, :]) + decode(last_ref[rows, :])
-    total = partial_ref[rows, :] + scale_ref[pl.ds(cell, 1), :] * right
-    outside_ref[...] = total
-    prob_ref[...] = total * factor_ref[rows, :]
+    scale_ref,
+    partial_ref,
+    factor_ref,
+    inside_ref,
+    last_ref,
+    outside_hbm,
+    prob_hbm,
+    outside_ref,
+    prob_ref,
+    sems,
+):
+    cells = scale_ref.shape[0]
+    step = outside_ref.shape[0] // cells
+    copies = []
+    for cell in range(cells):
+        rows = pl.ds(cell * step, step)
+        right = decode(inside_ref[rows, :]) + decode(last_ref[rows, :])
+        total = partial_ref[rows, :] + scale_ref[pl.ds(cell, 1), :] * right
+        outside_ref[rows, :] = total
+        copies.append(
+            pltpu.make_async_copy(
+                outside_ref.at[rows, :], outside_hbm.at[rows, :], sems.at[0, cell]
+            )
+        )
+        copies[-1].start()
+        prob_ref[rows, :] = total * factor_ref[rows, :]
+        copies.append(
+            pltpu.make_async_copy(prob_ref.at[rows, :], prob_hbm.at[rows, :], sems.at[1, cell])
+        )
+        copies[-1].start()
+    for copy in copies:
+        copy.wait()
 
 
 def routes(col_count):
@@ -228,7 +237,7 @@
     ).astype(jnp.int32)
     code = pltpu.VMEM((size, size), jnp.bfloat16)
     full = pltpu.VMEM((size, size), jnp.float32)
-    output = jax.ShapeDtypeStruct((size, size), jnp.float32)
+    output = pltpu.HBM((size, size), jnp.float32)
 
     def send(x, pairs):
         x = lax.ppermute(x, ("row", "col"), pairs)
@@ -249,7 +258,7 @@
         right_kernel,
         [HBM] * 2,
         (code, code),
-        [code, pltpu.SemaphoreType.DMA((2, CHUNKS))],
+        [code, pltpu.SemaphoreType.DMA((2,))],
     )(
         pltpu.with_memory_space_constraint(outside, pltpu.HBM),
         pltpu.with_memory_space_constraint(inside_tail, pltpu.HBM),
@@ -273,13 +282,12 @@
         [SMEM] * 3 + [VMEM] * 5,
         (full, pltpu.VMEM((cells, size), jnp.float32)),
     )(flags, pair_mask, split_weight, seq_head, seq_tail, left, q3, q1)
-    block = pl.BlockSpec((size // cells, size), lambda cell: (cell, 0))
     return pl.pallas_call(
         last_kernel,
-        grid=(cells,),
         in_specs=[VMEM] * 5,
-        out_specs=(block, block),
+        out_specs=(HBM, HBM),
         out_shape=(output, output),
+        scratch_shapes=[full, full, pltpu.SemaphoreType.DMA((2, cells))],
         compiler_params=PARAMS,
     )(scale, partial, factor, i2, q2)
 

time: 31.2 us -> 29.9 us (0.958)
  Pallas kernels: 10.8 us -> 9.4 us
    pallas_call x1, Pallas kernels: 2.63 us -> 1.83 us  [routed(): call(right_kernel, [HBM] * 2, (code, code), [code, pltpu.SemaphoreType.DM...]
    pallas_call x1, Pallas kernels: 2.1 us -> 1.54 us  [routed(): pl.pallas_call(last_kernel, in_specs=[VMEM] * 5, out_specs=(HBM, HBM), ou...]
  transfers between devices with their start and end apart: 5 -> 5, of which waited for: 3 -> 3; matrix products, arithmetic and copies ran while one was open for 0% -> 0% of each run, Pallas kernels for 16% -> 17%
where the time goes in v2:
time: 29.9 us; the launch traced here: 29.7 us
  waiting for transfers between devices  15.2 us (51%)
  Pallas kernels  9.4 us (31%)
  starting transfers between devices  2.27 us (8%)
  between operations  2.18 us (7%)
  local copies, waits for them, and re-layouts  0.59 us (2%)
    ppermute x5, waiting for transfers between devices, send(): x = lax.ppermute(x, ('row', 'col'), pairs)  15.2 us
    ppermute x5, starting transfers between devices, send(): x = lax.ppermute(x, ('row', 'col'), pairs)  2.27 us
    pallas_call x1, Pallas kernels, routed(): call(right_kernel, [HBM] * 2, (code, code), [code, pltpu.SemaphoreType.DM...  1.83 us
    pallas_call x1, Pallas kernels, routed(): pl.pallas_call(last_kernel, in_specs=[VMEM] * 5, out_specs=(HBM, HBM), ou...  1.54 us
    pallas_call x1, Pallas kernels, routed(): call(factor_kernel, [SMEM] * 3 + [VMEM] * 3 + [ANY], full)  1.5 us
    pallas_call x1, Pallas kernels, routed(): call(partial_kernel, [SMEM] * 3 + [VMEM] * 5, (full, pltpu.VMEM((cells, s...  1.32 us
    pallas_call x1, Pallas kernels, routed(): call(left_kernel, [SMEM] + [VMEM] * 2 + [ANY], (full, code))  1.12 us
    pallas_call x1, Pallas kernels, routed(): call(chip_kernel, [SMEM] + [VMEM] * 3, (full, code))(flags, left, i0, right)  0.87 us
  transfers between devices with their start and end apart: 5, of which 3 were waited for; matrix products, arithmetic and copies ran while one was open for 0% of the time, Pallas kernels for 17%

profile of v2, /device:TPU:29, one launch (start us, length us, event | category | flops | bytes accessed | tf_op | source)
XLA Modules:
  0.0 29.7 jit_solution(10452276328276607895)
XLA Ops:
  0.7 0.0 copy-start.1
  0.7 1.8 %shard_map.122 = (bf16[512,512]{1,0:T(8,128)(2,1)S(1)}, bf16[512,512]{1,0:T(8,128)(2,1)S(1)}) custom-call(bf16[512,512]{1,0:T(8,128)(2,1)} %out_hbm.1, bf16[512,512]{1,0:T(8,128)(2,1)} %tail_hbm.1), custom_call_target="tpu_custom_call" | custom-call | tf_op jit(solution)/shard_map/pallas_call | solution.py:257
  2.6 0.1 add_convert_fusion.flags_ref
  2.6 0.0 copy-done.1
  2.6 1.1 %shard_map.123 = (f32[512,512]{1,0:T(8,128)S(1)}, bf16[512,512]{1,0:T(8,128)(2,1)S(1)}) custom-call(s32[4]{0:T(128)S(1)} %add_convert_fusion.flags_ref, bf16[512,512]{1,0:T(8,128)(2,1)S(1)} %copy-done.1, bf16[512,512]{1,0:T(8,128)(2,1)S(1)} %get-tuple-element.10.out_ref, bf16[512,512]{1,0:T(8,128)(2,1)S(1)} %get-tuple-element.11.after_ref.right_ref.a_ref), custom_call_target="tpu_custom_call" | custom-call | tf_op jit(solution)/shard_map/pallas_call | solution.py:267
  3.8 0.7 %collective-permute-start = (bf16[512,512]{1,0:T(8,128)(2,1)S(1)}, bf16[512,512]{1,0:T(8,128)(2,1)S(1)}, u32[]{:S(2)}, u32[]{:S(2)}) collective-permute-start(bf16[512,512]{1,0:T(8,128)(2,1)S(1)} %get-tuple-element.13), channel_id=1, source_target_pairs={{0,8},{16,24},{8,0},{24,16},{1,9},{17,25},{9,1},{25,17},{2,10},{18... | collective-permute-start | bytes 1572872 | tf_op jit(solution)/shard_map/ppermute | solution.py:243
  4.5 0.9 %collective-permute-start.2 = (bf16[512,512]{1,0:T(8,128)(2,1)S(1)}, bf16[512,512]{1,0:T(8,128)(2,1)S(1)}, u32[]{:S(2)}, u32[]{:S(2)}) collective-permute-start(bf16[512,512]{1,0:T(8,128)(2,1)S(1)} %get-tuple-element.11.after_ref.right_ref.a_ref), channel_id=1, source_target_pairs={{1,0},{0,8},{8,5},{9,13},{17,16},{24,25},{16,24},{25,17},{19,18},{... | collective-permute-start | bytes 1572872 | tf_op jit(solution)/shard_map/ppermute | solution.py:243
  5.5 0.6 %collective-permute-done.other_ref = bf16[512,512]{1,0:T(8,128)(2,1)S(1)} collective-permute-done((bf16[512,512]{1,0:T(8,128)(2,1)S(1)}, bf16[512,512]{1,0:T(8,128)(2,1)S(1)}, u32[]{:S(2)}, u32[]{:S(2)}) %collective-permute-start) | collective-permute-done | bytes 524320 | tf_op jit(solution)/shard_map/ppermute | solution.py:243
  6.1 0.9 %shard_map.124 = (f32[512,512]{1,0:T(8,128)S(1)}, bf16[512,512]{1,0:T(8,128)(2,1)S(1)}) custom-call(s32[4]{0:T(128)S(1)} %add_convert_fusion.flags_ref, f32[512,512]{1,0:T(8,128)S(1)} %get-tuple-element.12.left_ref, bf16[512,512]{1,0:T(8,128)(2,1)S(1)} %collective-permute-done.other_ref, bf16[512,512]{1,0:T(8,128)(2,1)S(1)} %get-tuple-element.11.after_ref.right_ref.a_ref), custom_call_target="tpu_custom_call" | custom-call | tf_op jit(solution)/shard_map/pallas_call | solution.py:271
  6.9 0.0 copy-start
  6.9 0.4 %collective-permute-start.1 = (bf16[512,512]{1,0:T(8,128)(2,1)S(1)}, bf16[512,512]{1,0:T(8,128)(2,1)S(1)}, u32[]{:S(2)}, u32[]{:S(2)}) collective-permute-start(bf16[512,512]{1,0:T(8,128)(2,1)S(1)} %get-tuple-element.15), channel_id=1, source_target_pairs={{0,12},{9,1},{16,0},{8,24},{24,16},{25,9},{1,17},{17,25},{18,30},{... | collective-permute-start | bytes 1572872 | tf_op jit(solution)/shard_map/ppermute | solution.py:243
  8.7 0.0 copy-start.2
  8.7 0.0 copy-start.3
  8.7 0.0 copy-start.5
  8.7 4.6 %collective-permute-done.2.first_ref.b_ref.a_ref = bf16[512,512]{1,0:T(8,128)(2,1)S(1)} collective-permute-done((bf16[512,512]{1,0:T(8,128)(2,1)S(1)}, bf16[512,512]{1,0:T(8,128)(2,1)S(1)}, u32[]{:S(2)}, u32[]{:S(2)}) %collective-permute-start.2) | collective-permute-done | bytes 524320 | tf_op jit(solution)/shard_map/ppermute | solution.py:243
  13.4 0.6 %shard_map.126.after_ref = bf16[512,512]{1,0:T(8,128)(2,1)S(1)} custom-call(bf16[512,512]{1,0:T(8,128)(2,1)S(1)} %get-tuple-element.11.after_ref.right_ref.a_ref, bf16[512,512]{1,0:T(8,128)(2,1)S(1)} %collective-permute-done.2.first_ref.b_ref.a_ref), custom_call_target="tpu_custom_call" | custom-call | tf_op jit(solution)/shard_map/pallas_call | solution.py:273
  14.0 0.1 collective-permute-start.4
  14.1 0.0 copy-done
  14.1 0.0 copy-done.2
  14.1 0.0 copy-done.3
  14.1 0.0 copy-done.5
  14.1 1.5 %shard_map.127.after_ref.factor_ref = f32[512,512]{1,0:T(8,128)S(1)} custom-call(f32[4,4]{1,0:T(4,128)S(1)} %copy-done.5, s32[1]{0:T(128)S(6)} %copy.13.span_ref, f32[1]{0:T(128)S(6)} %copy.14.partition_ref, s32[1,512]{1,0:T(1,128)S(1)} %copy-done.2, s32[1,512]{1,0:T(1,128)S(1)} %copy-done.3, f32[512,512]{1,0:T(8,128)S(1)} %copy-done, ...), custom_call_target="tpu_custom_call" | custom-call | tf_op jit(solution)/shard_map/pallas_call | solution.py:275
  15.6 10.0 %collective-permute-done.1.middle_ref.b_ref = bf16[512,512]{1,0:T(8,128)(2,1)S(1)} collective-permute-done((bf16[512,512]{1,0:T(8,128)(2,1)S(1)}, bf16[512,512]{1,0:T(8,128)(2,1)S(1)}, u32[]{:S(2)}, u32[]{:S(2)}) %collective-permute-start.1) | collective-permute-done | bytes 524320 | tf_op jit(solution)/shard_map/ppermute | solution.py:243
  25.6 0.6 %shard_map.128 = bf16[512,512]{1,0:T(8,128)(2,1)S(1)} custom-call(s32[4]{0:T(128)S(1)} %add_convert_fusion.flags_ref, bf16[512,512]{1,0:T(8,128)(2,1)S(1)} %collective-permute-done.2.first_ref.b_ref.a_ref, bf16[512,512]{1,0:T(8,128)(2,1)S(1)} %collective-permute-done.1.middle_ref.b_ref, f32[512,512]{1,0:T(8,128)S(1)} %shard_map.127.after_ref.factor_ref), custom_call_target="tpu_custom_call" | custom-call | tf_op jit(solution)/shard_map/pallas_call | solution.py:278
  26.2 0.0 copy-start.6
  26.2 0.1 collective-permute-start.3
  26.3 0.0 copy-done.4
  26.3 0.6 %copy-done.6 = f32[4]{0:T(128)S(1)} copy-done((f32[4]{0:T(128)S(1)}, f32[4]{0:T(128)}, u32[]{:S(2)}) %copy-start.6) | copy-done | bytes 40
  26.8 1.3 %shard_map.125 = (f32[512,512]{1,0:T(8,128)S(1)}, f32[4,512]{1,0:T(4,128)S(1)}) custom-call(s32[4]{0:T(128)S(1)} %add_convert_fusion.flags_ref, s32[4,4]{1,0:T(4,128)S(1)} %copy-done.4, f32[4]{0:T(128)S(1)} %copy-done.6, s32[1,512]{1,0:T(1,128)S(1)} %copy-done.2, s32[1,512]{1,0:T(1,128)S(1)} %copy-done.3, f32[512,512]{1,0:T(8,128)S(1)} %get-tuple-element.14.left_ref, ...), custom_call_target="tpu_custom_call" | custom-call | tf_op jit(solution)/shard_map/pallas_call | solution.py:280
  28.2 0.0 collective-permute-done.4.last_ref
  28.2 0.0 collective-permute-done.3.inside_ref
  28.2 1.5 %shard_map.129 = (f32[512,512]{1,0:T(8,128)}, f32[512,512]{1,0:T(8,128)}) custom-call(f32[4,512]{1,0:T(4,128)S(1)} %get-tuple-element.16.scale_ref, f32[512,512]{1,0:T(8,128)S(1)} %get-tuple-element.17.partial_ref, f32[512,512]{1,0:T(8,128)S(1)} %shard_map.127.after_ref.factor_ref, bf16[512,512]{1,0:T(8,128)(2,1)S(1)} %collective-permute-done.3.inside_ref, ...), custom_call_target="tpu_custom_call" | custom-call | tf_op jit(solution)/shard_map/pallas_call | solution.py:285
  (1 shorter events, 0.0 us)
Async XLA Ops:
  0.7 1.9 %copy-start.1 = (bf16[512,512]{1,0:T(8,128)(2,1)S(1)}, bf16[512,512]{1,0:T(8,128)(2,1)}, u32[]{:S(2)}) copy-start(bf16[512,512]{1,0:T(8,128)(2,1)} %head_ref.3) | copy-start | bytes 1572868
  3.8 2.3 %collective-permute-start = (bf16[512,512]{1,0:T(8,128)(2,1)S(1)}, bf16[512,512]{1,0:T(8,128)(2,1)S(1)}, u32[]{:S(2)}, u32[]{:S(2)}) collective-permute-start(bf16[512,512]{1,0:T(8,128)(2,1)S(1)} %get-tuple-element.13), channel_id=1, source_target_pairs={{0,8},{16,24},{8,0},{24,16},{1,9},{17,25},{9,1},{25,17},{2,10},{18... | collective-permute-start | bytes 1572872 | tf_op jit(solution)/shard_map/ppermute | solution.py:243
  4.5 8.8 %collective-permute-start.2 = (bf16[512,512]{1,0:T(8,128)(2,1)S(1)}, bf16[512,512]{1,0:T(8,128)(2,1)S(1)}, u32[]{:S(2)}, u32[]{:S(2)}) collective-permute-start(bf16[512,512]{1,0:T(8,128)(2,1)S(1)} %get-tuple-element.11.after_ref.right_ref.a_ref), channel_id=1, source_target_pairs={{1,0},{0,8},{8,5},{9,13},{17,16},{24,25},{16,24},{25,17},{19,18},{... | collective-permute-start | bytes 1572872 | tf_op jit(solution)/shard_map/ppermute | solution.py:243
  6.9 7.1 %copy-start = (f32[512,512]{1,0:T(8,128)S(1)}, f32[512,512]{1,0:T(8,128)}, u32[]{:S(2)}) copy-start(f32[512,512]{1,0:T(8,128)} %pair_ref.1) | copy-start | bytes 3145732
  6.9 18.6 %collective-permute-start.1 = (bf16[512,512]{1,0:T(8,128)(2,1)S(1)}, bf16[512,512]{1,0:T(8,128)(2,1)S(1)}, u32[]{:S(2)}, u32[]{:S(2)}) collective-permute-start(bf16[512,512]{1,0:T(8,128)(2,1)S(1)} %get-tuple-element.15), channel_id=1, source_target_pairs={{0,12},{9,1},{16,0},{8,24},{24,16},{25,9},{1,17},{17,25},{18,30},{... | collective-permute-start | bytes 1572872 | tf_op jit(solution)/shard_map/ppermute | solution.py:243
  8.7 5.4 %copy-start.2 = (s32[1,512]{1,0:T(1,128)S(1)}, s32[1,512]{1,0:T(1,128)}, u32[]{:S(2)}) copy-start(s32[1,512]{1,0:T(1,128)} %head_ref.5) | copy-start | bytes 6148
  8.7 5.4 %copy-start.3 = (s32[1,512]{1,0:T(1,128)S(1)}, s32[1,512]{1,0:T(1,128)}, u32[]{:S(2)}) copy-start(s32[1,512]{1,0:T(1,128)} %tail_ref.3) | copy-start | bytes 6148
  8.7 5.4 %copy-start.5 = (f32[4,4]{1,0:T(4,128)S(1)}, f32[4,4]{1,0:T(4,128)}, u32[]{:S(2)}) copy-start(f32[4,4]{1,0:T(4,128)} %weight_ref.1) | copy-start | bytes 196
  14.0 14.2 %collective-permute-start.4 = (bf16[512,512]{1,0:T(8,128)(2,1)S(1)}, bf16[512,512]{1,0:T(8,128)(2,1)S(1)}, u32[]{:S(2)}, u32[]{:S(2)}) collective-permute-start(bf16[512,512]{1,0:T(8,128)(2,1)S(1)} %shard_map.126.after_ref), channel_id=1, source_target_pairs={{16,22},{0,8},{8,24},{24,16},{25,31},{9,1},{1,17},{17,25},{2,0},{1... | collective-permute-start | bytes 1572872 | tf_op jit(solution)/shard_map/ppermute | solution.py:243
  25.6 0.7 %copy-start.4 = (s32[4,4]{1,0:T(4,128)S(1)}, s32[4,4]{1,0:T(4,128)}, u32[]{:S(2)}) copy-start(s32[4,4]{1,0:T(4,128)} %mask_ref.1) | copy-start | bytes 196
  26.2 0.7 %copy-start.6 = (f32[4]{0:T(128)S(1)}, f32[4]{0:T(128)}, u32[]{:S(2)}) copy-start(f32[4]{0:T(128)} %split_ref.1) | copy-start | bytes 52
  26.2 2.0 %collective-permute-start.3 = (bf16[512,512]{1,0:T(8,128)(2,1)S(1)}, bf16[512,512]{1,0:T(8,128)(2,1)S(1)}, u32[]{:S(2)}, u32[]{:S(2)}) collective-permute-start(bf16[512,512]{1,0:T(8,128)(2,1)S(1)} %shard_map.128), channel_id=1, source_target_pairs={{0,8},{16,24},{8,0},{24,16},{1,9},{17,25},{9,1},{25,17},{2,10},{18... | collective-permute-start | bytes 1572872 | tf_op jit(solution)/shard_map/ppermute | solution.py:243

commit v3 on v2

--- a/solution.py
+++ b/solution.py
@@ -33,7 +33,7 @@
     return out
 
 
-def right_kernel(out_hbm, tail_hbm, out_ref, code_ref, tail_ref, sems):
+def right_kernel(out_hbm, tail_hbm, out_ref, code_ref, rest_ref, tail_ref, sems):
     tail = pltpu.make_async_copy(tail_hbm, tail_ref, sems.at[0])
     out = pltpu.make_async_copy(out_hbm, out_ref, sems.at[1])
     tail.start()
@@ -44,6 +44,8 @@
         out_ref[...], tail_ref[...], (((1,), (1,)), ((), ())), preferred_element_type=jnp.float32
     )
     code_ref[...] = encode(term * (1.0 / term.shape[0]))
+    half = rest_ref.shape[0]
+    rest_ref[...] = code_ref[pl.ds(half, half), :]
 
 
 def left_kernel(flags_ref, head_ref, out_ref, after_ref, left_ref, code_ref):
@@ -55,31 +57,24 @@
     code_ref[...] = encode(term)
 
 
-def chip_kernel(flags_ref, left_ref, other_ref, right_ref, left_out_ref, code_ref):
+def relay_kernel(flags_ref, right_ref, across_ref, after_ref, code_ref):
+    @pl.when(flags_ref[2] == 1)
+    def _():
+        code_ref[...] = across_ref[...]
+
+    @pl.when(flags_ref[2] == 0)
+    def _():
+        code_ref[...] = right_ref[pl.ds(0, code_ref.shape[0]), :]
+
+
+def chip_kernel(left_ref, other_ref, left_out_ref, code_ref):
     total = left_ref[...] + decode(other_ref[...])
     left_out_ref[...] = total
-
-    @pl.when(flags_ref[1] == 1)
-    def _():
-        code_ref[...] = right_ref[...]
-
-    @pl.when(flags_ref[1] == 0)
-    def _():
-        code_ref[...] = encode(total)
+    code_ref[...] = encode(total)
 
 
 def add_kernel(a_ref, b_ref, code_ref):
     code_ref[...] = encode(decode(a_ref[...]) + decode(b_ref[...]))
-
-
-def choose_kernel(flags_ref, a_ref, b_ref, after_ref, code_ref):
-    @pl.when(flags_ref[2] == 1)
-    def _():
-        code_ref[...] = a_ref[...]
-
-    @pl.when(flags_ref[2] == 0)
-    def _():
-        code_ref[...] = b_ref[...]
 
 
 def masked_row(mask_ref, row, size):
@@ -93,8 +88,26 @@
 
 
 def factor_kernel(
-    weight_ref, span_ref, partition_ref, head_ref, tail_ref, pair_ref, after_ref, factor_ref
-):
+    weight_ref,
+    head_ref,
+    tail_ref,
+    pair_ref,
+    span_hbm,
+    partition_hbm,
+    after_ref,
+    factor_ref,
+    span_ref,
+    partition_ref,
+    sems,
+):
+    scalars = [
+        pltpu.make_async_copy(span_hbm, span_ref, sems.at[0]),
+        pltpu.make_async_copy(partition_hbm, partition_ref, sems.at[1]),
+    ]
+    for copy in scalars:
+        copy.start()
+    for copy in scalars:
+        copy.wait()
     size = pair_ref.shape[0]
     kinds = weight_ref.shape[0]
     step = size // CHUNKS
@@ -124,6 +137,9 @@
     left_ref,
     middle_ref,
     first_ref,
+    across_ref,
+    far_ref,
+    inside_ref,
     partial_ref,
     scale_ref,
 ):
@@ -137,8 +153,15 @@
     for cell in range(cells):
         rows = pl.ds(cell * step, step)
         part = slice(cell * step, (cell + 1) * step)
+        rest = pl.ds(cell * step % far_ref.shape[0], step)
+        even, odd = (far_ref, inside_ref) if 2 * cell < cells else (across_ref, far_ref)
+        code = jnp.where(
+            flags_ref[1] == 1,
+            odd[rest, :].astype(jnp.float32),
+            even[rest, :].astype(jnp.float32),
+        )
         allowed = jnp.where(flags_ref[3] == 1, masked_row(mask_ref, cell, size), 0.0)
-        right = decode(first_ref[rows, :]) * tail_weight
+        right = (decode(first_ref[rows, :]) + decode(code)) * tail_weight
         left = (left_ref[rows, :] + decode(middle_ref[rows, :])) * head_weight[part]
         partial_ref[rows, :] = allowed * (right + left)
         scale_ref[pl.ds(cell, 1), :] = allowed * tail_weight
@@ -148,7 +171,6 @@
     scale_ref,
     partial_ref,
     factor_ref,
-    inside_ref,
     last_ref,
     outside_hbm,
     prob_hbm,
@@ -161,8 +183,7 @@
     copies = []
     for cell in range(cells):
         rows = pl.ds(cell * step, step)
-        right = decode(inside_ref[rows, :]) + decode(last_ref[rows, :])
-        total = partial_ref[rows, :] + scale_ref[pl.ds(cell, 1), :] * right
+        total = partial_ref[rows, :] + scale_ref[pl.ds(cell, 1), :] * decode(last_ref[rows, :])
         outside_ref[rows, :] = total
         copies.append(
             pltpu.make_async_copy(
@@ -185,25 +206,26 @@
     def at(x, y, core, z):
         return (2 * y + core) * col_count + 2 * (z % depth) + x
 
-    first, middle, last, inside = [], [], [], []
+    first, across, far, middle, last, inside = [], [], [], [], [], []
     for z in range(depth):
         o = z % 2
         n = 1 - o
-        first += [(at(1, o, 0, z), at(0, o, 0, z)), (at(0, o, 0, z), at(0, o, 1, z))]
-        first += [(at(0, o, 1, z), at(1, o, 0, z - 2)), (at(1, o, 1, z), at(1, o, 1, z - 2))]
-        first += [(at(1, n, 0, z), at(0, n, 0, z)), (at(0, n, 1, z), at(1, n, 1, z))]
-        first += [(at(0, n, 0, z), at(0, n, 1, z)), (at(1, n, 1, z), at(1, n, 0, z))]
-        middle += [(at(0, o, 0, z), at(0, o, 1, z - 2)), (at(1, o, 1, z), at(1, o, 0, z))]
         for x in range(2):
-            middle += [(at(x, n, x, z), at(x, o, x, z))]
-            last += [(at(x, n, x, z), at(x, n, x, z - 1)), (at(x, o, x, z), at(x, o, 1 - x, z))]
-            for pairs in (middle, last):
-                pairs += [(at(x, o, 1 - x, z), at(x, n, 1 - x, z))]
-                pairs += [(at(x, n, 1 - x, z), at(x, n, x, z))]
-            for core in range(2):
-                for side in range(2):
-                    inside += [(at(x, side, core, z), at(x, side, 1 - core, z))]
-    return first, middle, last, inside
+            mine, other = at(x, o, x, z), at(x, o, 1 - x, z)
+            near, spare = at(x, n, x, z), at(x, n, 1 - x, z)
+            first += [(mine, at(x, o, x, z - 2)), (spare, at(1 - x, n, 1 - x, z))]
+            first += [(near, other), (other, spare)]
+            across += [(other, at(1 - x, o, 1 - x, z)), (mine, other)]
+            middle += [(near, mine), (mine, other), (other, spare), (spare, near)]
+            last += [(near, at(x, n, x, z - 1)), (mine, other), (spare, near)]
+            last += [(other, at(x, o, 1 - x, z ^ 1))]
+            for side in range(2):
+                inside += [(at(x, side, core, z), at(x, side, 1 - core, z)) for core in range(2)]
+            for pairs in (across, far):
+                pairs += [(near, spare), (spare, near)]
+        far += [(at(1, o, 0, z), at(0, o, 0, z)), (at(0, o, 0, z), at(0, o, 1, z))]
+        far += [(at(0, o, 1, z), at(1, o, 0, z - 2)), (at(1, o, 1, z), at(1, o, 1, z - 2))]
+    return first, across, far, middle, last, inside
 
 
 def routed(
@@ -224,17 +246,16 @@
     row_count = lax.axis_size("row")
     row_id = lax.axis_index("row")
     col_id = lax.axis_index("col")
-    first, middle, last, inside = routes(lax.axis_size("col"))
+    first, across, far, middle, last, inside = routes(lax.axis_size("col"))
     reach = (col_id - row_id) % row_count
     reach = jnp.where(reach == 0, row_count, reach)
-    flags = jnp.stack(
-        [
-            col_id >= reach,
-            row_id // 2 == (col_id // 2) % 2,
-            col_id % 2 == 1,
-            row_id == col_id % row_count,
-        ]
-    ).astype(jnp.int32)
+    flags = [
+        col_id >= reach,
+        col_id % 2 == 1,
+        (col_id % 2) * (row_id % 2) == 1,
+        row_id == col_id % row_count,
+    ]
+    flags = jnp.stack(flags).astype(jnp.int32)
     code = pltpu.VMEM((size, size), jnp.bfloat16)
     full = pltpu.VMEM((size, size), jnp.float32)
     output = pltpu.HBM((size, size), jnp.float32)
@@ -254,42 +275,62 @@
             compiler_params=PARAMS,
         )
 
-    held, right = call(
+    half = pltpu.VMEM((size // 2, size), jnp.bfloat16)
+    held, right, rest = call(
         right_kernel,
         [HBM] * 2,
-        (code, code),
+        (code, code, half),
         [code, pltpu.SemaphoreType.DMA((2,))],
     )(
         pltpu.with_memory_space_constraint(outside, pltpu.HBM),
         pltpu.with_memory_space_constraint(inside_tail, pltpu.HBM),
     )
     q1 = send(right, first)
+    qx = send(rest, across)
     left, left_code = call(left_kernel, [SMEM] + [VMEM] * 2 + [ANY], (full, code))(
         flags, inside_head, held, right
     )
     i0 = send(left_code, inside)
-    left, moved = call(chip_kernel, [SMEM] + [VMEM] * 3, (full, code))(flags, left, i0, right)
-    q3 = send(moved, middle)
+    left, moved = call(chip_kernel, [VMEM] * 2, (full, code))(left, i0)
+    q4 = send(moved, middle)
+    relayed = call(relay_kernel, [SMEM] + [VMEM] * 2 + [ANY], half)(
+        flags, right, qx, moved
+    )
+    q3 = send(relayed, far)
     pair = call(add_kernel, [VMEM] * 2, code)(right, q1)
     q2 = send(pair, last)
-    factor = call(factor_kernel, [SMEM] * 3 + [VMEM] * 3 + [ANY], full)(
-        pair_weight, span_blocks, partition, seq_head, seq_tail, inside_pair, pair
-    )
-    chosen = call(choose_kernel, [SMEM] + [VMEM] * 2 + [ANY], code)(flags, q1, q3, factor)
-    i2 = send(chosen, inside)
+    factor = call(
+        factor_kernel,
+        [SMEM] + [VMEM] * 3 + [ANY] * 3,
+        full,
+        [pltpu.SMEM((1,), jnp.int32), pltpu.SMEM((1,), jnp.float32), pltpu.SemaphoreType.DMA((2,))],
+    )(pair_weight, seq_head, seq_tail, inside_pair, span_blocks, partition, pair)
+    i2 = send(q3, inside)
     partial, scale = call(
         partial_kernel,
-        [SMEM] * 3 + [VMEM] * 5,
+        [SMEM] * 3 + [VMEM] * 8,
         (full, pltpu.VMEM((cells, size), jnp.float32)),
-    )(flags, pair_mask, split_weight, seq_head, seq_tail, left, q3, q1)
+    )(
+        flags,
+        pair_mask,
+        split_weight,
+        seq_head,
+        seq_tail,
+        left,
+        q4,
+        q1,
+        qx,
+        q3,
+        i2,
+    )
     return pl.pallas_call(
         last_kernel,
-        in_specs=[VMEM] * 5,
+        in_specs=[VMEM] * 4,
         out_specs=(HBM, HBM),
         out_shape=(output, output),
         scratch_shapes=[full, full, pltpu.SemaphoreType.DMA((2, cells))],
         compiler_params=PARAMS,
-    )(scale, partial, factor, i2, q2)
+    )(scale, partial, factor, q2)
 
 
 def passed_along(x, axis, by):

time: 29.9 us -> 28.7 us (0.960)
  the two profiles are of different devices: /device:TPU:29 before, /device:TPU:0 now
where the time goes in v3:
time: 28.7 us; the launch traced here: 28.5 us
  waiting for transfers between devices  11.5 us (40%)
  Pallas kernels  9.75 us (34%)
  starting transfers between devices  4.4 us (15%)
  between operations  2.16 us (8%)
  local copies, waits for them, and re-layouts  0.65 us (2%)
    ppermute x7, waiting for transfers between devices, send(): x = lax.ppermute(x, ('row', 'col'), pairs)  11.5 us
    ppermute x7, starting transfers between devices, send(): x = lax.ppermute(x, ('row', 'col'), pairs)  4.4 us
    pallas_call x1, Pallas kernels, routed(): call(factor_kernel, [SMEM] + [VMEM] * 3 + [ANY] * 3, full, [pltpu.SMEM((1...  2.09 us
    pallas_call x1, Pallas kernels, routed(): call(right_kernel, [HBM] * 2, (code, code, half), [code, pltpu.SemaphoreT...  1.83 us
    pallas_call x1, Pallas kernels, routed(): call(partial_kernel, [SMEM] * 3 + [VMEM] * 8, (full, pltpu.VMEM((cells, s...  1.57 us
    pallas_call x1, Pallas kernels, routed(): pl.pallas_call(last_kernel, in_specs=[VMEM] * 4, out_specs=(HBM, HBM), ou...  1.46 us
    pallas_call x1, Pallas kernels, routed(): call(left_kernel, [SMEM] + [VMEM] * 2 + [ANY], (full, code))  1.13 us
    unnamed x14, local copies, waits for them, and re-layouts  0.65 us
  transfers between devices with their start and end apart: 7, of which 3 were waited for; matrix products, arithmetic and copies ran while one was open for 0% of the time, Pallas kernels for 19%

profile of v3, /device:TPU:0, one launch (start us, length us, event | category | flops | bytes accessed | tf_op | source)
XLA Modules:
  0.0 28.5 jit_solution(8879456370398248636)
XLA Ops:
  0.7 0.0 copy-start.1
  0.7 1.8 %shard_map.122 = (bf16[512,512]{1,0:T(8,128)(2,1)S(1)}, bf16[512,512]{1,0:T(8,128)(2,1)S(1)}, bf16[256,512]{1,0:T(8,128)(2,1)S(1)}) custom-call(bf16[512,512]{1,0:T(8,128)(2,1)} %out_hbm.1, bf16[512,512]{1,0:T(8,128)(2,1)} %tail_hbm.1), custom_call_target="tpu_custom_call" | custom-call | tf_op jit(solution)/shard_map/pallas_call | solution.py:279
  2.5 0.1 add_convert_fusion.flags_ref
  2.6 0.0 copy-done.1
  2.6 1.1 %shard_map.123 = (f32[512,512]{1,0:T(8,128)S(1)}, bf16[512,512]{1,0:T(8,128)(2,1)S(1)}) custom-call(s32[4]{0:T(128)S(1)} %add_convert_fusion.flags_ref, bf16[512,512]{1,0:T(8,128)(2,1)S(1)} %copy-done.1, bf16[512,512]{1,0:T(8,128)(2,1)S(1)} %get-tuple-element.11.out_ref, bf16[512,512]{1,0:T(8,128)(2,1)S(1)} %get-tuple-element.12.after_ref.right_ref.a_ref), custom_call_target="tpu_custom_call" | custom-call | tf_op jit(solution)/shard_map/pallas_call | solution.py:290
  3.8 0.6 %collective-permute-start = (bf16[512,512]{1,0:T(8,128)(2,1)S(1)}, bf16[512,512]{1,0:T(8,128)(2,1)S(1)}, u32[]{:S(2)}, u32[]{:S(2)}) collective-permute-start(bf16[512,512]{1,0:T(8,128)(2,1)S(1)} %get-tuple-element.14), channel_id=1, source_target_pairs={{0,8},{8,0},{16,24},{24,16},{1,9},{9,1},{17,25},{25,17},{2,10},{10... | collective-permute-start | bytes 1572872 | tf_op jit(solution)/shard_map/ppermute | solution.py:264
  4.3 3.6 %collective-permute-start.2 = (bf16[512,512]{1,0:T(8,128)(2,1)S(1)}, bf16[512,512]{1,0:T(8,128)(2,1)S(1)}, u32[]{:S(2)}, u32[]{:S(2)}) collective-permute-start(bf16[512,512]{1,0:T(8,128)(2,1)S(1)} %get-tuple-element.12.after_ref.right_ref.a_ref), channel_id=1, source_target_pairs={{0,4},{24,25},{16,8},{8,24},{9,13},{17,16},{25,1},{1,17},{18,22},{... | collective-permute-start | bytes 1572872 | tf_op jit(solution)/shard_map/ppermute | solution.py:264
  8.0 0.0 collective-permute-start.3
  8.0 0.0 collective-permute-done.other_ref
  8.0 0.5 %shard_map.124 = (f32[512,512]{1,0:T(8,128)S(1)}, bf16[512,512]{1,0:T(8,128)(2,1)S(1)}) custom-call(f32[512,512]{1,0:T(8,128)S(1)} %get-tuple-element.13.left_ref, bf16[512,512]{1,0:T(8,128)(2,1)S(1)} %collective-permute-done.other_ref), custom_call_target="tpu_custom_call" | custom-call | tf_op jit(solution)/shard_map/pallas_call | solution.py:294
  8.4 5.9 %collective-permute-done.3.across_ref = bf16[256,512]{1,0:T(8,128)(2,1)S(1)} collective-permute-done((bf16[256,512]{1,0:T(8,128)(2,1)S(1)}, bf16[256,512]{1,0:T(8,128)(2,1)S(1)}, u32[]{:S(2)}, u32[]{:S(2)}) %collective-permute-start.3) | collective-permute-done | bytes 262176 | tf_op jit(solution)/shard_map/ppermute | solution.py:264
  14.3 0.6 %shard_map.125 = bf16[256,512]{1,0:T(8,128)(2,1)S(1)} custom-call(s32[4]{0:T(128)S(1)} %add_convert_fusion.flags_ref, bf16[512,512]{1,0:T(8,128)(2,1)S(1)} %get-tuple-element.12.after_ref.right_ref.a_ref, bf16[256,512]{1,0:T(8,128)(2,1)S(1)} %collective-permute-done.3.across_ref, bf16[512,512]{1,0:T(8,128)(2,1)S(1)} %get-tuple-element.16.after_ref), custom_call_target="tpu_custom_call" | custom-call | tf_op jit(solution)/shard_map/pallas_call | solution.py:296
  14.9 0.0 copy-start
  14.9 0.1 collective-permute-start.4
  15.0 0.1 collective-permute-start.1
  15.1 0.1 collective-permute-done.2.first_ref.b_ref
  15.1 0.6 %shard_map.127.after_ref = bf16[512,512]{1,0:T(8,128)(2,1)S(1)} custom-call(bf16[512,512]{1,0:T(8,128)(2,1)S(1)} %get-tuple-element.12.after_ref.right_ref.a_ref, bf16[512,512]{1,0:T(8,128)(2,1)S(1)} %collective-permute-done.2.first_ref.b_ref), custom_call_target="tpu_custom_call" | custom-call | tf_op jit(solution)/shard_map/pallas_call | solution.py:300
  15.8 0.0 copy-start.2
  15.8 0.1 collective-permute-start.6
  15.8 5.5 %collective-permute-done.4.far_ref = bf16[256,512]{1,0:T(8,128)(2,1)S(1)} collective-permute-done((bf16[256,512]{1,0:T(8,128)(2,1)S(1)}, bf16[256,512]{1,0:T(8,128)(2,1)S(1)}, u32[]{:S(2)}, u32[]{:S(2)}) %collective-permute-start.4) | collective-permute-done | bytes 262176 | tf_op jit(solution)/shard_map/ppermute | solution.py:264
  21.3 0.0 collective-permute-start.5
  22.6 0.0 copy-done
  22.7 0.0 copy-done.3
  22.7 0.0 copy-start.4
  22.7 2.1 %shard_map.128.factor_ref = f32[512,512]{1,0:T(8,128)S(1)} custom-call(f32[4,4]{1,0:T(4,128)S(1)} %copy-done.5, s32[1,512]{1,0:T(1,128)S(1)} %copy-done.2, s32[1,512]{1,0:T(1,128)S(1)} %copy-done.3, f32[512,512]{1,0:T(8,128)S(1)} %copy-done, s32[1]{0:T(128)S(6)} %copy.13.span_hbm, f32[1]{0:T(128)S(6)} %copy.14.partition_hbm, ...), custom_call_target="tpu_custom_call" | custom-call | tf_op jit(solution)/shard_map/pallas_call | solution.py:302
  24.8 0.0 copy-start.6
  24.8 0.0 collective-permute-done.5.inside_ref
  24.8 0.0 collective-permute-done.1.middle_ref
  24.8 0.6 %copy-done.6 = f32[4]{0:T(128)S(1)} copy-done((f32[4]{0:T(128)S(1)}, f32[4]{0:T(128)}, u32[]{:S(2)}) %copy-start.6) | copy-done | bytes 40
  25.5 1.6 %shard_map.126 = (f32[512,512]{1,0:T(8,128)S(1)}, f32[4,512]{1,0:T(4,128)S(1)}) custom-call(s32[4]{0:T(128)S(1)} %add_convert_fusion.flags_ref, s32[4,4]{1,0:T(4,128)S(1)} %copy-done.4, f32[4]{0:T(128)S(1)} %copy-done.6, s32[1,512]{1,0:T(1,128)S(1)} %copy-done.2, s32[1,512]{1,0:T(1,128)S(1)} %copy-done.3, f32[512,512]{1,0:T(8,128)S(1)} %get-tuple-element.15.left_ref, ...), custom_call_target="tpu_custom_call" | custom-call | tf_op jit(solution)/shard_map/pallas_call | solution.py:309
  27.0 0.0 collective-permute-done.6.last_ref
  27.0 1.5 %shard_map.129 = (f32[512,512]{1,0:T(8,128)}, f32[512,512]{1,0:T(8,128)}) custom-call(f32[4,512]{1,0:T(4,128)S(1)} %get-tuple-element.18.scale_ref, f32[512,512]{1,0:T(8,128)S(1)} %get-tuple-element.19.partial_ref, f32[512,512]{1,0:T(8,128)S(1)} %shard_map.128.factor_ref, bf16[512,512]{1,0:T(8,128)(2,1)S(1)} %collective-permute-done.6.last_ref), custom_call_target="tpu_custom_call" | custom-call | tf_op jit(solution)/shard_map/pallas_call | solution.py:326
  (5 shorter events, 0.0 us)
Async XLA Ops:
  0.7 1.9 %copy-start.1 = (bf16[512,512]{1,0:T(8,128)(2,1)S(1)}, bf16[512,512]{1,0:T(8,128)(2,1)}, u32[]{:S(2)}) copy-start(bf16[512,512]{1,0:T(8,128)(2,1)} %head_ref.3) | copy-start | bytes 1572868
  3.8 4.2 %collective-permute-start = (bf16[512,512]{1,0:T(8,128)(2,1)S(1)}, bf16[512,512]{1,0:T(8,128)(2,1)S(1)}, u32[]{:S(2)}, u32[]{:S(2)}) collective-permute-start(bf16[512,512]{1,0:T(8,128)(2,1)S(1)} %get-tuple-element.14), channel_id=1, source_target_pairs={{0,8},{8,0},{16,24},{24,16},{1,9},{9,1},{17,25},{25,17},{2,10},{10... | collective-permute-start | bytes 1572872 | tf_op jit(solution)/shard_map/ppermute | solution.py:264
  4.3 10.8 %collective-permute-start.2 = (bf16[512,512]{1,0:T(8,128)(2,1)S(1)}, bf16[512,512]{1,0:T(8,128)(2,1)S(1)}, u32[]{:S(2)}, u32[]{:S(2)}) collective-permute-start(bf16[512,512]{1,0:T(8,128)(2,1)S(1)} %get-tuple-element.12.after_ref.right_ref.a_ref), channel_id=1, source_target_pairs={{0,4},{24,25},{16,8},{8,24},{9,13},{17,16},{25,1},{1,17},{18,22},{... | collective-permute-start | bytes 1572872 | tf_op jit(solution)/shard_map/ppermute | solution.py:264
  8.0 6.4 %collective-permute-start.3 = (bf16[256,512]{1,0:T(8,128)(2,1)S(1)}, bf16[256,512]{1,0:T(8,128)(2,1)S(1)}, u32[]{:S(2)}, u32[]{:S(2)}) collective-permute-start(bf16[256,512]{1,0:T(8,128)(2,1)S(1)} %get-tuple-element.17), channel_id=1, source_target_pairs={{8,9},{0,8},{16,24},{24,16},{1,0},{9,1},{25,17},{17,25},{26,27},{1... | collective-permute-start | bytes 786440 | tf_op jit(solution)/shard_map/ppermute | solution.py:264
  14.9 7.7 %copy-start = (f32[512,512]{1,0:T(8,128)S(1)}, f32[512,512]{1,0:T(8,128)}, u32[]{:S(2)}) copy-start(f32[512,512]{1,0:T(8,128)} %pair_ref.1) | copy-start | bytes 3145732
  14.9 6.4 %collective-permute-start.4 = (bf16[256,512]{1,0:T(8,128)(2,1)S(1)}, bf16[256,512]{1,0:T(8,128)(2,1)S(1)}, u32[]{:S(2)}, u32[]{:S(2)}) collective-permute-start(bf16[256,512]{1,0:T(8,128)(2,1)S(1)} %shard_map.125), channel_id=1, source_target_pairs={{16,24},{24,16},{25,17},{17,25},{1,0},{0,8},{8,5},{9,13},{2,10},{1... | collective-permute-start | bytes 786440 | tf_op jit(solution)/shard_map/ppermute | solution.py:264
  15.0 9.8 %collective-permute-start.1 = (bf16[512,512]{1,0:T(8,128)(2,1)S(1)}, bf16[512,512]{1,0:T(8,128)(2,1)S(1)}, u32[]{:S(2)}, u32[]{:S(2)}) collective-permute-start(bf16[512,512]{1,0:T(8,128)(2,1)S(1)} %get-tuple-element.16.after_ref), channel_id=1, source_target_pairs={{16,0},{0,8},{8,24},{24,16},{25,9},{9,1},{1,17},{17,25},{2,18},{18... | collective-permute-start | bytes 1572872 | tf_op jit(solution)/shard_map/ppermute | solution.py:264
  15.1 7.5 %copy-start.3 = (s32[1,512]{1,0:T(1,128)S(1)}, s32[1,512]{1,0:T(1,128)}, u32[]{:S(2)}) copy-start(s32[1,512]{1,0:T(1,128)} %tail_ref.3) | copy-start | bytes 6148
  15.1 7.5 %copy-start.5 = (f32[4,4]{1,0:T(4,128)S(1)}, f32[4,4]{1,0:T(4,128)}, u32[]{:S(2)}) copy-start(f32[4,4]{1,0:T(4,128)} %weight_ref.1) | copy-start | bytes 196
  15.8 6.9 %copy-start.2 = (s32[1,512]{1,0:T(1,128)S(1)}, s32[1,512]{1,0:T(1,128)}, u32[]{:S(2)}) copy-start(s32[1,512]{1,0:T(1,128)} %head_ref.5) | copy-start | bytes 6148
  15.8 11.3 %collective-permute-start.6 = (bf16[512,512]{1,0:T(8,128)(2,1)S(1)}, bf16[512,512]{1,0:T(8,128)(2,1)S(1)}, u32[]{:S(2)}, u32[]{:S(2)}) collective-permute-start(bf16[512,512]{1,0:T(8,128)(2,1)S(1)} %shard_map.127.after_ref), channel_id=1, source_target_pairs={{16,22},{0,8},{24,16},{8,10},{25,31},{9,1},{17,25},{1,3},{2,0},{18... | collective-permute-start | bytes 1572872 | tf_op jit(solution)/shard_map/ppermute | solution.py:264
  21.3 3.5 %collective-permute-start.5 = (bf16[256,512]{1,0:T(8,128)(2,1)S(1)}, bf16[256,512]{1,0:T(8,128)(2,1)S(1)}, u32[]{:S(2)}, u32[]{:S(2)}) collective-permute-start(bf16[256,512]{1,0:T(8,128)(2,1)S(1)} %collective-permute-done.4.far_ref), channel_id=1, source_target_pairs={{0,8},{8,0},{16,24},{24,16},{1,9},{9,1},{17,25},{25,17},{2,10},{10... | collective-permute-start | bytes 786440 | tf_op jit(solution)/shard_map/ppermute | solution.py:264
  22.7 2.1 %copy-start.4 = (s32[4,4]{1,0:T(4,128)S(1)}, s32[4,4]{1,0:T(4,128)}, u32[]{:S(2)}) copy-start(s32[4,4]{1,0:T(4,128)} %mask_ref.1) | copy-start | bytes 196
  24.8 0.7 %copy-start.6 = (f32[4]{0:T(128)S(1)}, f32[4]{0:T(128)}, u32[]{:S(2)}) copy-start(f32[4]{0:T(128)} %split_ref.1) | copy-start | bytes 52

commit v4 on v3

--- a/solution.py
+++ b/solution.py
@@ -1,3 +1,5 @@
+import functools
+
 import jax
 import jax.numpy as jnp
 from jax import lax
@@ -26,6 +28,10 @@
     return jnp.exp2(jnp.log2(code.astype(jnp.float32)) * 0.1) * 0.25
 
 
+def place():
+    return lax.axis_index("row"), lax.axis_index("col")
+
+
 def pick(codes, value, count):
     out = jnp.full(codes.shape, value(0))
     for k in range(1, count):
@@ -33,7 +39,7 @@
     return out
 
 
-def right_kernel(out_hbm, tail_hbm, out_ref, code_ref, rest_ref, tail_ref, sems):
+def right_kernel(out_hbm, tail_hbm, out_ref, code_ref, top_ref, rest_ref, tail_ref, sems):
     tail = pltpu.make_async_copy(tail_hbm, tail_ref, sems.at[0])
     out = pltpu.make_async_copy(out_hbm, out_ref, sems.at[1])
     tail.start()
@@ -45,26 +51,20 @@
     )
     code_ref[...] = encode(term * (1.0 / term.shape[0]))
     half = rest_ref.shape[0]
+    top_ref[...] = code_ref[pl.ds(0, half), :]
     rest_ref[...] = code_ref[pl.ds(half, half), :]
 
 
-def left_kernel(flags_ref, head_ref, out_ref, after_ref, left_ref, code_ref):
+def left_kernel(rows, head_ref, out_ref, after_ref, left_ref, code_ref):
     term = lax.dot_general(
         head_ref[...], out_ref[...], (((0,), (0,)), ((), ())), preferred_element_type=jnp.float32
     )
-    term = jnp.where(flags_ref[0] == 1, term * (1.0 / term.shape[0]), 0.0)
+    row_id, col_id = place()
+    reach = lax.rem(col_id - row_id + 2 * rows, rows)
+    reach = jnp.where(reach == 0, rows, reach)
+    term = jnp.where(col_id >= reach, term * (1.0 / term.shape[0]), 0.0)
     left_ref[...] = term
     code_ref[...] = encode(term)
-
-
-def relay_kernel(flags_ref, right_ref, across_ref, after_ref, code_ref):
-    @pl.when(flags_ref[2] == 1)
-    def _():
-        code_ref[...] = across_ref[...]
-
-    @pl.when(flags_ref[2] == 0)
-    def _():
-        code_ref[...] = right_ref[pl.ds(0, code_ref.shape[0]), :]
 
 
 def chip_kernel(left_ref, other_ref, left_out_ref, code_ref):
@@ -129,17 +129,16 @@
 
 
 def partial_kernel(
-    flags_ref,
+    rows_count,
     mask_ref,
     split_ref,
     head_ref,
     tail_ref,
     left_ref,
     middle_ref,
-    first_ref,
+    far_ref,
     across_ref,
-    far_ref,
-    inside_ref,
+    direct_ref,
     partial_ref,
     scale_ref,
 ):
@@ -147,21 +146,21 @@
     cells = mask_ref.shape[0]
     step = size // cells
     kinds = split_ref.shape[0]
+    row_id, col_id = place()
+    is_owner = row_id == lax.rem(col_id, rows_count)
     head = column(head_ref[...].astype(jnp.float32)).astype(jnp.int32)
     tail_weight = pick(tail_ref[...], lambda k: split_ref[k], kinds)
     head_weight = pick(head, lambda k: split_ref[k], kinds)
     for cell in range(cells):
         rows = pl.ds(cell * step, step)
         part = slice(cell * step, (cell + 1) * step)
-        rest = pl.ds(cell * step % far_ref.shape[0], step)
-        even, odd = (far_ref, inside_ref) if 2 * cell < cells else (across_ref, far_ref)
-        code = jnp.where(
-            flags_ref[1] == 1,
-            odd[rest, :].astype(jnp.float32),
-            even[rest, :].astype(jnp.float32),
-        )
-        allowed = jnp.where(flags_ref[3] == 1, masked_row(mask_ref, cell, size), 0.0)
-        right = (decode(first_ref[rows, :]) + decode(code)) * tail_weight
+        if 2 * cell < cells:
+            code = direct_ref[rows, :].astype(jnp.float32)
+        else:
+            code = across_ref[pl.ds((cell - cells // 2) * step, step), :].astype(jnp.float32)
+            code = jnp.where(lax.rem(col_id, 2) == 0, code, 0.0)
+        allowed = jnp.where(is_owner, masked_row(mask_ref, cell, size), 0.0)
+        right = (decode(far_ref[rows, :]) + decode(code)) * tail_weight
         left = (left_ref[rows, :] + decode(middle_ref[rows, :])) * head_weight[part]
         partial_ref[rows, :] = allowed * (right + left)
         scale_ref[pl.ds(cell, 1), :] = allowed * tail_weight
@@ -171,6 +170,7 @@
     scale_ref,
     partial_ref,
     factor_ref,
+    relay_ref,
     last_ref,
     outside_hbm,
     prob_hbm,
@@ -178,12 +178,17 @@
     prob_ref,
     sems,
 ):
+    _, col_id = place()
     cells = scale_ref.shape[0]
     step = outside_ref.shape[0] // cells
     copies = []
     for cell in range(cells):
         rows = pl.ds(cell * step, step)
-        total = partial_ref[rows, :] + scale_ref[pl.ds(cell, 1), :] * decode(last_ref[rows, :])
+        right = decode(last_ref[rows, :])
+        if 2 * cell >= cells:
+            code = relay_ref[pl.ds((cell - cells // 2) * step, step), :].astype(jnp.float32)
+            right += decode(jnp.where(lax.rem(col_id, 2) == 1, code, 0.0))
+        total = partial_ref[rows, :] + scale_ref[pl.ds(cell, 1), :] * right
         outside_ref[rows, :] = total
         copies.append(
             pltpu.make_async_copy(
@@ -206,26 +211,28 @@
     def at(x, y, core, z):
         return (2 * y + core) * col_count + 2 * (z % depth) + x
 
-    first, across, far, middle, last, inside = [], [], [], [], [], []
+    first, across, far, direct, middle, relay, last, inside = [[] for _ in range(8)]
     for z in range(depth):
         o = z % 2
         n = 1 - o
         for x in range(2):
             mine, other = at(x, o, x, z), at(x, o, 1 - x, z)
             near, spare = at(x, n, x, z), at(x, n, 1 - x, z)
-            first += [(mine, at(x, o, x, z - 2)), (spare, at(1 - x, n, 1 - x, z))]
-            first += [(near, other), (other, spare)]
+            first += [(mine, other), (other, mine)]
+            first += [(spare, at(1 - x, n, 1 - x, z)), (near, spare)]
             across += [(other, at(1 - x, o, 1 - x, z)), (mine, other)]
+            far += [(mine, at(x, o, x, z - 2)), (other, spare), (spare, near), (near, other)]
+            direct += [(other, at(1 - x, o, 1 - x, z + 2 * x - 2)), (mine, other)]
             middle += [(near, mine), (mine, other), (other, spare), (spare, near)]
             last += [(near, at(x, n, x, z - 1)), (mine, other), (spare, near)]
             last += [(other, at(x, o, 1 - x, z ^ 1))]
             for side in range(2):
                 inside += [(at(x, side, core, z), at(x, side, 1 - core, z)) for core in range(2)]
-            for pairs in (across, far):
+            for pairs in (across, direct, relay):
                 pairs += [(near, spare), (spare, near)]
-        far += [(at(1, o, 0, z), at(0, o, 0, z)), (at(0, o, 0, z), at(0, o, 1, z))]
-        far += [(at(0, o, 1, z), at(1, o, 0, z - 2)), (at(1, o, 1, z), at(1, o, 1, z - 2))]
-    return first, across, far, middle, last, inside
+        relay += [(at(1, o, 1, z), at(1, o, 1, z - 2)), (at(1, o, 0, z), at(0, o, 0, z))]
+        relay += [(at(0, o, 0, z), at(0, o, 1, z)), (at(0, o, 1, z), at(1, o, 0, z))]
+    return first, across, far, direct, middle, relay, last, inside
 
 
 def routed(
@@ -244,18 +251,7 @@
     size = outside.shape[1]
     cells = pair_mask.shape[0]
     row_count = lax.axis_size("row")
-    row_id = lax.axis_index("row")
-    col_id = lax.axis_index("col")
-    first, across, far, middle, last, inside = routes(lax.axis_size("col"))
-    reach = (col_id - row_id) % row_count
-    reach = jnp.where(reach == 0, row_count, reach)
-    flags = [
-        col_id >= reach,
-        col_id % 2 == 1,
-        (col_id % 2) * (row_id % 2) == 1,
-        row_id == col_id % row_count,
-    ]
-    flags = jnp.stack(flags).astype(jnp.int32)
+    first, across, far, direct, middle, relay, last, inside = routes(lax.axis_size("col"))
     code = pltpu.VMEM((size, size), jnp.bfloat16)
     full = pltpu.VMEM((size, size), jnp.float32)
     output = pltpu.HBM((size, size), jnp.float32)
@@ -276,10 +272,10 @@
         )
 
     half = pltpu.VMEM((size // 2, size), jnp.bfloat16)
-    held, right, rest = call(
+    held, right, top, rest = call(
         right_kernel,
         [HBM] * 2,
-        (code, code, half),
+        (code, code, half, half),
         [code, pltpu.SemaphoreType.DMA((2,))],
     )(
         pltpu.with_memory_space_constraint(outside, pltpu.HBM),
@@ -287,16 +283,15 @@
     )
     q1 = send(right, first)
     qx = send(rest, across)
-    left, left_code = call(left_kernel, [SMEM] + [VMEM] * 2 + [ANY], (full, code))(
-        flags, inside_head, held, right
-    )
+    qh = send(right, far)
+    qa = send(top, direct)
+    left, left_code = call(
+        functools.partial(left_kernel, row_count), [VMEM] * 2 + [ANY], (full, code)
+    )(inside_head, held, right)
     i0 = send(left_code, inside)
     left, moved = call(chip_kernel, [VMEM] * 2, (full, code))(left, i0)
     q4 = send(moved, middle)
-    relayed = call(relay_kernel, [SMEM] + [VMEM] * 2 + [ANY], half)(
-        flags, right, qx, moved
-    )
-    q3 = send(relayed, far)
+    q3 = send(qx, relay)
     pair = call(add_kernel, [VMEM] * 2, code)(right, q1)
     q2 = send(pair, last)
     factor = call(
@@ -305,32 +300,29 @@
         full,
         [pltpu.SMEM((1,), jnp.int32), pltpu.SMEM((1,), jnp.float32), pltpu.SemaphoreType.DMA((2,))],
     )(pair_weight, seq_head, seq_tail, inside_pair, span_blocks, partition, pair)
-    i2 = send(q3, inside)
     partial, scale = call(
-        partial_kernel,
-        [SMEM] * 3 + [VMEM] * 8,
+        functools.partial(partial_kernel, row_count),
+        [SMEM] * 2 + [VMEM] * 7,
         (full, pltpu.VMEM((cells, size), jnp.float32)),
     )(
-        flags,
         pair_mask,
         split_weight,
         seq_head,
         seq_tail,
         left,
         q4,
-        q1,
+        qh,
         qx,
-        q3,
-        i2,
+        qa,
     )
     return pl.pallas_call(
         last_kernel,
-        in_specs=[VMEM] * 4,
+        in_specs=[VMEM] * 5,
         out_specs=(HBM, HBM),
         out_shape=(output, output),
         scratch_shapes=[full, full, pltpu.SemaphoreType.DMA((2, cells))],
         compiler_params=PARAMS,
-    )(scale, partial, factor, q2)
+    )(scale, partial, factor, q3, q2)
 
 
 def passed_along(x, axis, by):

time: 28.7 us -> 27.7 us (0.965)
  starting transfers between devices: 4.4 us -> 10.2 us
  waiting for transfers between devices: 11.5 us -> 6.62 us
  Pallas kernels: 9.75 us -> 8.61 us
  local copies, waits for them, and re-layouts: 0.65 us -> 0.03 us
    ppermute x7 -> x8, starting transfers between devices: 4.4 us -> 10.2 us  [send(): x = lax.ppermute(x, ('row', 'col'), pairs)]
    ppermute x7 -> x8, waiting for transfers between devices: 11.5 us -> 6.62 us  [send(): x = lax.ppermute(x, ('row', 'col'), pairs)]
    pallas_call x5 -> x4, Pallas kernels: 6.55 us -> 5.44 us  [the longest x1 1.83 us: routed(): call(right_kernel, [HBM] * 2, (code, code, half, half), [code, pltpu.Sema...]
    unnamed x14, local copies, waits for them, and re-layouts: 0.65 us -> 0.03 us
  transfers between devices with their start and end apart: 7 -> 8, of which waited for: 3 -> 4; matrix products, arithmetic and copies ran while one was open for 0% -> 0% of each run, Pallas kernels for 19% -> 17%
where the time goes in v4:
time: 27.7 us; the launch traced here: 27.6 us
  starting transfers between devices  10.2 us (37%)
  Pallas kernels  8.61 us (31%)
  waiting for transfers between devices  6.62 us (24%)
  between operations  2.07 us (7%)
    ppermute x8, starting transfers between devices, send(): x = lax.ppermute(x, ('row', 'col'), pairs)  10.2 us
    ppermute x8, waiting for transfers between devices, send(): x = lax.ppermute(x, ('row', 'col'), pairs)  6.62 us
    pallas_call x1, Pallas kernels, routed(): call(factor_kernel, [SMEM] + [VMEM] * 3 + [ANY] * 3, full, [pltpu.SMEM((1...  2.07 us
    pallas_call x1, Pallas kernels, routed(): call(right_kernel, [HBM] * 2, (code, code, half, half), [code, pltpu.Sema...  1.83 us
    pallas_call x1, Pallas kernels, routed(): call(functools.partial(partial_kernel, row_count), [SMEM] * 2 + [VMEM] *...  1.56 us
    pallas_call x1, Pallas kernels, routed(): pl.pallas_call(last_kernel, in_specs=[VMEM] * 5, out_specs=(HBM, HBM), ou...  1.45 us
    pallas_call x1, Pallas kernels, routed(): pair = call(add_kernel, [VMEM] * 2, code)(right, q1)  0.63 us
    pallas_call x1, Pallas kernels, routed(): call(functools.partial(left_kernel, row_count), [VMEM] * 2 + [ANY], (full...  0.59 us
  transfers between devices with their start and end apart: 8, of which 4 were waited for; matrix products, arithmetic and copies ran while one was open for 0% of the time, Pallas kernels for 17%

profile of v4, /device:TPU:0, one launch (start us, length us, event | category | flops | bytes accessed | tf_op | source)
XLA Modules:
  0.0 27.6 jit_solution(10860764183638652162)
XLA Ops:
  0.6 0.0 copy-start.1
  0.6 1.8 %shard_map.122 = (bf16[512,512]{1,0:T(8,128)(2,1)S(1)}, bf16[512,512]{1,0:T(8,128)(2,1)S(1)}, bf16[256,512]{1,0:T(8,128)(2,1)S(1)}, bf16[256,512]{1,0:T(8,128)(2,1)S(1)}) custom-call(bf16[512,512]{1,0:T(8,128)(2,1)} %out_hbm.1, bf16[512,512]{1,0:T(8,128)(2,1)} %tail_hbm.1), custom_call_target="tpu_custom_call" | custom-call | tf_op jit(solution)/shard_map/pallas_call | solution.py:275
  2.5 0.0 copy-done.1
  2.5 0.6 %shard_map.123 = (f32[512,512]{1,0:T(8,128)S(1)}, bf16[512,512]{1,0:T(8,128)(2,1)S(1)}) custom-call(bf16[512,512]{1,0:T(8,128)(2,1)S(1)} %copy-done.1, bf16[512,512]{1,0:T(8,128)(2,1)S(1)} %get-tuple-element.12.out_ref, bf16[512,512]{1,0:T(8,128)(2,1)S(1)} %get-tuple-element.13.after_ref.a_ref), custom_call_target="tpu_custom_call" | custom-call | tf_op jit(solution)/shard_map/pallas_call | solution.py:288
  3.1 0.6 %collective-permute-start = (bf16[512,512]{1,0:T(8,128)(2,1)S(1)}, bf16[512,512]{1,0:T(8,128)(2,1)S(1)}, u32[]{:S(2)}, u32[]{:S(2)}) collective-permute-start(bf16[512,512]{1,0:T(8,128)(2,1)S(1)} %get-tuple-element.15), channel_id=1, source_target_pairs={{0,8},{8,0},{16,24},{24,16},{1,9},{9,1},{17,25},{25,17},{2,10},{10... | collective-permute-start | bytes 1572872 | tf_op jit(solution)/shard_map/ppermute | solution.py:260
  3.6 0.1 collective-permute-start.5
  3.7 4.0 %collective-permute-start.2 = (bf16[512,512]{1,0:T(8,128)(2,1)S(1)}, bf16[512,512]{1,0:T(8,128)(2,1)S(1)}, u32[]{:S(2)}, u32[]{:S(2)}) collective-permute-start(bf16[512,512]{1,0:T(8,128)(2,1)S(1)} %get-tuple-element.13.after_ref.a_ref), channel_id=1, source_target_pairs={{0,4},{8,24},{24,16},{16,8},{9,13},{1,17},{17,25},{25,1},{18,22},{... | collective-permute-start | bytes 1572872 | tf_op jit(solution)/shard_map/ppermute | solution.py:260
  7.7 0.0 collective-permute-done.other_ref
  7.7 0.5 %shard_map.124 = (f32[512,512]{1,0:T(8,128)S(1)}, bf16[512,512]{1,0:T(8,128)(2,1)S(1)}) custom-call(f32[512,512]{1,0:T(8,128)S(1)} %get-tuple-element.14.left_ref, bf16[512,512]{1,0:T(8,128)(2,1)S(1)} %collective-permute-done.other_ref), custom_call_target="tpu_custom_call" | custom-call | tf_op jit(solution)/shard_map/pallas_call | solution.py:292
  8.2 0.0 copy-start
  8.2 0.1 collective-permute-start.1
  8.3 0.2 collective-permute-start.3
  8.5 0.0 collective-permute-done.5.b_ref
  8.5 0.6 %shard_map.126.after_ref = bf16[512,512]{1,0:T(8,128)(2,1)S(1)} custom-call(bf16[512,512]{1,0:T(8,128)(2,1)S(1)} %get-tuple-element.13.after_ref.a_ref, bf16[512,512]{1,0:T(8,128)(2,1)S(1)} %collective-permute-done.5.b_ref), custom_call_target="tpu_custom_call" | custom-call | tf_op jit(solution)/shard_map/pallas_call | solution.py:295
  9.1 0.9 %collective-permute-start.7 = (bf16[512,512]{1,0:T(8,128)(2,1)S(1)}, bf16[512,512]{1,0:T(8,128)(2,1)S(1)}, u32[]{:S(2)}, u32[]{:S(2)}) collective-permute-start(bf16[512,512]{1,0:T(8,128)(2,1)S(1)} %shard_map.126.after_ref), channel_id=1, source_target_pairs={{16,22},{0,8},{24,16},{8,10},{25,31},{9,1},{17,25},{1,3},{2,0},{18... | collective-permute-start | bytes 1572872 | tf_op jit(solution)/shard_map/ppermute | solution.py:260
  10.0 4.4 %collective-permute-start.4 = (bf16[256,512]{1,0:T(8,128)(2,1)S(1)}, bf16[256,512]{1,0:T(8,128)(2,1)S(1)}, u32[]{:S(2)}, u32[]{:S(2)}) collective-permute-start(bf16[256,512]{1,0:T(8,128)(2,1)S(1)} %get-tuple-element.19), channel_id=1, source_target_pairs={{8,13},{0,8},{16,24},{24,16},{1,0},{9,1},{25,17},{17,25},{26,31},{... | collective-permute-start | bytes 786440 | tf_op jit(solution)/shard_map/ppermute | solution.py:260
  14.5 0.2 collective-permute-done.3.across_ref
  14.7 0.0 collective-permute-start.6
  16.0 0.0 copy-done
  16.0 0.0 copy-done.5
  16.0 0.0 copy-done.3
  16.1 0.0 copy-start.4
  16.1 2.1 %shard_map.127.factor_ref = f32[512,512]{1,0:T(8,128)S(1)} custom-call(f32[4,4]{1,0:T(4,128)S(1)} %copy-done.5, s32[1,512]{1,0:T(1,128)S(1)} %copy-done.2, s32[1,512]{1,0:T(1,128)S(1)} %copy-done.3, f32[512,512]{1,0:T(8,128)S(1)} %copy-done, s32[1]{0:T(128)S(6)} %copy.13.span_hbm, f32[1]{0:T(128)S(6)} %copy.14.partition_hbm, ...), custom_call_target="tpu_custom_call" | custom-call | tf_op jit(solution)/shard_map/pallas_call | solution.py:297
  18.2 0.0 copy-start.6
  18.2 1.9 %collective-permute-done.4.direct_ref = bf16[256,512]{1,0:T(8,128)(2,1)S(1)} collective-permute-done((bf16[256,512]{1,0:T(8,128)(2,1)S(1)}, bf16[256,512]{1,0:T(8,128)(2,1)S(1)}, u32[]{:S(2)}, u32[]{:S(2)}) %collective-permute-start.4) | collective-permute-done | bytes 262176 | tf_op jit(solution)/shard_map/ppermute | solution.py:260
  20.1 0.0 collective-permute-done.2.far_ref
  20.1 0.0 collective-permute-done.1.middle_ref
  20.1 0.0 copy-done.4
  20.1 1.6 %shard_map.125 = (f32[512,512]{1,0:T(8,128)S(1)}, f32[4,512]{1,0:T(4,128)S(1)}) custom-call(s32[4,4]{1,0:T(4,128)S(1)} %copy-done.4, f32[4]{0:T(128)S(1)} %copy-done.6, s32[1,512]{1,0:T(1,128)S(1)} %copy-done.2, s32[1,512]{1,0:T(1,128)S(1)} %copy-done.3, f32[512,512]{1,0:T(8,128)S(1)} %get-tuple-element.16.left_ref, ...), custom_call_target="tpu_custom_call" | custom-call | tf_op jit(solution)/shard_map/pallas_call | solution.py:303
  21.6 1.2 %collective-permute-done.6.relay_ref = bf16[256,512]{1,0:T(8,128)(2,1)S(1)} collective-permute-done((bf16[256,512]{1,0:T(8,128)(2,1)S(1)}, bf16[256,512]{1,0:T(8,128)(2,1)S(1)}, u32[]{:S(2)}, u32[]{:S(2)}) %collective-permute-start.6) | collective-permute-done | bytes 262176 | tf_op jit(solution)/shard_map/ppermute | solution.py:260
  22.9 3.3 %collective-permute-done.7.last_ref = bf16[512,512]{1,0:T(8,128)(2,1)S(1)} collective-permute-done((bf16[512,512]{1,0:T(8,128)(2,1)S(1)}, bf16[512,512]{1,0:T(8,128)(2,1)S(1)}, u32[]{:S(2)}, u32[]{:S(2)}) %collective-permute-start.7) | collective-permute-done | bytes 524320 | tf_op jit(solution)/shard_map/ppermute | solution.py:260
  26.1 1.5 %shard_map.128 = (f32[512,512]{1,0:T(8,128)}, f32[512,512]{1,0:T(8,128)}) custom-call(f32[4,512]{1,0:T(4,128)S(1)} %get-tuple-element.20.scale_ref, f32[512,512]{1,0:T(8,128)S(1)} %get-tuple-element.21.partial_ref, f32[512,512]{1,0:T(8,128)S(1)} %shard_map.127.factor_ref, bf16[256,512]{1,0:T(8,128)(2,1)S(1)} %collective-permute-done.6.relay_ref, ...), custom_call_target="tpu_custom_call" | custom-call | tf_op jit(solution)/shard_map/pallas_call | solution.py:318
  (5 shorter events, 0.0 us)
Async XLA Ops:
  0.6 1.9 %copy-start.1 = (bf16[512,512]{1,0:T(8,128)(2,1)S(1)}, bf16[512,512]{1,0:T(8,128)(2,1)}, u32[]{:S(2)}) copy-start(bf16[512,512]{1,0:T(8,128)(2,1)} %head_ref.3) | copy-start | bytes 1572868
  3.1 4.6 %collective-permute-start = (bf16[512,512]{1,0:T(8,128)(2,1)S(1)}, bf16[512,512]{1,0:T(8,128)(2,1)S(1)}, u32[]{:S(2)}, u32[]{:S(2)}) collective-permute-start(bf16[512,512]{1,0:T(8,128)(2,1)S(1)} %get-tuple-element.15), channel_id=1, source_target_pairs={{0,8},{8,0},{16,24},{24,16},{1,9},{9,1},{17,25},{25,17},{2,10},{10... | collective-permute-start | bytes 1572872 | tf_op jit(solution)/shard_map/ppermute | solution.py:260
  3.6 4.8 %collective-permute-start.5 = (bf16[512,512]{1,0:T(8,128)(2,1)S(1)}, bf16[512,512]{1,0:T(8,128)(2,1)S(1)}, u32[]{:S(2)}, u32[]{:S(2)}) collective-permute-start(bf16[512,512]{1,0:T(8,128)(2,1)S(1)} %get-tuple-element.13.after_ref.a_ref), channel_id=1, source_target_pairs={{0,8},{8,0},{24,25},{16,24},{9,1},{1,9},{17,16},{25,17},{18,26},{2... | collective-permute-start | bytes 1572872 | tf_op jit(solution)/shard_map/ppermute | solution.py:260
  3.7 16.3 %collective-permute-start.2 = (bf16[512,512]{1,0:T(8,128)(2,1)S(1)}, bf16[512,512]{1,0:T(8,128)(2,1)S(1)}, u32[]{:S(2)}, u32[]{:S(2)}) collective-permute-start(bf16[512,512]{1,0:T(8,128)(2,1)S(1)} %get-tuple-element.13.after_ref.a_ref), channel_id=1, source_target_pairs={{0,4},{8,24},{24,16},{16,8},{9,13},{1,17},{17,25},{25,1},{18,22},{... | collective-permute-start | bytes 1572872 | tf_op jit(solution)/shard_map/ppermute | solution.py:260
  8.2 7.8 %copy-start = (f32[512,512]{1,0:T(8,128)S(1)}, f32[512,512]{1,0:T(8,128)}, u32[]{:S(2)}) copy-start(f32[512,512]{1,0:T(8,128)} %pair_ref.1) | copy-start | bytes 3145732
  8.2 11.8 %collective-permute-start.1 = (bf16[512,512]{1,0:T(8,128)(2,1)S(1)}, bf16[512,512]{1,0:T(8,128)(2,1)S(1)}, u32[]{:S(2)}, u32[]{:S(2)}) collective-permute-start(bf16[512,512]{1,0:T(8,128)(2,1)S(1)} %get-tuple-element.17), channel_id=1, source_target_pairs={{16,0},{0,8},{8,24},{24,16},{25,9},{9,1},{1,17},{17,25},{2,18},{18... | collective-permute-start | bytes 1572872 | tf_op jit(solution)/shard_map/ppermute | solution.py:260
  8.3 6.4 %collective-permute-start.3 = (bf16[256,512]{1,0:T(8,128)(2,1)S(1)}, bf16[256,512]{1,0:T(8,128)(2,1)S(1)}, u32[]{:S(2)}, u32[]{:S(2)}) collective-permute-start(bf16[256,512]{1,0:T(8,128)(2,1)S(1)} %get-tuple-element.18), channel_id=1, source_target_pairs={{8,9},{0,8},{16,24},{24,16},{1,0},{9,1},{25,17},{17,25},{26,27},{1... | collective-permute-start | bytes 786440 | tf_op jit(solution)/shard_map/ppermute | solution.py:260
  8.5 7.6 %copy-start.5 = (f32[4,4]{1,0:T(4,128)S(1)}, f32[4,4]{1,0:T(4,128)}, u32[]{:S(2)}) copy-start(f32[4,4]{1,0:T(4,128)} %weight_ref.1) | copy-start | bytes 196
  9.1 17.0 %collective-permute-start.7 = (bf16[512,512]{1,0:T(8,128)(2,1)S(1)}, bf16[512,512]{1,0:T(8,128)(2,1)S(1)}, u32[]{:S(2)}, u32[]{:S(2)}) collective-permute-start(bf16[512,512]{1,0:T(8,128)(2,1)S(1)} %shard_map.126.after_ref), channel_id=1, source_target_pairs={{16,22},{0,8},{24,16},{8,10},{25,31},{9,1},{17,25},{1,3},{2,0},{18... | collective-permute-start | bytes 1572872 | tf_op jit(solution)/shard_map/ppermute | solution.py:260
  10.0 6.0 %copy-start.3 = (s32[1,512]{1,0:T(1,128)S(1)}, s32[1,512]{1,0:T(1,128)}, u32[]{:S(2)}) copy-start(s32[1,512]{1,0:T(1,128)} %tail_ref.3) | copy-start | bytes 6148
  10.0 6.0 %copy-start.2 = (s32[1,512]{1,0:T(1,128)S(1)}, s32[1,512]{1,0:T(1,128)}, u32[]{:S(2)}) copy-start(s32[1,512]{1,0:T(1,128)} %head_ref.5) | copy-start | bytes 6148
  10.0 10.0 %collective-permute-start.4 = (bf16[256,512]{1,0:T(8,128)(2,1)S(1)}, bf16[256,512]{1,0:T(8,128)(2,1)S(1)}, u32[]{:S(2)}, u32[]{:S(2)}) collective-permute-start(bf16[256,512]{1,0:T(8,128)(2,1)S(1)} %get-tuple-element.19), channel_id=1, source_target_pairs={{8,13},{0,8},{16,24},{24,16},{1,0},{9,1},{25,17},{17,25},{26,31},{... | collective-permute-start | bytes 786440 | tf_op jit(solution)/shard_map/ppermute | solution.py:260
  14.7 8.1 %collective-permute-start.6 = (bf16[256,512]{1,0:T(8,128)(2,1)S(1)}, bf16[256,512]{1,0:T(8,128)(2,1)S(1)}, u32[]{:S(2)}, u32[]{:S(2)}) collective-permute-start(bf16[256,512]{1,0:T(8,128)(2,1)S(1)} %collective-permute-done.3.across_ref), channel_id=1, source_target_pairs={{16,24},{24,16},{25,17},{17,25},{9,13},{1,0},{0,8},{8,1},{2,10},{1... | collective-permute-start | bytes 786440 | tf_op jit(solution)/shard_map/ppermute | solution.py:260
  16.1 4.0 %copy-start.4 = (s32[4,4]{1,0:T(4,128)S(1)}, s32[4,4]{1,0:T(4,128)}, u32[]{:S(2)}) copy-start(s32[4,4]{1,0:T(4,128)} %mask_ref.1) | copy-start | bytes 196
  18.2 1.9 %copy-start.6 = (f32[4]{0:T(128)S(1)}, f32[4]{0:T(128)}, u32[]{:S(2)}) copy-start(f32[4]{0:T(128)} %split_ref.1) | copy-start | bytes 52

commit v5 on v4

--- a/solution.py
+++ b/solution.py
@@ -17,15 +17,24 @@
 PARAMS = pltpu.CompilerParams(vmem_limit_bytes=16 << 20)
 
 
+SPLIT = 0.25
+GAIN = 2.0**6.2
+
+
 def encode(x):
-    y = x * 4.0
+    high = x >= SPLIT
+    y = x * jnp.where(high, 4.0 / GAIN, 4.0 * GAIN)
     y2 = y * y
-    y4 = y2 * y2
-    return (y4 * y4 * y2).astype(jnp.bfloat16)
+    y5 = y2 * y2 * y
+    y10 = y5 * y5
+    y20 = y10 * y10
+    return jnp.where(high, y20, -y20).astype(jnp.bfloat16)
 
 
 def decode(code):
-    return jnp.exp2(jnp.log2(code.astype(jnp.float32)) * 0.1) * 0.25
+    y = code.astype(jnp.float32)
+    root = jnp.exp2(jnp.log2(jnp.abs(y)) * 0.05)
+    return root * jnp.where(y > 0.0, 0.25 * GAIN, 0.25 / GAIN)
 
 
 def place():

time: 27.7 us -> 28.4 us (1.025)
  Pallas kernels: 8.61 us -> 9.73 us
    pallas_call x1, Pallas kernels: 0.63 us -> 0.94 us  [routed(): pair = call(add_kernel, [VMEM] * 2, code)(right, q1)]
  transfers between devices with their start and end apart: 8 -> 8, of which waited for: 4 -> 4; matrix products, arithmetic and copies ran while one was open for 0% -> 0% of each run, Pallas kernels for 17% -> 19%
where the time goes in v5:
time: 28.4 us; the launch traced here: 28.3 us
  starting transfers between devices  10.1 us (36%)
  Pallas kernels  9.73 us (34%)
  waiting for transfers between devices  6.37 us (22%)
  between operations  2.06 us (7%)
    ppermute x8, starting transfers between devices, send(): x = lax.ppermute(x, ('row', 'col'), pairs)  10.1 us
    ppermute x8, waiting for transfers between devices, send(): x = lax.ppermute(x, ('row', 'col'), pairs)  6.37 us
    pallas_call x1, Pallas kernels, routed(): call(factor_kernel, [SMEM] + [VMEM] * 3 + [ANY] * 3, full, [pltpu.SMEM((1...  2.07 us
    pallas_call x1, Pallas kernels, routed(): call(right_kernel, [HBM] * 2, (code, code, half, half), [code, pltpu.Sema...  2 us
    pallas_call x1, Pallas kernels, routed(): call(functools.partial(partial_kernel, row_count), [SMEM] * 2 + [VMEM] *...  1.81 us
    pallas_call x1, Pallas kernels, routed(): pl.pallas_call(last_kernel, in_specs=[VMEM] * 5, out_specs=(HBM, HBM), ou...  1.49 us
    pallas_call x1, Pallas kernels, routed(): pair = call(add_kernel, [VMEM] * 2, code)(right, q1)  0.94 us
    pallas_call x1, Pallas kernels, routed(): call(functools.partial(left_kernel, row_count), [VMEM] * 2 + [ANY], (full...  0.76 us
  transfers between devices with their start and end apart: 8, of which 4 were waited for; matrix products, arithmetic and copies ran while one was open for 0% of the time, Pallas kernels for 19%

profile of v5, /device:TPU:0, one launch (start us, length us, event | category | flops | bytes accessed | tf_op | source)
XLA Modules:
  0.0 28.3 jit_solution(16923526769719049337)
XLA Ops:
  0.6 0.0 copy-start.1
  0.6 2.0 %shard_map.122 = (bf16[512,512]{1,0:T(8,128)(2,1)S(1)}, bf16[512,512]{1,0:T(8,128)(2,1)S(1)}, bf16[256,512]{1,0:T(8,128)(2,1)S(1)}, bf16[256,512]{1,0:T(8,128)(2,1)S(1)}) custom-call(bf16[512,512]{1,0:T(8,128)(2,1)} %out_hbm.1, bf16[512,512]{1,0:T(8,128)(2,1)} %tail_hbm.1), custom_call_target="tpu_custom_call" | custom-call | tf_op jit(solution)/shard_map/pallas_call | solution.py:284
  2.7 0.0 copy-done.1
  2.7 0.8 %shard_map.123 = (f32[512,512]{1,0:T(8,128)S(1)}, bf16[512,512]{1,0:T(8,128)(2,1)S(1)}) custom-call(bf16[512,512]{1,0:T(8,128)(2,1)S(1)} %copy-done.1, bf16[512,512]{1,0:T(8,128)(2,1)S(1)} %get-tuple-element.12.out_ref, bf16[512,512]{1,0:T(8,128)(2,1)S(1)} %get-tuple-element.13.after_ref.a_ref), custom_call_target="tpu_custom_call" | custom-call | tf_op jit(solution)/shard_map/pallas_call | solution.py:297
  3.4 0.6 %collective-permute-start = (bf16[512,512]{1,0:T(8,128)(2,1)S(1)}, bf16[512,512]{1,0:T(8,128)(2,1)S(1)}, u32[]{:S(2)}, u32[]{:S(2)}) collective-permute-start(bf16[512,512]{1,0:T(8,128)(2,1)S(1)} %get-tuple-element.15), channel_id=1, source_target_pairs={{0,8},{8,0},{16,24},{24,16},{1,9},{9,1},{17,25},{25,17},{2,10},{10... | collective-permute-start | bytes 1572872 | tf_op jit(solution)/shard_map/ppermute | solution.py:269
  4.0 0.1 collective-permute-start.5
  4.1 4.0 %collective-permute-start.2 = (bf16[512,512]{1,0:T(8,128)(2,1)S(1)}, bf16[512,512]{1,0:T(8,128)(2,1)S(1)}, u32[]{:S(2)}, u32[]{:S(2)}) collective-permute-start(bf16[512,512]{1,0:T(8,128)(2,1)S(1)} %get-tuple-element.13.after_ref.a_ref), channel_id=1, source_target_pairs={{0,4},{8,24},{24,16},{16,8},{9,13},{1,17},{17,25},{25,1},{18,22},{... | collective-permute-start | bytes 1572872 | tf_op jit(solution)/shard_map/ppermute | solution.py:269
  8.1 0.0 collective-permute-done.other_ref
  8.1 0.7 %shard_map.124 = (f32[512,512]{1,0:T(8,128)S(1)}, bf16[512,512]{1,0:T(8,128)(2,1)S(1)}) custom-call(f32[512,512]{1,0:T(8,128)S(1)} %get-tuple-element.14.left_ref, bf16[512,512]{1,0:T(8,128)(2,1)S(1)} %collective-permute-done.other_ref), custom_call_target="tpu_custom_call" | custom-call | tf_op jit(solution)/shard_map/pallas_call | solution.py:301
  8.7 0.0 copy-start
  8.7 0.1 collective-permute-start.1
  8.8 0.2 collective-permute-start.3
  9.0 0.0 collective-permute-done.5.b_ref
  9.0 0.9 %shard_map.126.after_ref = bf16[512,512]{1,0:T(8,128)(2,1)S(1)} custom-call(bf16[512,512]{1,0:T(8,128)(2,1)S(1)} %get-tuple-element.13.after_ref.a_ref, bf16[512,512]{1,0:T(8,128)(2,1)S(1)} %collective-permute-done.5.b_ref), custom_call_target="tpu_custom_call" | custom-call | tf_op jit(solution)/shard_map/pallas_call | solution.py:304
  9.9 0.9 %collective-permute-start.7 = (bf16[512,512]{1,0:T(8,128)(2,1)S(1)}, bf16[512,512]{1,0:T(8,128)(2,1)S(1)}, u32[]{:S(2)}, u32[]{:S(2)}) collective-permute-start(bf16[512,512]{1,0:T(8,128)(2,1)S(1)} %shard_map.126.after_ref), channel_id=1, source_target_pairs={{16,22},{0,8},{24,16},{8,10},{25,31},{9,1},{17,25},{1,3},{2,0},{18... | collective-permute-start | bytes 1572872 | tf_op jit(solution)/shard_map/ppermute | solution.py:269
  10.9 4.2 %collective-permute-start.4 = (bf16[256,512]{1,0:T(8,128)(2,1)S(1)}, bf16[256,512]{1,0:T(8,128)(2,1)S(1)}, u32[]{:S(2)}, u32[]{:S(2)}) collective-permute-start(bf16[256,512]{1,0:T(8,128)(2,1)S(1)} %get-tuple-element.19), channel_id=1, source_target_pairs={{8,13},{0,8},{16,24},{24,16},{1,0},{9,1},{25,17},{17,25},{26,31},{... | collective-permute-start | bytes 786440 | tf_op jit(solution)/shard_map/ppermute | solution.py:269
  15.1 0.1 collective-permute-done.3.across_ref
  15.2 0.0 collective-permute-start.6
  16.6 0.0 copy-done
  16.6 0.0 copy-done.5
  16.6 0.0 copy-done.3
  16.6 0.0 copy-start.4
  16.6 2.1 %shard_map.127.factor_ref = f32[512,512]{1,0:T(8,128)S(1)} custom-call(f32[4,4]{1,0:T(4,128)S(1)} %copy-done.5, s32[1,512]{1,0:T(1,128)S(1)} %copy-done.2, s32[1,512]{1,0:T(1,128)S(1)} %copy-done.3, f32[512,512]{1,0:T(8,128)S(1)} %copy-done, s32[1]{0:T(128)S(6)} %copy.13.span_hbm, f32[1]{0:T(128)S(6)} %copy.14.partition_hbm, ...), custom_call_target="tpu_custom_call" | custom-call | tf_op jit(solution)/shard_map/pallas_call | solution.py:306
  18.7 0.0 copy-start.6
  18.7 2.0 %collective-permute-done.4.direct_ref = bf16[256,512]{1,0:T(8,128)(2,1)S(1)} collective-permute-done((bf16[256,512]{1,0:T(8,128)(2,1)S(1)}, bf16[256,512]{1,0:T(8,128)(2,1)S(1)}, u32[]{:S(2)}, u32[]{:S(2)}) %collective-permute-start.4) | collective-permute-done | bytes 262176 | tf_op jit(solution)/shard_map/ppermute | solution.py:269
  20.7 0.0 collective-permute-done.2.far_ref
  20.7 0.0 collective-permute-done.1.middle_ref
  20.7 0.0 copy-done.6
  20.7 1.8 %shard_map.125 = (f32[512,512]{1,0:T(8,128)S(1)}, f32[4,512]{1,0:T(4,128)S(1)}) custom-call(s32[4,4]{1,0:T(4,128)S(1)} %copy-done.4, f32[4]{0:T(128)S(1)} %copy-done.6, s32[1,512]{1,0:T(1,128)S(1)} %copy-done.2, s32[1,512]{1,0:T(1,128)S(1)} %copy-done.3, f32[512,512]{1,0:T(8,128)S(1)} %get-tuple-element.16.left_ref, ...), custom_call_target="tpu_custom_call" | custom-call | tf_op jit(solution)/shard_map/pallas_call | solution.py:312
  22.5 1.0 %collective-permute-done.6.relay_ref = bf16[256,512]{1,0:T(8,128)(2,1)S(1)} collective-permute-done((bf16[256,512]{1,0:T(8,128)(2,1)S(1)}, bf16[256,512]{1,0:T(8,128)(2,1)S(1)}, u32[]{:S(2)}, u32[]{:S(2)}) %collective-permute-start.6) | collective-permute-done | bytes 262176 | tf_op jit(solution)/shard_map/ppermute | solution.py:269
  23.5 3.3 %collective-permute-done.7.last_ref = bf16[512,512]{1,0:T(8,128)(2,1)S(1)} collective-permute-done((bf16[512,512]{1,0:T(8,128)(2,1)S(1)}, bf16[512,512]{1,0:T(8,128)(2,1)S(1)}, u32[]{:S(2)}, u32[]{:S(2)}) %collective-permute-start.7) | collective-permute-done | bytes 524320 | tf_op jit(solution)/shard_map/ppermute | solution.py:269
  26.8 1.5 %shard_map.128 = (f32[512,512]{1,0:T(8,128)}, f32[512,512]{1,0:T(8,128)}) custom-call(f32[4,512]{1,0:T(4,128)S(1)} %get-tuple-element.20.scale_ref, f32[512,512]{1,0:T(8,128)S(1)} %get-tuple-element.21.partial_ref, f32[512,512]{1,0:T(8,128)S(1)} %shard_map.127.factor_ref, bf16[256,512]{1,0:T(8,128)(2,1)S(1)} %collective-permute-done.6.relay_ref, ...), custom_call_target="tpu_custom_call" | custom-call | tf_op jit(solution)/shard_map/pallas_call | solution.py:327
  (5 shorter events, 0.0 us)
Async XLA Ops:
  0.6 2.0 %copy-start.1 = (bf16[512,512]{1,0:T(8,128)(2,1)S(1)}, bf16[512,512]{1,0:T(8,128)(2,1)}, u32[]{:S(2)}) copy-start(bf16[512,512]{1,0:T(8,128)(2,1)} %head_ref.3) | copy-start | bytes 1572868
  3.4 4.6 %collective-permute-start = (bf16[512,512]{1,0:T(8,128)(2,1)S(1)}, bf16[512,512]{1,0:T(8,128)(2,1)S(1)}, u32[]{:S(2)}, u32[]{:S(2)}) collective-permute-start(bf16[512,512]{1,0:T(8,128)(2,1)S(1)} %get-tuple-element.15), channel_id=1, source_target_pairs={{0,8},{8,0},{16,24},{24,16},{1,9},{9,1},{17,25},{25,17},{2,10},{10... | collective-permute-start | bytes 1572872 | tf_op jit(solution)/shard_map/ppermute | solution.py:269
  4.0 5.0 %collective-permute-start.5 = (bf16[512,512]{1,0:T(8,128)(2,1)S(1)}, bf16[512,512]{1,0:T(8,128)(2,1)S(1)}, u32[]{:S(2)}, u32[]{:S(2)}) collective-permute-start(bf16[512,512]{1,0:T(8,128)(2,1)S(1)} %get-tuple-element.13.after_ref.a_ref), channel_id=1, source_target_pairs={{0,8},{8,0},{24,25},{16,24},{9,1},{1,9},{17,16},{25,17},{18,26},{2... | collective-permute-start | bytes 1572872 | tf_op jit(solution)/shard_map/ppermute | solution.py:269
  4.1 16.6 %collective-permute-start.2 = (bf16[512,512]{1,0:T(8,128)(2,1)S(1)}, bf16[512,512]{1,0:T(8,128)(2,1)S(1)}, u32[]{:S(2)}, u32[]{:S(2)}) collective-permute-start(bf16[512,512]{1,0:T(8,128)(2,1)S(1)} %get-tuple-element.13.after_ref.a_ref), channel_id=1, source_target_pairs={{0,4},{8,24},{24,16},{16,8},{9,13},{1,17},{17,25},{25,1},{18,22},{... | collective-permute-start | bytes 1572872 | tf_op jit(solution)/shard_map/ppermute | solution.py:269
  8.7 7.8 %copy-start = (f32[512,512]{1,0:T(8,128)S(1)}, f32[512,512]{1,0:T(8,128)}, u32[]{:S(2)}) copy-start(f32[512,512]{1,0:T(8,128)} %pair_ref.1) | copy-start | bytes 3145732
  8.7 12.0 %collective-permute-start.1 = (bf16[512,512]{1,0:T(8,128)(2,1)S(1)}, bf16[512,512]{1,0:T(8,128)(2,1)S(1)}, u32[]{:S(2)}, u32[]{:S(2)}) collective-permute-start(bf16[512,512]{1,0:T(8,128)(2,1)S(1)} %get-tuple-element.17), channel_id=1, source_target_pairs={{16,0},{0,8},{8,24},{24,16},{25,9},{9,1},{1,17},{17,25},{2,18},{18... | collective-permute-start | bytes 1572872 | tf_op jit(solution)/shard_map/ppermute | solution.py:269
  8.8 6.4 %collective-permute-start.3 = (bf16[256,512]{1,0:T(8,128)(2,1)S(1)}, bf16[256,512]{1,0:T(8,128)(2,1)S(1)}, u32[]{:S(2)}, u32[]{:S(2)}) collective-permute-start(bf16[256,512]{1,0:T(8,128)(2,1)S(1)} %get-tuple-element.18), channel_id=1, source_target_pairs={{8,9},{0,8},{16,24},{24,16},{1,0},{9,1},{25,17},{17,25},{26,27},{1... | collective-permute-start | bytes 786440 | tf_op jit(solution)/shard_map/ppermute | solution.py:269
  9.0 7.6 %copy-start.5 = (f32[4,4]{1,0:T(4,128)S(1)}, f32[4,4]{1,0:T(4,128)}, u32[]{:S(2)}) copy-start(f32[4,4]{1,0:T(4,128)} %weight_ref.1) | copy-start | bytes 196
  9.9 16.8 %collective-permute-start.7 = (bf16[512,512]{1,0:T(8,128)(2,1)S(1)}, bf16[512,512]{1,0:T(8,128)(2,1)S(1)}, u32[]{:S(2)}, u32[]{:S(2)}) collective-permute-start(bf16[512,512]{1,0:T(8,128)(2,1)S(1)} %shard_map.126.after_ref), channel_id=1, source_target_pairs={{16,22},{0,8},{24,16},{8,10},{25,31},{9,1},{17,25},{1,3},{2,0},{18... | collective-permute-start | bytes 1572872 | tf_op jit(solution)/shard_map/ppermute | solution.py:269
  10.9 5.7 %copy-start.3 = (s32[1,512]{1,0:T(1,128)S(1)}, s32[1,512]{1,0:T(1,128)}, u32[]{:S(2)}) copy-start(s32[1,512]{1,0:T(1,128)} %tail_ref.3) | copy-start | bytes 6148
  10.9 5.7 %copy-start.2 = (s32[1,512]{1,0:T(1,128)S(1)}, s32[1,512]{1,0:T(1,128)}, u32[]{:S(2)}) copy-start(s32[1,512]{1,0:T(1,128)} %head_ref.5) | copy-start | bytes 6148
  10.9 9.8 %collective-permute-start.4 = (bf16[256,512]{1,0:T(8,128)(2,1)S(1)}, bf16[256,512]{1,0:T(8,128)(2,1)S(1)}, u32[]{:S(2)}, u32[]{:S(2)}) collective-permute-start(bf16[256,512]{1,0:T(8,128)(2,1)S(1)} %get-tuple-element.19), channel_id=1, source_target_pairs={{8,13},{0,8},{16,24},{24,16},{1,0},{9,1},{25,17},{17,25},{26,31},{... | collective-permute-start | bytes 786440 | tf_op jit(solution)/shard_map/ppermute | solution.py:269
  15.2 8.3 %collective-permute-start.6 = (bf16[256,512]{1,0:T(8,128)(2,1)S(1)}, bf16[256,512]{1,0:T(8,128)(2,1)S(1)}, u32[]{:S(2)}, u32[]{:S(2)}) collective-permute-start(bf16[256,512]{1,0:T(8,128)(2,1)S(1)} %collective-permute-done.3.across_ref), channel_id=1, source_target_pairs={{16,24},{24,16},{25,17},{17,25},{9,13},{1,0},{0,8},{8,1},{2,10},{1... | collective-permute-start | bytes 786440 | tf_op jit(solution)/shard_map/ppermute | solution.py:269
  16.6 4.1 %copy-start.4 = (s32[4,4]{1,0:T(4,128)S(1)}, s32[4,4]{1,0:T(4,128)}, u32[]{:S(2)}) copy-start(s32[4,4]{1,0:T(4,128)} %mask_ref.1) | copy-start | bytes 196
  18.7 2.0 %copy-start.6 = (f32[4]{0:T(128)S(1)}, f32[4]{0:T(128)}, u32[]{:S(2)}) copy-start(f32[4]{0:T(128)} %split_ref.1) | copy-start | bytes 52

commit v6 on v5

--- a/solution.py
+++ b/solution.py
@@ -18,22 +18,20 @@
 
 
 SPLIT = 0.25
-GAIN = 2.0**6.2
-
-
-def encode(x):
-    high = x >= SPLIT
-    y = x * jnp.where(high, 4.0 / GAIN, 4.0 * GAIN)
+GAIN = 2.0**5.9
+
+
+def encode(x, scale=1.0):
+    y = x * jnp.where(x >= SPLIT / scale, scale * 4.0 / GAIN, scale * -4.0 * GAIN)
     y2 = y * y
     y5 = y2 * y2 * y
     y10 = y5 * y5
-    y20 = y10 * y10
-    return jnp.where(high, y20, -y20).astype(jnp.bfloat16)
+    return (y10 * y10 * y).astype(jnp.bfloat16)
 
 
 def decode(code):
     y = code.astype(jnp.float32)
-    root = jnp.exp2(jnp.log2(jnp.abs(y)) * 0.05)
+    root = jnp.exp2(jnp.log2(jnp.abs(y)) * (1.0 / 21.0))
     return root * jnp.where(y > 0.0, 0.25 * GAIN, 0.25 / GAIN)
 
 
@@ -58,10 +56,11 @@
     term = lax.dot_general(
         out_ref[...], tail_ref[...], (((1,), (1,)), ((), ())), preferred_element_type=jnp.float32
     )
-    code_ref[...] = encode(term * (1.0 / term.shape[0]))
-    half = rest_ref.shape[0]
-    top_ref[...] = code_ref[pl.ds(0, half), :]
-    rest_ref[...] = code_ref[pl.ds(half, half), :]
+    half = top_ref.shape[0]
+    for part, part_ref in ((pl.ds(0, half), top_ref), (pl.ds(half, half), rest_ref)):
+        code = encode(term[part.start : part.start + half], 1.0 / term.shape[0])
+        code_ref[part, :] = code
+        part_ref[...] = code
 
 
 def left_kernel(rows, head_ref, out_ref, after_ref, left_ref, code_ref):

time: 28.4 us -> 28.3 us (level)
  no operation moved by 1% of the time
where the time goes in v6:
time: 28.3 us; the launch traced here: 28.1 us
  starting transfers between devices  10.1 us (36%)
  Pallas kernels  9.59 us (34%)
  waiting for transfers between devices  6.37 us (23%)
  between operations  2.07 us (7%)
    ppermute x8, starting transfers between devices, send(): x = lax.ppermute(x, ('row', 'col'), pairs)  10.1 us
    ppermute x8, waiting for transfers between devices, send(): x = lax.ppermute(x, ('row', 'col'), pairs)  6.37 us
    pallas_call x1, Pallas kernels, routed(): call(factor_kernel, [SMEM] + [VMEM] * 3 + [ANY] * 3, full, [pltpu.SMEM((1...  2.07 us
    pallas_call x1, Pallas kernels, routed(): call(right_kernel, [HBM] * 2, (code, code, half, half), [code, pltpu.Sema...  1.94 us
    pallas_call x1, Pallas kernels, routed(): call(functools.partial(partial_kernel, row_count), [SMEM] * 2 + [VMEM] *...  1.81 us
    pallas_call x1, Pallas kernels, routed(): pl.pallas_call(last_kernel, in_specs=[VMEM] * 5, out_specs=(HBM, HBM), ou...  1.49 us
    pallas_call x1, Pallas kernels, routed(): pair = call(add_kernel, [VMEM] * 2, code)(right, q1)  0.91 us
    pallas_call x1, Pallas kernels, routed(): call(functools.partial(left_kernel, row_count), [VMEM] * 2 + [ANY], (full...  0.73 us
  transfers between devices with their start and end apart: 8, of which 4 were waited for; matrix products, arithmetic and copies ran while one was open for 0% of the time, Pallas kernels for 19%

profile of v6, /device:TPU:0, one launch (start us, length us, event | category | flops | bytes accessed | tf_op | source)
XLA Modules:
  0.0 28.1 jit_solution(3746580523021873166)
XLA Ops:
  0.6 0.0 copy-start.1
  0.6 1.9 %shard_map.122 = (bf16[512,512]{1,0:T(8,128)(2,1)S(1)}, bf16[512,512]{1,0:T(8,128)(2,1)S(1)}, bf16[256,512]{1,0:T(8,128)(2,1)S(1)}, bf16[256,512]{1,0:T(8,128)(2,1)S(1)}) custom-call(bf16[512,512]{1,0:T(8,128)(2,1)} %out_hbm.1, bf16[512,512]{1,0:T(8,128)(2,1)} %tail_hbm.1), custom_call_target="tpu_custom_call" | custom-call | tf_op jit(solution)/shard_map/pallas_call | solution.py:283
  2.6 0.0 copy-done.1
  2.6 0.7 %shard_map.123 = (f32[512,512]{1,0:T(8,128)S(1)}, bf16[512,512]{1,0:T(8,128)(2,1)S(1)}) custom-call(bf16[512,512]{1,0:T(8,128)(2,1)S(1)} %copy-done.1, bf16[512,512]{1,0:T(8,128)(2,1)S(1)} %get-tuple-element.12.out_ref, bf16[512,512]{1,0:T(8,128)(2,1)S(1)} %get-tuple-element.13.after_ref.a_ref), custom_call_target="tpu_custom_call" | custom-call | tf_op jit(solution)/shard_map/pallas_call | solution.py:296
  3.3 0.6 %collective-permute-start = (bf16[512,512]{1,0:T(8,128)(2,1)S(1)}, bf16[512,512]{1,0:T(8,128)(2,1)S(1)}, u32[]{:S(2)}, u32[]{:S(2)}) collective-permute-start(bf16[512,512]{1,0:T(8,128)(2,1)S(1)} %get-tuple-element.15), channel_id=1, source_target_pairs={{0,8},{8,0},{16,24},{24,16},{1,9},{9,1},{17,25},{25,17},{2,10},{10... | collective-permute-start | bytes 1572872 | tf_op jit(solution)/shard_map/ppermute | solution.py:268
  3.9 0.1 collective-permute-start.5
  4.0 4.0 %collective-permute-start.2 = (bf16[512,512]{1,0:T(8,128)(2,1)S(1)}, bf16[512,512]{1,0:T(8,128)(2,1)S(1)}, u32[]{:S(2)}, u32[]{:S(2)}) collective-permute-start(bf16[512,512]{1,0:T(8,128)(2,1)S(1)} %get-tuple-element.13.after_ref.a_ref), channel_id=1, source_target_pairs={{0,4},{8,24},{24,16},{16,8},{9,13},{1,17},{17,25},{25,1},{18,22},{... | collective-permute-start | bytes 1572872 | tf_op jit(solution)/shard_map/ppermute | solution.py:268
  8.0 0.0 collective-permute-done.other_ref
  8.0 0.7 %shard_map.124 = (f32[512,512]{1,0:T(8,128)S(1)}, bf16[512,512]{1,0:T(8,128)(2,1)S(1)}) custom-call(f32[512,512]{1,0:T(8,128)S(1)} %get-tuple-element.14.left_ref, bf16[512,512]{1,0:T(8,128)(2,1)S(1)} %collective-permute-done.other_ref), custom_call_target="tpu_custom_call" | custom-call | tf_op jit(solution)/shard_map/pallas_call | solution.py:300
  8.6 0.0 copy-start
  8.6 0.1 collective-permute-start.1
  8.7 0.2 collective-permute-start.3
  8.9 0.0 collective-permute-done.5.b_ref
  8.9 0.9 %shard_map.126.after_ref = bf16[512,512]{1,0:T(8,128)(2,1)S(1)} custom-call(bf16[512,512]{1,0:T(8,128)(2,1)S(1)} %get-tuple-element.13.after_ref.a_ref, bf16[512,512]{1,0:T(8,128)(2,1)S(1)} %collective-permute-done.5.b_ref), custom_call_target="tpu_custom_call" | custom-call | tf_op jit(solution)/shard_map/pallas_call | solution.py:303
  9.8 0.9 %collective-permute-start.7 = (bf16[512,512]{1,0:T(8,128)(2,1)S(1)}, bf16[512,512]{1,0:T(8,128)(2,1)S(1)}, u32[]{:S(2)}, u32[]{:S(2)}) collective-permute-start(bf16[512,512]{1,0:T(8,128)(2,1)S(1)} %shard_map.126.after_ref), channel_id=1, source_target_pairs={{16,22},{0,8},{24,16},{8,10},{25,31},{9,1},{17,25},{1,3},{2,0},{18... | collective-permute-start | bytes 1572872 | tf_op jit(solution)/shard_map/ppermute | solution.py:268
  10.8 4.2 %collective-permute-start.4 = (bf16[256,512]{1,0:T(8,128)(2,1)S(1)}, bf16[256,512]{1,0:T(8,128)(2,1)S(1)}, u32[]{:S(2)}, u32[]{:S(2)}) collective-permute-start(bf16[256,512]{1,0:T(8,128)(2,1)S(1)} %get-tuple-element.19), channel_id=1, source_target_pairs={{8,13},{0,8},{16,24},{24,16},{1,0},{9,1},{25,17},{17,25},{26,31},{... | collective-permute-start | bytes 786440 | tf_op jit(solution)/shard_map/ppermute | solution.py:268
  15.0 0.2 collective-permute-done.3.across_ref
  15.1 0.0 collective-permute-start.6
  16.4 0.0 copy-done
  16.5 0.0 copy-done.5
  16.5 0.0 copy-done.3
  16.5 0.0 copy-start.4
  16.5 2.1 %shard_map.127.factor_ref = f32[512,512]{1,0:T(8,128)S(1)} custom-call(f32[4,4]{1,0:T(4,128)S(1)} %copy-done.5, s32[1,512]{1,0:T(1,128)S(1)} %copy-done.2, s32[1,512]{1,0:T(1,128)S(1)} %copy-done.3, f32[512,512]{1,0:T(8,128)S(1)} %copy-done, s32[1]{0:T(128)S(6)} %copy.13.span_hbm, f32[1]{0:T(128)S(6)} %copy.14.partition_hbm, ...), custom_call_target="tpu_custom_call" | custom-call | tf_op jit(solution)/shard_map/pallas_call | solution.py:305
  18.6 0.0 copy-start.6
  18.6 2.0 %collective-permute-done.4.direct_ref = bf16[256,512]{1,0:T(8,128)(2,1)S(1)} collective-permute-done((bf16[256,512]{1,0:T(8,128)(2,1)S(1)}, bf16[256,512]{1,0:T(8,128)(2,1)S(1)}, u32[]{:S(2)}, u32[]{:S(2)}) %collective-permute-start.4) | collective-permute-done | bytes 262176 | tf_op jit(solution)/shard_map/ppermute | solution.py:268
  20.6 0.0 collective-permute-done.2.far_ref
  20.6 0.0 collective-permute-done.1.middle_ref
  20.6 0.0 copy-done.6
  20.6 1.8 %shard_map.125 = (f32[512,512]{1,0:T(8,128)S(1)}, f32[4,512]{1,0:T(4,128)S(1)}) custom-call(s32[4,4]{1,0:T(4,128)S(1)} %copy-done.4, f32[4]{0:T(128)S(1)} %copy-done.6, s32[1,512]{1,0:T(1,128)S(1)} %copy-done.2, s32[1,512]{1,0:T(1,128)S(1)} %copy-done.3, f32[512,512]{1,0:T(8,128)S(1)} %get-tuple-element.16.left_ref, ...), custom_call_target="tpu_custom_call" | custom-call | tf_op jit(solution)/shard_map/pallas_call | solution.py:311
  22.4 1.0 %collective-permute-done.6.relay_ref = bf16[256,512]{1,0:T(8,128)(2,1)S(1)} collective-permute-done((bf16[256,512]{1,0:T(8,128)(2,1)S(1)}, bf16[256,512]{1,0:T(8,128)(2,1)S(1)}, u32[]{:S(2)}, u32[]{:S(2)}) %collective-permute-start.6) | collective-permute-done | bytes 262176 | tf_op jit(solution)/shard_map/ppermute | solution.py:268
  23.4 3.3 %collective-permute-done.7.last_ref = bf16[512,512]{1,0:T(8,128)(2,1)S(1)} collective-permute-done((bf16[512,512]{1,0:T(8,128)(2,1)S(1)}, bf16[512,512]{1,0:T(8,128)(2,1)S(1)}, u32[]{:S(2)}, u32[]{:S(2)}) %collective-permute-start.7) | collective-permute-done | bytes 524320 | tf_op jit(solution)/shard_map/ppermute | solution.py:268
  26.6 1.5 %shard_map.128 = (f32[512,512]{1,0:T(8,128)}, f32[512,512]{1,0:T(8,128)}) custom-call(f32[4,512]{1,0:T(4,128)S(1)} %get-tuple-element.20.scale_ref, f32[512,512]{1,0:T(8,128)S(1)} %get-tuple-element.21.partial_ref, f32[512,512]{1,0:T(8,128)S(1)} %shard_map.127.factor_ref, bf16[256,512]{1,0:T(8,128)(2,1)S(1)} %collective-permute-done.6.relay_ref, ...), custom_call_target="tpu_custom_call" | custom-call | tf_op jit(solution)/shard_map/pallas_call | solution.py:326
  (5 shorter events, 0.0 us)
Async XLA Ops:
  0.6 2.0 %copy-start.1 = (bf16[512,512]{1,0:T(8,128)(2,1)S(1)}, bf16[512,512]{1,0:T(8,128)(2,1)}, u32[]{:S(2)}) copy-start(bf16[512,512]{1,0:T(8,128)(2,1)} %head_ref.3) | copy-start | bytes 1572868
  3.3 4.6 %collective-permute-start = (bf16[512,512]{1,0:T(8,128)(2,1)S(1)}, bf16[512,512]{1,0:T(8,128)(2,1)S(1)}, u32[]{:S(2)}, u32[]{:S(2)}) collective-permute-start(bf16[512,512]{1,0:T(8,128)(2,1)S(1)} %get-tuple-element.15), channel_id=1, source_target_pairs={{0,8},{8,0},{16,24},{24,16},{1,9},{9,1},{17,25},{25,17},{2,10},{10... | collective-permute-start | bytes 1572872 | tf_op jit(solution)/shard_map/ppermute | solution.py:268
  3.9 5.0 %collective-permute-start.5 = (bf16[512,512]{1,0:T(8,128)(2,1)S(1)}, bf16[512,512]{1,0:T(8,128)(2,1)S(1)}, u32[]{:S(2)}, u32[]{:S(2)}) collective-permute-start(bf16[512,512]{1,0:T(8,128)(2,1)S(1)} %get-tuple-element.13.after_ref.a_ref), channel_id=1, source_target_pairs={{0,8},{8,0},{24,25},{16,24},{9,1},{1,9},{17,16},{25,17},{18,26},{2... | collective-permute-start | bytes 1572872 | tf_op jit(solution)/shard_map/ppermute | solution.py:268
  4.0 16.6 %collective-permute-start.2 = (bf16[512,512]{1,0:T(8,128)(2,1)S(1)}, bf16[512,512]{1,0:T(8,128)(2,1)S(1)}, u32[]{:S(2)}, u32[]{:S(2)}) collective-permute-start(bf16[512,512]{1,0:T(8,128)(2,1)S(1)} %get-tuple-element.13.after_ref.a_ref), channel_id=1, source_target_pairs={{0,4},{8,24},{24,16},{16,8},{9,13},{1,17},{17,25},{25,1},{18,22},{... | collective-permute-start | bytes 1572872 | tf_op jit(solution)/shard_map/ppermute | solution.py:268
  8.6 7.8 %copy-start = (f32[512,512]{1,0:T(8,128)S(1)}, f32[512,512]{1,0:T(8,128)}, u32[]{:S(2)}) copy-start(f32[512,512]{1,0:T(8,128)} %pair_ref.1) | copy-start | bytes 3145732
  8.6 11.9 %collective-permute-start.1 = (bf16[512,512]{1,0:T(8,128)(2,1)S(1)}, bf16[512,512]{1,0:T(8,128)(2,1)S(1)}, u32[]{:S(2)}, u32[]{:S(2)}) collective-permute-start(bf16[512,512]{1,0:T(8,128)(2,1)S(1)} %get-tuple-element.17), channel_id=1, source_target_pairs={{16,0},{0,8},{8,24},{24,16},{25,9},{9,1},{1,17},{17,25},{2,18},{18... | collective-permute-start | bytes 1572872 | tf_op jit(solution)/shard_map/ppermute | solution.py:268
  8.7 6.4 %collective-permute-start.3 = (bf16[256,512]{1,0:T(8,128)(2,1)S(1)}, bf16[256,512]{1,0:T(8,128)(2,1)S(1)}, u32[]{:S(2)}, u32[]{:S(2)}) collective-permute-start(bf16[256,512]{1,0:T(8,128)(2,1)S(1)} %get-tuple-element.18), channel_id=1, source_target_pairs={{8,9},{0,8},{16,24},{24,16},{1,0},{9,1},{25,17},{17,25},{26,27},{1... | collective-permute-start | bytes 786440 | tf_op jit(solution)/shard_map/ppermute | solution.py:268
  8.9 7.6 %copy-start.5 = (f32[4,4]{1,0:T(4,128)S(1)}, f32[4,4]{1,0:T(4,128)}, u32[]{:S(2)}) copy-start(f32[4,4]{1,0:T(4,128)} %weight_ref.1) | copy-start | bytes 196
  9.8 16.8 %collective-permute-start.7 = (bf16[512,512]{1,0:T(8,128)(2,1)S(1)}, bf16[512,512]{1,0:T(8,128)(2,1)S(1)}, u32[]{:S(2)}, u32[]{:S(2)}) collective-permute-start(bf16[512,512]{1,0:T(8,128)(2,1)S(1)} %shard_map.126.after_ref), channel_id=1, source_target_pairs={{16,22},{0,8},{24,16},{8,10},{25,31},{9,1},{17,25},{1,3},{2,0},{18... | collective-permute-start | bytes 1572872 | tf_op jit(solution)/shard_map/ppermute | solution.py:268
  10.7 5.7 %copy-start.3 = (s32[1,512]{1,0:T(1,128)S(1)}, s32[1,512]{1,0:T(1,128)}, u32[]{:S(2)}) copy-start(s32[1,512]{1,0:T(1,128)} %tail_ref.3) | copy-start | bytes 6148
  10.8 5.7 %copy-start.2 = (s32[1,512]{1,0:T(1,128)S(1)}, s32[1,512]{1,0:T(1,128)}, u32[]{:S(2)}) copy-start(s32[1,512]{1,0:T(1,128)} %head_ref.5) | copy-start | bytes 6148
  10.8 9.8 %collective-permute-start.4 = (bf16[256,512]{1,0:T(8,128)(2,1)S(1)}, bf16[256,512]{1,0:T(8,128)(2,1)S(1)}, u32[]{:S(2)}, u32[]{:S(2)}) collective-permute-start(bf16[256,512]{1,0:T(8,128)(2,1)S(1)} %get-tuple-element.19), channel_id=1, source_target_pairs={{8,13},{0,8},{16,24},{24,16},{1,0},{9,1},{25,17},{17,25},{26,31},{... | collective-permute-start | bytes 786440 | tf_op jit(solution)/shard_map/ppermute | solution.py:268
  15.1 8.2 %collective-permute-start.6 = (bf16[256,512]{1,0:T(8,128)(2,1)S(1)}, bf16[256,512]{1,0:T(8,128)(2,1)S(1)}, u32[]{:S(2)}, u32[]{:S(2)}) collective-permute-start(bf16[256,512]{1,0:T(8,128)(2,1)S(1)} %collective-permute-done.3.across_ref), channel_id=1, source_target_pairs={{16,24},{24,16},{25,17},{17,25},{9,13},{1,0},{0,8},{8,1},{2,10},{1... | collective-permute-start | bytes 786440 | tf_op jit(solution)/shard_map/ppermute | solution.py:268
  16.5 4.1 %copy-start.4 = (s32[4,4]{1,0:T(4,128)S(1)}, s32[4,4]{1,0:T(4,128)}, u32[]{:S(2)}) copy-start(s32[4,4]{1,0:T(4,128)} %mask_ref.1) | copy-start | bytes 196
  18.6 2.0 %copy-start.6 = (f32[4]{0:T(128)S(1)}, f32[4]{0:T(128)}, u32[]{:S(2)}) copy-start(f32[4]{0:T(128)} %split_ref.1) | copy-start | bytes 52

commit v7 on v6

--- a/solution.py
+++ b/solution.py
@@ -81,8 +81,12 @@
     code_ref[...] = encode(total)
 
 
-def add_kernel(a_ref, b_ref, code_ref):
-    code_ref[...] = encode(decode(a_ref[...]) + decode(b_ref[...]))
+def own_kernel(code_ref, after_ref, value_ref):
+    value_ref[...] = decode(code_ref[...])
+
+
+def add_kernel(own_ref, code_ref, sum_ref):
+    sum_ref[...] = encode(own_ref[...] + decode(code_ref[...]))
 
 
 def masked_row(mask_ref, row, size):
@@ -300,7 +304,8 @@
     left, moved = call(chip_kernel, [VMEM] * 2, (full, code))(left, i0)
     q4 = send(moved, middle)
     q3 = send(qx, relay)
-    pair = call(add_kernel, [VMEM] * 2, code)(right, q1)
+    own = call(own_kernel, [VMEM, ANY], full)(right, moved)
+    pair = call(add_kernel, [VMEM] * 2, code)(own, q1)
     q2 = send(pair, last)
     factor = call(
         factor_kernel,

time: 28.3 us -> 28 us (0.989)
  starting transfers between devices: 10.1 us -> 9.75 us
    ppermute x8, starting transfers between devices: 10.1 us -> 9.75 us  [send(): x = lax.ppermute(x, ('row', 'col'), pairs)]
    pallas_call x1 -> x2, Pallas kernels: 0.91 us -> 0.92 us  [the longest x1 0.64 us: routed(): pair = call(add_kernel, [VMEM] * 2, code)(own, q1)]
  transfers between devices with their start and end apart: 8 -> 8, of which waited for: 4 -> 4; matrix products, arithmetic and copies ran while one was open for 0% -> 0% of each run, Pallas kernels for 19% -> 20%
where the time goes in v7:
time: 28 us; the launch traced here: 27.9 us
  starting transfers between devices  9.75 us (35%)
  Pallas kernels  9.63 us (34%)
  waiting for transfers between devices  6.35 us (23%)
  between operations  2.09 us (7%)
    ppermute x8, starting transfers between devices, send(): x = lax.ppermute(x, ('row', 'col'), pairs)  9.75 us
    ppermute x8, waiting for transfers between devices, send(): x = lax.ppermute(x, ('row', 'col'), pairs)  6.35 us
    pallas_call x1, Pallas kernels, routed(): call(factor_kernel, [SMEM] + [VMEM] * 3 + [ANY] * 3, full, [pltpu.SMEM((1...  2.1 us
    pallas_call x1, Pallas kernels, routed(): call(right_kernel, [HBM] * 2, (code, code, half, half), [code, pltpu.Sema...  1.94 us
    pallas_call x1, Pallas kernels, routed(): call(functools.partial(partial_kernel, row_count), [SMEM] * 2 + [VMEM] *...  1.81 us
    pallas_call x1, Pallas kernels, routed(): pl.pallas_call(last_kernel, in_specs=[VMEM] * 5, out_specs=(HBM, HBM), ou...  1.48 us
    pallas_call x1, Pallas kernels, routed(): call(functools.partial(left_kernel, row_count), [VMEM] * 2 + [ANY], (full...  0.73 us
    pallas_call x1, Pallas kernels, routed(): left, moved = call(chip_kernel, [VMEM] * 2, (full, code))(left, i0)  0.66 us
  transfers between devices with their start and end apart: 8, of which 4 were waited for; matrix products, arithmetic and copies ran while one was open for 0% of the time, Pallas kernels for 20%

profile of v7, /device:TPU:0, one launch (start us, length us, event | category | flops | bytes accessed | tf_op | source)
XLA Modules:
  0.0 27.9 jit_solution(11212707440333585135)
XLA Ops:
  0.6 1.9 %shard_map.122 = (bf16[512,512]{1,0:T(8,128)(2,1)S(1)}, bf16[512,512]{1,0:T(8,128)(2,1)S(1)}, bf16[256,512]{1,0:T(8,128)(2,1)S(1)}, bf16[256,512]{1,0:T(8,128)(2,1)S(1)}) custom-call(bf16[512,512]{1,0:T(8,128)(2,1)} %out_hbm.1, bf16[512,512]{1,0:T(8,128)(2,1)} %tail_hbm.1), custom_call_target="tpu_custom_call" | custom-call | tf_op jit(solution)/shard_map/pallas_call | solution.py:287
  2.6 0.7 %shard_map.123 = (f32[512,512]{1,0:T(8,128)S(1)}, bf16[512,512]{1,0:T(8,128)(2,1)S(1)}) custom-call(bf16[512,512]{1,0:T(8,128)(2,1)S(1)} %copy-done.1, bf16[512,512]{1,0:T(8,128)(2,1)S(1)} %get-tuple-element.12.out_ref, bf16[512,512]{1,0:T(8,128)(2,1)S(1)} %get-tuple-element.13.after_ref.code_ref), custom_call_target="tpu_custom_call" | custom-call | tf_op jit(solution)/shard_map/pallas_call | solution.py:300
  3.3 0.6 %collective-permute-start = (bf16[512,512]{1,0:T(8,128)(2,1)S(1)}, bf16[512,512]{1,0:T(8,128)(2,1)S(1)}, u32[]{:S(2)}, u32[]{:S(2)}) collective-permute-start(bf16[512,512]{1,0:T(8,128)(2,1)S(1)} %get-tuple-element.15), channel_id=1, source_target_pairs={{0,8},{8,0},{16,24},{24,16},{1,9},{9,1},{17,25},{25,17},{2,10},{10... | collective-permute-start | bytes 1572872 | tf_op jit(solution)/shard_map/ppermute | solution.py:272
  3.9 0.1 collective-permute-start.5
  4.0 4.0 %collective-permute-start.2 = (bf16[512,512]{1,0:T(8,128)(2,1)S(1)}, bf16[512,512]{1,0:T(8,128)(2,1)S(1)}, u32[]{:S(2)}, u32[]{:S(2)}) collective-permute-start(bf16[512,512]{1,0:T(8,128)(2,1)S(1)} %get-tuple-element.13.after_ref.code_ref), channel_id=1, source_target_pairs={{0,4},{8,24},{24,16},{16,8},{9,13},{1,17},{17,25},{25,1},{18,22},{... | collective-permute-start | bytes 1572872 | tf_op jit(solution)/shard_map/ppermute | solution.py:272
  8.0 0.0 collective-permute-done.other_ref
  8.0 0.7 %shard_map.124 = (f32[512,512]{1,0:T(8,128)S(1)}, bf16[512,512]{1,0:T(8,128)(2,1)S(1)}) custom-call(f32[512,512]{1,0:T(8,128)S(1)} %get-tuple-element.14.left_ref, bf16[512,512]{1,0:T(8,128)(2,1)S(1)} %collective-permute-done.other_ref), custom_call_target="tpu_custom_call" | custom-call | tf_op jit(solution)/shard_map/pallas_call | solution.py:304
  8.6 0.1 collective-permute-start.1
  8.7 0.2 collective-permute-start.3
  8.9 0.3 %shard_map.126.own_ref = f32[512,512]{1,0:T(8,128)S(1)} custom-call(bf16[512,512]{1,0:T(8,128)(2,1)S(1)} %get-tuple-element.13.after_ref.code_ref, bf16[512,512]{1,0:T(8,128)(2,1)S(1)} %get-tuple-element.17.after_ref), custom_call_target="tpu_custom_call" | custom-call | tf_op jit(solution)/shard_map/pallas_call | solution.py:307
  9.2 0.0 copy-start
  9.2 0.0 collective-permute-done.5.code_ref
  9.2 0.0 copy-start.5
  9.2 0.6 %shard_map.127.after_ref = bf16[512,512]{1,0:T(8,128)(2,1)S(1)} custom-call(f32[512,512]{1,0:T(8,128)S(1)} %shard_map.126.own_ref, bf16[512,512]{1,0:T(8,128)(2,1)S(1)} %collective-permute-done.5.code_ref), custom_call_target="tpu_custom_call" | custom-call | tf_op jit(solution)/shard_map/pallas_call | solution.py:308
  9.8 0.9 %collective-permute-start.7 = (bf16[512,512]{1,0:T(8,128)(2,1)S(1)}, bf16[512,512]{1,0:T(8,128)(2,1)S(1)}, u32[]{:S(2)}, u32[]{:S(2)}) collective-permute-start(bf16[512,512]{1,0:T(8,128)(2,1)S(1)} %shard_map.127.after_ref), channel_id=1, source_target_pairs={{16,22},{0,8},{24,16},{8,10},{25,31},{9,1},{17,25},{1,3},{2,0},{18... | collective-permute-start | bytes 1572872 | tf_op jit(solution)/shard_map/ppermute | solution.py:272
  10.8 3.9 %collective-permute-start.4 = (bf16[256,512]{1,0:T(8,128)(2,1)S(1)}, bf16[256,512]{1,0:T(8,128)(2,1)S(1)}, u32[]{:S(2)}, u32[]{:S(2)}) collective-permute-start(bf16[256,512]{1,0:T(8,128)(2,1)S(1)} %get-tuple-element.19), channel_id=1, source_target_pairs={{8,13},{0,8},{16,24},{24,16},{1,0},{9,1},{25,17},{17,25},{26,31},{... | collective-permute-start | bytes 786440 | tf_op jit(solution)/shard_map/ppermute | solution.py:272
  14.7 0.4 %collective-permute-done.3.across_ref = bf16[256,512]{1,0:T(8,128)(2,1)S(1)} collective-permute-done((bf16[256,512]{1,0:T(8,128)(2,1)S(1)}, bf16[256,512]{1,0:T(8,128)(2,1)S(1)}, u32[]{:S(2)}, u32[]{:S(2)}) %collective-permute-start.3) | collective-permute-done | bytes 262176 | tf_op jit(solution)/shard_map/ppermute | solution.py:272
  15.1 0.0 collective-permute-start.6
  16.4 0.0 copy-done
  16.4 0.0 copy-done.5
  16.5 0.0 copy-done.3
  16.5 0.0 copy-done.2
  16.5 0.0 copy-start.4
  16.5 2.1 %shard_map.128.factor_ref = f32[512,512]{1,0:T(8,128)S(1)} custom-call(f32[4,4]{1,0:T(4,128)S(1)} %copy-done.5, s32[1,512]{1,0:T(1,128)S(1)} %copy-done.2, s32[1,512]{1,0:T(1,128)S(1)} %copy-done.3, f32[512,512]{1,0:T(8,128)S(1)} %copy-done, s32[1]{0:T(128)S(6)} %copy.13.span_hbm, f32[1]{0:T(128)S(6)} %copy.14.partition_hbm, ...), custom_call_target="tpu_custom_call" | custom-call | tf_op jit(solution)/shard_map/pallas_call | solution.py:310
  18.6 0.0 copy-start.6
  18.6 1.7 %collective-permute-done.4.direct_ref = bf16[256,512]{1,0:T(8,128)(2,1)S(1)} collective-permute-done((bf16[256,512]{1,0:T(8,128)(2,1)S(1)}, bf16[256,512]{1,0:T(8,128)(2,1)S(1)}, u32[]{:S(2)}, u32[]{:S(2)}) %collective-permute-start.4) | collective-permute-done | bytes 262176 | tf_op jit(solution)/shard_map/ppermute | solution.py:272
  20.3 0.0 collective-permute-done.2.far_ref
  20.3 0.0 collective-permute-done.1.middle_ref
  20.3 1.8 %shard_map.125 = (f32[512,512]{1,0:T(8,128)S(1)}, f32[4,512]{1,0:T(4,128)S(1)}) custom-call(s32[4,4]{1,0:T(4,128)S(1)} %copy-done.4, f32[4]{0:T(128)S(1)} %copy-done.6, s32[1,512]{1,0:T(1,128)S(1)} %copy-done.2, s32[1,512]{1,0:T(1,128)S(1)} %copy-done.3, f32[512,512]{1,0:T(8,128)S(1)} %get-tuple-element.16.left_ref, ...), custom_call_target="tpu_custom_call" | custom-call | tf_op jit(solution)/shard_map/pallas_call | solution.py:316
  22.1 1.0 %collective-permute-done.6.relay_ref = bf16[256,512]{1,0:T(8,128)(2,1)S(1)} collective-permute-done((bf16[256,512]{1,0:T(8,128)(2,1)S(1)}, bf16[256,512]{1,0:T(8,128)(2,1)S(1)}, u32[]{:S(2)}, u32[]{:S(2)}) %collective-permute-start.6) | collective-permute-done | bytes 262176 | tf_op jit(solution)/shard_map/ppermute | solution.py:272
  23.1 3.3 %collective-permute-done.7.last_ref = bf16[512,512]{1,0:T(8,128)(2,1)S(1)} collective-permute-done((bf16[512,512]{1,0:T(8,128)(2,1)S(1)}, bf16[512,512]{1,0:T(8,128)(2,1)S(1)}, u32[]{:S(2)}, u32[]{:S(2)}) %collective-permute-start.7) | collective-permute-done | bytes 524320 | tf_op jit(solution)/shard_map/ppermute | solution.py:272
  26.4 1.5 %shard_map.129 = (f32[512,512]{1,0:T(8,128)}, f32[512,512]{1,0:T(8,128)}) custom-call(f32[4,512]{1,0:T(4,128)S(1)} %get-tuple-element.20.scale_ref, f32[512,512]{1,0:T(8,128)S(1)} %get-tuple-element.21.partial_ref, f32[512,512]{1,0:T(8,128)S(1)} %shard_map.128.factor_ref, bf16[256,512]{1,0:T(8,128)(2,1)S(1)} %collective-permute-done.6.relay_ref, ...), custom_call_target="tpu_custom_call" | custom-call | tf_op jit(solution)/shard_map/pallas_call | solution.py:331
  (6 shorter events, 0.0 us)
Async XLA Ops:
  0.6 2.0 %copy-start.1 = (bf16[512,512]{1,0:T(8,128)(2,1)S(1)}, bf16[512,512]{1,0:T(8,128)(2,1)}, u32[]{:S(2)}) copy-start(bf16[512,512]{1,0:T(8,128)(2,1)} %head_ref.3) | copy-start | bytes 1572868
  3.3 4.6 %collective-permute-start = (bf16[512,512]{1,0:T(8,128)(2,1)S(1)}, bf16[512,512]{1,0:T(8,128)(2,1)S(1)}, u32[]{:S(2)}, u32[]{:S(2)}) collective-permute-start(bf16[512,512]{1,0:T(8,128)(2,1)S(1)} %get-tuple-element.15), channel_id=1, source_target_pairs={{0,8},{8,0},{16,24},{24,16},{1,9},{9,1},{17,25},{25,17},{2,10},{10... | collective-permute-start | bytes 1572872 | tf_op jit(solution)/shard_map/ppermute | solution.py:272
  3.9 5.3 %collective-permute-start.5 = (bf16[512,512]{1,0:T(8,128)(2,1)S(1)}, bf16[512,512]{1,0:T(8,128)(2,1)S(1)}, u32[]{:S(2)}, u32[]{:S(2)}) collective-permute-start(bf16[512,512]{1,0:T(8,128)(2,1)S(1)} %get-tuple-element.13.after_ref.code_ref), channel_id=1, source_target_pairs={{0,8},{8,0},{24,25},{16,24},{9,1},{1,9},{17,16},{25,17},{18,26},{2... | collective-permute-start | bytes 1572872 | tf_op jit(solution)/shard_map/ppermute | solution.py:272
  4.0 16.3 %collective-permute-start.2 = (bf16[512,512]{1,0:T(8,128)(2,1)S(1)}, bf16[512,512]{1,0:T(8,128)(2,1)S(1)}, u32[]{:S(2)}, u32[]{:S(2)}) collective-permute-start(bf16[512,512]{1,0:T(8,128)(2,1)S(1)} %get-tuple-element.13.after_ref.code_ref), channel_id=1, source_target_pairs={{0,4},{8,24},{24,16},{16,8},{9,13},{1,17},{17,25},{25,1},{18,22},{... | collective-permute-start | bytes 1572872 | tf_op jit(solution)/shard_map/ppermute | solution.py:272
  8.6 11.7 %collective-permute-start.1 = (bf16[512,512]{1,0:T(8,128)(2,1)S(1)}, bf16[512,512]{1,0:T(8,128)(2,1)S(1)}, u32[]{:S(2)}, u32[]{:S(2)}) collective-permute-start(bf16[512,512]{1,0:T(8,128)(2,1)S(1)} %get-tuple-element.17.after_ref), channel_id=1, source_target_pairs={{16,0},{0,8},{8,24},{24,16},{25,9},{9,1},{1,17},{17,25},{2,18},{18... | collective-permute-start | bytes 1572872 | tf_op jit(solution)/shard_map/ppermute | solution.py:272
  8.7 6.4 %collective-permute-start.3 = (bf16[256,512]{1,0:T(8,128)(2,1)S(1)}, bf16[256,512]{1,0:T(8,128)(2,1)S(1)}, u32[]{:S(2)}, u32[]{:S(2)}) collective-permute-start(bf16[256,512]{1,0:T(8,128)(2,1)S(1)} %get-tuple-element.18), channel_id=1, source_target_pairs={{8,9},{0,8},{16,24},{24,16},{1,0},{9,1},{25,17},{17,25},{26,27},{1... | collective-permute-start | bytes 786440 | tf_op jit(solution)/shard_map/ppermute | solution.py:272
  9.2 7.3 %copy-start = (f32[512,512]{1,0:T(8,128)S(1)}, f32[512,512]{1,0:T(8,128)}, u32[]{:S(2)}) copy-start(f32[512,512]{1,0:T(8,128)} %pair_ref.1) | copy-start | bytes 3145732
  9.2 7.3 %copy-start.5 = (f32[4,4]{1,0:T(4,128)S(1)}, f32[4,4]{1,0:T(4,128)}, u32[]{:S(2)}) copy-start(f32[4,4]{1,0:T(4,128)} %weight_ref.1) | copy-start | bytes 196
  9.8 16.5 %collective-permute-start.7 = (bf16[512,512]{1,0:T(8,128)(2,1)S(1)}, bf16[512,512]{1,0:T(8,128)(2,1)S(1)}, u32[]{:S(2)}, u32[]{:S(2)}) collective-permute-start(bf16[512,512]{1,0:T(8,128)(2,1)S(1)} %shard_map.127.after_ref), channel_id=1, source_target_pairs={{16,22},{0,8},{24,16},{8,10},{25,31},{9,1},{17,25},{1,3},{2,0},{18... | collective-permute-start | bytes 1572872 | tf_op jit(solution)/shard_map/ppermute | solution.py:272
  10.8 5.7 %copy-start.3 = (s32[1,512]{1,0:T(1,128)S(1)}, s32[1,512]{1,0:T(1,128)}, u32[]{:S(2)}) copy-start(s32[1,512]{1,0:T(1,128)} %tail_ref.3) | copy-start | bytes 6148
  10.8 5.7 %copy-start.2 = (s32[1,512]{1,0:T(1,128)S(1)}, s32[1,512]{1,0:T(1,128)}, u32[]{:S(2)}) copy-start(s32[1,512]{1,0:T(1,128)} %head_ref.5) | copy-start | bytes 6148
  10.8 9.5 %collective-permute-start.4 = (bf16[256,512]{1,0:T(8,128)(2,1)S(1)}, bf16[256,512]{1,0:T(8,128)(2,1)S(1)}, u32[]{:S(2)}, u32[]{:S(2)}) collective-permute-start(bf16[256,512]{1,0:T(8,128)(2,1)S(1)} %get-tuple-element.19), channel_id=1, source_target_pairs={{8,13},{0,8},{16,24},{24,16},{1,0},{9,1},{25,17},{17,25},{26,31},{... | collective-permute-start | bytes 786440 | tf_op jit(solution)/shard_map/ppermute | solution.py:272
  15.1 8.0 %collective-permute-start.6 = (bf16[256,512]{1,0:T(8,128)(2,1)S(1)}, bf16[256,512]{1,0:T(8,128)(2,1)S(1)}, u32[]{:S(2)}, u32[]{:S(2)}) collective-permute-start(bf16[256,512]{1,0:T(8,128)(2,1)S(1)} %collective-permute-done.3.across_ref), channel_id=1, source_target_pairs={{16,24},{24,16},{25,17},{17,25},{9,13},{1,0},{0,8},{8,1},{2,10},{1... | collective-permute-start | bytes 786440 | tf_op jit(solution)/shard_map/ppermute | solution.py:272
  16.5 3.8 %copy-start.4 = (s32[4,4]{1,0:T(4,128)S(1)}, s32[4,4]{1,0:T(4,128)}, u32[]{:S(2)}) copy-start(s32[4,4]{1,0:T(4,128)} %mask_ref.1) | copy-start | bytes 196
  18.6 1.7 %copy-start.6 = (f32[4]{0:T(128)S(1)}, f32[4]{0:T(128)}, u32[]{:S(2)}) copy-start(f32[4]{0:T(128)} %split_ref.1) | copy-start | bytes 52

commit v8 on v7

--- a/solution.py
+++ b/solution.py
@@ -194,23 +194,26 @@
     cells = scale_ref.shape[0]
     step = outside_ref.shape[0] // cells
     copies = []
-    for cell in range(cells):
-        rows = pl.ds(cell * step, step)
+    groups = [(0, step // 2), (step // 2, step - step // 2)]
+    groups += [(cell * step, step) for cell in range(1, cells)]
+    for group, (begin, count) in enumerate(groups):
+        cell = begin // step
+        rows = pl.ds(begin, count)
         right = decode(last_ref[rows, :])
         if 2 * cell >= cells:
-            code = relay_ref[pl.ds((cell - cells // 2) * step, step), :].astype(jnp.float32)
+            code = relay_ref[pl.ds(begin - cells // 2 * step, count), :].astype(jnp.float32)
             right += decode(jnp.where(lax.rem(col_id, 2) == 1, code, 0.0))
         total = partial_ref[rows, :] + scale_ref[pl.ds(cell, 1), :] * right
         outside_ref[rows, :] = total
         copies.append(
             pltpu.make_async_copy(
-                outside_ref.at[rows, :], outside_hbm.at[rows, :], sems.at[0, cell]
+                outside_ref.at[rows, :], outside_hbm.at[rows, :], sems.at[0, group]
             )
         )
         copies[-1].start()
         prob_ref[rows, :] = total * factor_ref[rows, :]
         copies.append(
-            pltpu.make_async_copy(prob_ref.at[rows, :], prob_hbm.at[rows, :], sems.at[1, cell])
+            pltpu.make_async_copy(prob_ref.at[rows, :], prob_hbm.at[rows, :], sems.at[1, group])
         )
         copies[-1].start()
     for copy in copies:
@@ -333,7 +336,7 @@
         in_specs=[VMEM] * 5,
         out_specs=(HBM, HBM),
         out_shape=(output, output),
-        scratch_shapes=[full, full, pltpu.SemaphoreType.DMA((2, cells))],
+        scratch_shapes=[full, full, pltpu.SemaphoreType.DMA((2, cells + 1))],
         compiler_params=PARAMS,
     )(scale, partial, factor, q3, q2)
 

time: 28 us -> 28 us (level)
  no operation moved by 1% of the time
where the time goes in v8:
time: 28 us; the launch traced here: 27.8 us
  starting transfers between devices  9.75 us (35%)
  Pallas kernels  9.62 us (34%)
  waiting for transfers between devices  6.35 us (23%)
  between operations  2.09 us (7%)
    ppermute x8, starting transfers between devices, send(): x = lax.ppermute(x, ('row', 'col'), pairs)  9.75 us
    ppermute x8, waiting for transfers between devices, send(): x = lax.ppermute(x, ('row', 'col'), pairs)  6.35 us
    pallas_call x1, Pallas kernels, routed(): call(factor_kernel, [SMEM] + [VMEM] * 3 + [ANY] * 3, full, [pltpu.SMEM((1...  2.1 us
    pallas_call x1, Pallas kernels, routed(): call(right_kernel, [HBM] * 2, (code, code, half, half), [code, pltpu.Sema...  1.94 us
    pallas_call x1, Pallas kernels, routed(): call(functools.partial(partial_kernel, row_count), [SMEM] * 2 + [VMEM] *...  1.81 us
    pallas_call x1, Pallas kernels, routed(): pl.pallas_call(last_kernel, in_specs=[VMEM] * 5, out_specs=(HBM, HBM), ou...  1.47 us
    pallas_call x1, Pallas kernels, routed(): call(functools.partial(left_kernel, row_count), [VMEM] * 2 + [ANY], (full...  0.73 us
    pallas_call x1, Pallas kernels, routed(): left, moved = call(chip_kernel, [VMEM] * 2, (full, code))(left, i0)  0.66 us
  transfers between devices with their start and end apart: 8, of which 4 were waited for; matrix products, arithmetic and copies ran while one was open for 0% of the time, Pallas kernels for 20%

profile of v8, /device:TPU:0, one launch (start us, length us, event | category | flops | bytes accessed | tf_op | source)
XLA Modules:
  0.0 27.8 jit_solution(13729920701190992287)
XLA Ops:
  0.6 1.9 %shard_map.122 = (bf16[512,512]{1,0:T(8,128)(2,1)S(1)}, bf16[512,512]{1,0:T(8,128)(2,1)S(1)}, bf16[256,512]{1,0:T(8,128)(2,1)S(1)}, bf16[256,512]{1,0:T(8,128)(2,1)S(1)}) custom-call(bf16[512,512]{1,0:T(8,128)(2,1)} %out_hbm.1, bf16[512,512]{1,0:T(8,128)(2,1)} %tail_hbm.1), custom_call_target="tpu_custom_call" | custom-call | tf_op jit(solution)/shard_map/pallas_call | solution.py:290
  2.6 0.7 %shard_map.123 = (f32[512,512]{1,0:T(8,128)S(1)}, bf16[512,512]{1,0:T(8,128)(2,1)S(1)}) custom-call(bf16[512,512]{1,0:T(8,128)(2,1)S(1)} %copy-done.1, bf16[512,512]{1,0:T(8,128)(2,1)S(1)} %get-tuple-element.12.out_ref, bf16[512,512]{1,0:T(8,128)(2,1)S(1)} %get-tuple-element.13.after_ref.code_ref), custom_call_target="tpu_custom_call" | custom-call | tf_op jit(solution)/shard_map/pallas_call | solution.py:303
  3.3 0.6 %collective-permute-start = (bf16[512,512]{1,0:T(8,128)(2,1)S(1)}, bf16[512,512]{1,0:T(8,128)(2,1)S(1)}, u32[]{:S(2)}, u32[]{:S(2)}) collective-permute-start(bf16[512,512]{1,0:T(8,128)(2,1)S(1)} %get-tuple-element.15), channel_id=1, source_target_pairs={{0,8},{8,0},{16,24},{24,16},{1,9},{9,1},{17,25},{25,17},{2,10},{10... | collective-permute-start | bytes 1572872 | tf_op jit(solution)/shard_map/ppermute | solution.py:275
  3.9 0.1 collective-permute-start.5
  4.0 4.0 %collective-permute-start.2 = (bf16[512,512]{1,0:T(8,128)(2,1)S(1)}, bf16[512,512]{1,0:T(8,128)(2,1)S(1)}, u32[]{:S(2)}, u32[]{:S(2)}) collective-permute-start(bf16[512,512]{1,0:T(8,128)(2,1)S(1)} %get-tuple-element.13.after_ref.code_ref), channel_id=1, source_target_pairs={{0,4},{8,24},{24,16},{16,8},{9,13},{1,17},{17,25},{25,1},{18,22},{... | collective-permute-start | bytes 1572872 | tf_op jit(solution)/shard_map/ppermute | solution.py:275
  8.0 0.0 collective-permute-done.other_ref
  8.0 0.7 %shard_map.124 = (f32[512,512]{1,0:T(8,128)S(1)}, bf16[512,512]{1,0:T(8,128)(2,1)S(1)}) custom-call(f32[512,512]{1,0:T(8,128)S(1)} %get-tuple-element.14.left_ref, bf16[512,512]{1,0:T(8,128)(2,1)S(1)} %collective-permute-done.other_ref), custom_call_target="tpu_custom_call" | custom-call | tf_op jit(solution)/shard_map/pallas_call | solution.py:307
  8.6 0.1 collective-permute-start.1
  8.7 0.2 collective-permute-start.3
  8.9 0.3 %shard_map.126.own_ref = f32[512,512]{1,0:T(8,128)S(1)} custom-call(bf16[512,512]{1,0:T(8,128)(2,1)S(1)} %get-tuple-element.13.after_ref.code_ref, bf16[512,512]{1,0:T(8,128)(2,1)S(1)} %get-tuple-element.17.after_ref), custom_call_target="tpu_custom_call" | custom-call | tf_op jit(solution)/shard_map/pallas_call | solution.py:310
  9.2 0.0 copy-start
  9.2 0.0 collective-permute-done.5.code_ref
  9.2 0.0 copy-start.5
  9.2 0.6 %shard_map.127.after_ref = bf16[512,512]{1,0:T(8,128)(2,1)S(1)} custom-call(f32[512,512]{1,0:T(8,128)S(1)} %shard_map.126.own_ref, bf16[512,512]{1,0:T(8,128)(2,1)S(1)} %collective-permute-done.5.code_ref), custom_call_target="tpu_custom_call" | custom-call | tf_op jit(solution)/shard_map/pallas_call | solution.py:311
  9.8 0.9 %collective-permute-start.7 = (bf16[512,512]{1,0:T(8,128)(2,1)S(1)}, bf16[512,512]{1,0:T(8,128)(2,1)S(1)}, u32[]{:S(2)}, u32[]{:S(2)}) collective-permute-start(bf16[512,512]{1,0:T(8,128)(2,1)S(1)} %shard_map.127.after_ref), channel_id=1, source_target_pairs={{16,22},{0,8},{24,16},{8,10},{25,31},{9,1},{17,25},{1,3},{2,0},{18... | collective-permute-start | bytes 1572872 | tf_op jit(solution)/shard_map/ppermute | solution.py:275
  10.8 3.9 %collective-permute-start.4 = (bf16[256,512]{1,0:T(8,128)(2,1)S(1)}, bf16[256,512]{1,0:T(8,128)(2,1)S(1)}, u32[]{:S(2)}, u32[]{:S(2)}) collective-permute-start(bf16[256,512]{1,0:T(8,128)(2,1)S(1)} %get-tuple-element.19), channel_id=1, source_target_pairs={{8,13},{0,8},{16,24},{24,16},{1,0},{9,1},{25,17},{17,25},{26,31},{... | collective-permute-start | bytes 786440 | tf_op jit(solution)/shard_map/ppermute | solution.py:275
  14.7 0.4 %collective-permute-done.3.across_ref = bf16[256,512]{1,0:T(8,128)(2,1)S(1)} collective-permute-done((bf16[256,512]{1,0:T(8,128)(2,1)S(1)}, bf16[256,512]{1,0:T(8,128)(2,1)S(1)}, u32[]{:S(2)}, u32[]{:S(2)}) %collective-permute-start.3) | collective-permute-done | bytes 262176 | tf_op jit(solution)/shard_map/ppermute | solution.py:275
  15.1 0.0 collective-permute-start.6
  16.4 0.0 copy-done
  16.4 0.0 copy-done.5
  16.5 0.0 copy-done.3
  16.5 0.0 copy-done.2
  16.5 0.0 copy-start.4
  16.5 2.1 %shard_map.128.factor_ref = f32[512,512]{1,0:T(8,128)S(1)} custom-call(f32[4,4]{1,0:T(4,128)S(1)} %copy-done.5, s32[1,512]{1,0:T(1,128)S(1)} %copy-done.2, s32[1,512]{1,0:T(1,128)S(1)} %copy-done.3, f32[512,512]{1,0:T(8,128)S(1)} %copy-done, s32[1]{0:T(128)S(6)} %copy.13.span_hbm, f32[1]{0:T(128)S(6)} %copy.14.partition_hbm, ...), custom_call_target="tpu_custom_call" | custom-call | tf_op jit(solution)/shard_map/pallas_call | solution.py:313
  18.6 0.0 copy-start.6
  18.6 1.7 %collective-permute-done.4.direct_ref = bf16[256,512]{1,0:T(8,128)(2,1)S(1)} collective-permute-done((bf16[256,512]{1,0:T(8,128)(2,1)S(1)}, bf16[256,512]{1,0:T(8,128)(2,1)S(1)}, u32[]{:S(2)}, u32[]{:S(2)}) %collective-permute-start.4) | collective-permute-done | bytes 262176 | tf_op jit(solution)/shard_map/ppermute | solution.py:275
  20.3 0.0 collective-permute-done.2.far_ref
  20.3 0.0 collective-permute-done.1.middle_ref
  20.3 1.8 %shard_map.125 = (f32[512,512]{1,0:T(8,128)S(1)}, f32[4,512]{1,0:T(4,128)S(1)}) custom-call(s32[4,4]{1,0:T(4,128)S(1)} %copy-done.4, f32[4]{0:T(128)S(1)} %copy-done.6, s32[1,512]{1,0:T(1,128)S(1)} %copy-done.2, s32[1,512]{1,0:T(1,128)S(1)} %copy-done.3, f32[512,512]{1,0:T(8,128)S(1)} %get-tuple-element.16.left_ref, ...), custom_call_target="tpu_custom_call" | custom-call | tf_op jit(solution)/shard_map/pallas_call | solution.py:319
  22.1 1.0 %collective-permute-done.6.relay_ref = bf16[256,512]{1,0:T(8,128)(2,1)S(1)} collective-permute-done((bf16[256,512]{1,0:T(8,128)(2,1)S(1)}, bf16[256,512]{1,0:T(8,128)(2,1)S(1)}, u32[]{:S(2)}, u32[]{:S(2)}) %collective-permute-start.6) | collective-permute-done | bytes 262176 | tf_op jit(solution)/shard_map/ppermute | solution.py:275
  23.1 3.3 %collective-permute-done.7.last_ref = bf16[512,512]{1,0:T(8,128)(2,1)S(1)} collective-permute-done((bf16[512,512]{1,0:T(8,128)(2,1)S(1)}, bf16[512,512]{1,0:T(8,128)(2,1)S(1)}, u32[]{:S(2)}, u32[]{:S(2)}) %collective-permute-start.7) | collective-permute-done | bytes 524320 | tf_op jit(solution)/shard_map/ppermute | solution.py:275
  26.4 1.5 %shard_map.129 = (f32[512,512]{1,0:T(8,128)}, f32[512,512]{1,0:T(8,128)}) custom-call(f32[4,512]{1,0:T(4,128)S(1)} %get-tuple-element.20.scale_ref, f32[512,512]{1,0:T(8,128)S(1)} %get-tuple-element.21.partial_ref, f32[512,512]{1,0:T(8,128)S(1)} %shard_map.128.factor_ref, bf16[256,512]{1,0:T(8,128)(2,1)S(1)} %collective-permute-done.6.relay_ref, ...), custom_call_target="tpu_custom_call" | custom-call | tf_op jit(solution)/shard_map/pallas_call | solution.py:334
  (6 shorter events, 0.0 us)
Async XLA Ops:
  0.6 2.0 %copy-start.1 = (bf16[512,512]{1,0:T(8,128)(2,1)S(1)}, bf16[512,512]{1,0:T(8,128)(2,1)}, u32[]{:S(2)}) copy-start(bf16[512,512]{1,0:T(8,128)(2,1)} %head_ref.3) | copy-start | bytes 1572868
  3.3 4.6 %collective-permute-start = (bf16[512,512]{1,0:T(8,128)(2,1)S(1)}, bf16[512,512]{1,0:T(8,128)(2,1)S(1)}, u32[]{:S(2)}, u32[]{:S(2)}) collective-permute-start(bf16[512,512]{1,0:T(8,128)(2,1)S(1)} %get-tuple-element.15), channel_id=1, source_target_pairs={{0,8},{8,0},{16,24},{24,16},{1,9},{9,1},{17,25},{25,17},{2,10},{10... | collective-permute-start | bytes 1572872 | tf_op jit(solution)/shard_map/ppermute | solution.py:275
  3.9 5.3 %collective-permute-start.5 = (bf16[512,512]{1,0:T(8,128)(2,1)S(1)}, bf16[512,512]{1,0:T(8,128)(2,1)S(1)}, u32[]{:S(2)}, u32[]{:S(2)}) collective-permute-start(bf16[512,512]{1,0:T(8,128)(2,1)S(1)} %get-tuple-element.13.after_ref.code_ref), channel_id=1, source_target_pairs={{0,8},{8,0},{24,25},{16,24},{9,1},{1,9},{17,16},{25,17},{18,26},{2... | collective-permute-start | bytes 1572872 | tf_op jit(solution)/shard_map/ppermute | solution.py:275
  4.0 16.3 %collective-permute-start.2 = (bf16[512,512]{1,0:T(8,128)(2,1)S(1)}, bf16[512,512]{1,0:T(8,128)(2,1)S(1)}, u32[]{:S(2)}, u32[]{:S(2)}) collective-permute-start(bf16[512,512]{1,0:T(8,128)(2,1)S(1)} %get-tuple-element.13.after_ref.code_ref), channel_id=1, source_target_pairs={{0,4},{8,24},{24,16},{16,8},{9,13},{1,17},{17,25},{25,1},{18,22},{... | collective-permute-start | bytes 1572872 | tf_op jit(solution)/shard_map/ppermute | solution.py:275
  8.6 11.7 %collective-permute-start.1 = (bf16[512,512]{1,0:T(8,128)(2,1)S(1)}, bf16[512,512]{1,0:T(8,128)(2,1)S(1)}, u32[]{:S(2)}, u32[]{:S(2)}) collective-permute-start(bf16[512,512]{1,0:T(8,128)(2,1)S(1)} %get-tuple-element.17.after_ref), channel_id=1, source_target_pairs={{16,0},{0,8},{8,24},{24,16},{25,9},{9,1},{1,17},{17,25},{2,18},{18... | collective-permute-start | bytes 1572872 | tf_op jit(solution)/shard_map/ppermute | solution.py:275
  8.7 6.4 %collective-permute-start.3 = (bf16[256,512]{1,0:T(8,128)(2,1)S(1)}, bf16[256,512]{1,0:T(8,128)(2,1)S(1)}, u32[]{:S(2)}, u32[]{:S(2)}) collective-permute-start(bf16[256,512]{1,0:T(8,128)(2,1)S(1)} %get-tuple-element.18), channel_id=1, source_target_pairs={{8,9},{0,8},{16,24},{24,16},{1,0},{9,1},{25,17},{17,25},{26,27},{1... | collective-permute-start | bytes 786440 | tf_op jit(solution)/shard_map/ppermute | solution.py:275
  9.2 7.3 %copy-start = (f32[512,512]{1,0:T(8,128)S(1)}, f32[512,512]{1,0:T(8,128)}, u32[]{:S(2)}) copy-start(f32[512,512]{1,0:T(8,128)} %pair_ref.1) | copy-start | bytes 3145732
  9.2 7.3 %copy-start.5 = (f32[4,4]{1,0:T(4,128)S(1)}, f32[4,4]{1,0:T(4,128)}, u32[]{:S(2)}) copy-start(f32[4,4]{1,0:T(4,128)} %weight_ref.1) | copy-start | bytes 196
  9.8 16.5 %collective-permute-start.7 = (bf16[512,512]{1,0:T(8,128)(2,1)S(1)}, bf16[512,512]{1,0:T(8,128)(2,1)S(1)}, u32[]{:S(2)}, u32[]{:S(2)}) collective-permute-start(bf16[512,512]{1,0:T(8,128)(2,1)S(1)} %shard_map.127.after_ref), channel_id=1, source_target_pairs={{16,22},{0,8},{24,16},{8,10},{25,31},{9,1},{17,25},{1,3},{2,0},{18... | collective-permute-start | bytes 1572872 | tf_op jit(solution)/shard_map/ppermute | solution.py:275
  10.8 5.7 %copy-start.3 = (s32[1,512]{1,0:T(1,128)S(1)}, s32[1,512]{1,0:T(1,128)}, u32[]{:S(2)}) copy-start(s32[1,512]{1,0:T(1,128)} %tail_ref.3) | copy-start | bytes 6148
  10.8 5.7 %copy-start.2 = (s32[1,512]{1,0:T(1,128)S(1)}, s32[1,512]{1,0:T(1,128)}, u32[]{:S(2)}) copy-start(s32[1,512]{1,0:T(1,128)} %head_ref.5) | copy-start | bytes 6148
  10.8 9.5 %collective-permute-start.4 = (bf16[256,512]{1,0:T(8,128)(2,1)S(1)}, bf16[256,512]{1,0:T(8,128)(2,1)S(1)}, u32[]{:S(2)}, u32[]{:S(2)}) collective-permute-start(bf16[256,512]{1,0:T(8,128)(2,1)S(1)} %get-tuple-element.19), channel_id=1, source_target_pairs={{8,13},{0,8},{16,24},{24,16},{1,0},{9,1},{25,17},{17,25},{26,31},{... | collective-permute-start | bytes 786440 | tf_op jit(solution)/shard_map/ppermute | solution.py:275
  15.1 8.0 %collective-permute-start.6 = (bf16[256,512]{1,0:T(8,128)(2,1)S(1)}, bf16[256,512]{1,0:T(8,128)(2,1)S(1)}, u32[]{:S(2)}, u32[]{:S(2)}) collective-permute-start(bf16[256,512]{1,0:T(8,128)(2,1)S(1)} %collective-permute-done.3.across_ref), channel_id=1, source_target_pairs={{16,24},{24,16},{25,17},{17,25},{9,13},{1,0},{0,8},{8,1},{2,10},{1... | collective-permute-start | bytes 786440 | tf_op jit(solution)/shard_map/ppermute | solution.py:275
  16.5 3.8 %copy-start.4 = (s32[4,4]{1,0:T(4,128)S(1)}, s32[4,4]{1,0:T(4,128)}, u32[]{:S(2)}) copy-start(s32[4,4]{1,0:T(4,128)} %mask_ref.1) | copy-start | bytes 196
  18.6 1.7 %copy-start.6 = (f32[4]{0:T(128)S(1)}, f32[4]{0:T(128)}, u32[]{:S(2)}) copy-start(f32[4]{0:T(128)} %split_ref.1) | copy-start | bytes 52
